TPU v7x, 256 devices: a whole 4x4x8 slice. The times are simulated.
256 devices in a mesh: tm: 8 (over x, core), pair: 32 (over z, y).
Axes of the slice: x: 4, y: 4, z: 8, core: 2. Of those that a mesh axis runs over, the one named last changes fastest.
Arguments:
- mode_fields: bfloat16 [2, 256, 4096], P(None, None, 'tm'), may hold values from -6 to 6
- raman_taps: bfloat16 [128], replicated, may hold values from -0.5 to 0.5
- pair_blocks: int32 [32, 16, 2], P('pair'), may hold values from 0 to 31
- light_blocks: int32 [32, 16, 2], P('pair'), may hold values from 0 to 31
- target_blocks: int32 [1024, 1], P('pair'), may hold values from 0 to 31; in each aligned block of 32 rows (0 to 31, 32 to 63, ...) at most 2 rows name the same one
- raman_values: bfloat16 [32, 16, 2, 4096], P('pair'), may hold values from -0.03125 to 0.03125
- live_slots: int32 [32], P('pair'), may hold values from 11 to 16, as said below
Outputs:
- raman_term: float32 [2, 256, 4096], P(None, 'pair', 'tm')
Inputs may be any that keep to these rules, and one draw needn't show every extreme that they name: `target_blocks`: within the 32 rows of one index of pair, no mode block is named by more than 2 rows, a bound that some block reaches. `live_slots`: some index of pair uses all 16 slots in every draw; every index uses at least 11.
All inputs are finite; a program needn't handle non-finite values.
Results may differ from a plain program's by a relative error of at most 0.004.
Values may be sent and summed in bfloat16 or wider, within the bound.
A program may use at most 64 MiB of HBM per device.

v0:
```python
import jax
import jax.numpy as jnp
from jax import lax
from jax.sharding import PartitionSpec as P

MB = 8


def toeplitz_table(tap_values):
    tap_count = tap_values.shape[0]
    row_index = jnp.arange(2 * tap_count, dtype=jnp.int32)[:, None]
    col_index = jnp.arange(tap_count, dtype=jnp.int32)[None, :]
    lag_index = tap_count + col_index - row_index
    tap_index = jnp.clip(lag_index - 1, 0, tap_count - 1)
    chosen = jnp.take(tap_values, tap_index)
    return jnp.where((lag_index >= 1) & (lag_index <= tap_count), chosen, jnp.zeros_like(chosen))


def delayed(signal, toeplitz):
    tap_count = toeplitz.shape[1]
    out_length = signal.shape[1] - tap_count
    block_total = out_length // tap_count
    row_total = signal.shape[0]
    pieces = signal.reshape(row_total, block_total + 1, tap_count)
    windows = jnp.concatenate([pieces[:, :-1], pieces[:, 1:]], axis=2)
    flat_windows = windows.reshape(row_total * block_total, 2 * tap_count)
    result = jnp.dot(flat_windows, toeplitz, preferred_element_type=jnp.float32)
    return result.reshape(row_total, out_length)


def slot_partials(blocked, pair_ids, light_ids, values, toeplitz):
    tap_count = toeplitz.shape[1]
    block_size = blocked.shape[2]
    length = blocked.shape[3] - tap_count
    square = block_size * block_size
    left_field = blocked[pair_ids[0]]
    right_field = blocked[pair_ids[1]]
    left_real = left_field[0].astype(jnp.float32)[:, None]
    left_imag = left_field[1].astype(jnp.float32)[:, None]
    right_real = right_field[0].astype(jnp.float32)[None]
    right_imag = right_field[1].astype(jnp.float32)[None]
    real_part = (left_real * right_real + left_imag * right_imag).reshape(square, -1)
    imag_part = (left_imag * right_real - left_real * right_imag).reshape(square, -1)
    intensity = jnp.concatenate([real_part, imag_part], 0).astype(jnp.bfloat16)
    response = delayed(intensity, toeplitz).astype(jnp.bfloat16)
    partials = []
    for entry_index in range(values.shape[0]):
        matrix = values[entry_index].reshape(square, square)
        mixed_real = jnp.dot(matrix, response[:square], preferred_element_type=jnp.float32).reshape(
            block_size, block_size, length
        )
        mixed_imag = jnp.dot(matrix, response[square:], preferred_element_type=jnp.float32).reshape(
            block_size, block_size, length
        )
        light_field = blocked[light_ids[entry_index]][:, :, tap_count:]
        light_real = light_field[0][None]
        light_imag = light_field[1][None]
        out_real = jnp.sum(
            light_real.astype(jnp.float32) * mixed_real
            - light_imag.astype(jnp.float32) * mixed_imag,
            axis=1,
        )
        out_imag = jnp.sum(
            light_real.astype(jnp.float32) * mixed_imag
            + light_imag.astype(jnp.float32) * mixed_real,
            axis=1,
        )
        partials.append(jnp.stack([out_real, out_imag]))
    return partials


def local(
    mode_fields, raman_taps, pair_blocks, light_blocks, target_blocks, raman_values, live_slots
):
    toeplitz = toeplitz_table(raman_taps)
    tap_count = toeplitz.shape[1]
    block_size = MB
    tm_count = lax.axis_size("tm")
    pair_count = lax.axis_size("pair")
    slot_count = pair_blocks.shape[1]
    entries = light_blocks.shape[2]
    mode_count = mode_fields.shape[1]
    blocks = mode_count // block_size
    live_count = live_slots[0]
    targets = target_blocks.reshape(slot_count, entries)
    gathered = lax.all_gather(mode_fields, "tm", axis=2, tiled=True)
    window = jnp.concatenate([jnp.zeros((2, mode_count, tap_count), jnp.bfloat16), gathered], 2)
    first_slot = lax.axis_index("tm")
    my_slots = slot_count // tm_count
    full_length = window.shape[2]
    length = full_length - tap_count
    blocked = jnp.transpose(window.reshape(2, blocks, block_size, full_length), (1, 0, 2, 3))
    buffers = jnp.zeros((blocks, 2, block_size, length), jnp.float32)

    def one_slot(turn_index, buffers):
        slot_index = first_slot + tm_count * turn_index
        partials = slot_partials(
            blocked,
            pair_blocks[0, slot_index],
            light_blocks[0, slot_index],
            raman_values[0, slot_index],
            toeplitz,
        )
        for entry_index in range(entries):
            target = targets[slot_index, entry_index]
            current = lax.dynamic_index_in_dim(buffers, target, 0, True)
            buffers = lax.dynamic_update_index_in_dim(
                buffers, current + partials[entry_index][None], target, 0
            )
        return buffers

    turn_count = jnp.clip((live_count - first_slot + tm_count - 1) // tm_count, 0, my_slots)
    buffers = lax.fori_loop(0, turn_count, one_slot, buffers)
    owned = blocks // pair_count
    received = lax.all_to_all(buffers, "pair", split_axis=0, concat_axis=0, tiled=True)
    shared = received.reshape(pair_count, owned, 2, block_size, length).sum(axis=0)
    result = jnp.transpose(shared, (1, 0, 2, 3)).reshape(2, owned * block_size, length)
    result = lax.psum_scatter(result, "tm", scatter_dimension=2, tiled=True)
    return result


def solution(mesh):
    return jax.shard_map(
        local,
        mesh=mesh,
        in_specs=(
            P(None, None, "tm"),
            P(),
            P("pair", None, None),
            P("pair", None, None),
            P("pair", None),
            P("pair", None, None, None),
            P("pair"),
        ),
        out_specs=P(None, "pair", "tm"),
        check_vma=False,
    )
```

profile of v0, /device:TPU:11, one launch (start us, length us, event | category | flops | bytes accessed | tf_op | source)
XLA Modules:
  0.0 494.8 jit_solution(10129818427244811848)
XLA Ops:
  6.5 0.7 all-gather.2.cloned.1.call-update
  8.0 0.5 broadcast.114
  8.5 1.3 reduce.9
  10.1 191.6 %gather_fusion = bf16[32768]{0:T(1024)(128)(2,1)S(1)} fusion(bf16[128]{0:T(256)(128)(2,1)S(1)} %copy-done, s32[32768]{0:T(1024)S(1)} %fusion.13), kind=kCustom, calls=%fused_computation | custom fusion | bytes 262144 | tf_op jit(solution)/shard_map/jit(_take)/gather | solution.py:15
  201.8 2.5 pad_bitcast_fusion
  204.3 2.3 copy.10
  206.5 4.2 broadcast_in_dim.14
  210.8 49.7 %while.10 = (s32[]{:T(128)}, f32[32,2,8,4096]{3,2,1,0:T(8,128)}, s32[]{:T(128)}, s32[]{:T(128)}, s32[16,2]{0,1:T(2,128)S(1)}, /*index=5*/s32[1,16,2]{1,2,0:T(2,1...) while((s32[]{:T(128)}, f32[32,2,8,4096]{3,2,1,0:T(8,128)}, ...), condition=%wide.region_5.6_spmd, body=%wide.region_0.5_spmd.sunk | while | flops 414126080 | bytes 33235484 | solution.py:113
  210.8 0.7 constant_dynamic-slice_fusion.6
  215.2 0.6 fusion.69
  219.5 0.6 fusion.74
  223.8 0.9 dynamic-slice_reduce_fusion.3
  224.8 1.0 dynamic-slice_bitcast_fusion.7
  225.9 1.0 fusion.70
  226.9 0.3 subtract_convert_fusion.2
  227.2 0.3 add.170
  227.5 0.3 sub.152
  227.9 0.5 fusion.71
  228.4 0.3 pad_maximum_fusion.2
  228.8 0.7 convolution_convert_fusion.2
  229.5 0.2 reshape.206
  230.0 0.3 fusion.77
  230.3 0.8 subtract_reduce_fusion.5
  231.1 0.3 fusion.73
  231.4 0.8 subtract_reduce_fusion.4
  232.2 1.7 fusion.76
  233.9 1.7 fusion.79
  235.6 0.6 constant_dynamic-slice_fusion.6
  240.1 0.6 fusion.69
  244.4 0.6 fusion.74
  248.6 0.9 dynamic-slice_reduce_fusion.3
  249.7 1.0 dynamic-slice_bitcast_fusion.7
  250.7 1.0 fusion.70
  251.8 0.3 subtract_convert_fusion.2
  252.0 0.3 add.170
  252.4 0.3 sub.152
  252.8 0.5 fusion.71
  253.3 0.3 pad_maximum_fusion.2
  253.6 0.7 convolution_convert_fusion.2
  254.9 0.3 fusion.77
  255.1 0.8 subtract_reduce_fusion.5
  256.0 0.3 fusion.73
  256.3 0.8 subtract_reduce_fusion.4
  257.1 1.7 fusion.76
  258.8 1.7 fusion.79
  260.5 195.1 %all_to_all.5 = f32[32,2,8,4096]{3,2,1,0:T(8,128)} all-to-all(f32[32,2,8,4096]{3,2,1,0:T(8,128)} %get-tuple-element.58), channel_id=1, replica_groups=mesh['tm'=8,'pair'=32] {'pair'}, dimensions={0} | all-to-all | bytes 16777216 | tf_op jit(solution)/shard_map/all_to_all | solution.py:115
  455.6 4.5 reduce_sum.45
  460.1 27.9 %reduce-scatter.2.cloned.1.call-done = f32[2,8,512]{2,1,0:T(8,128)} async-done(((f32[2,8,4096]{2,1,0:T(8,128)}), f32[2,8,512]{2,1,0:T(8,128)}) %reduce-scatter.2.cloned.1.call-update) | async-done | bytes 32784 | tf_op jit(solution)/shard_map/reduce_scatter | solution.py:118
  (34 shorter events, 2.1 us)
Async XLA Ops:
  6.5 3.5 copy-start
  6.5 195.2 %all-gather.2.cloned.1.call-start = ((), (), s32[]{:S(2)}) async-start(), calls=%async_computation.2 | async-start | bytes 4718592 | tf_op jit(solution)/shard_map/all_gather | solution.py:86
  7.3 480.7 %reduce-scatter.2.cloned.1.call-start = ((), (), s32[]{:S(2)}) async-start(), calls=%async_computation.3 | async-start | bytes 294912 | tf_op jit(solution)/shard_map/reduce_scatter | solution.py:118
  206.5 4.2 copy-start.1
  206.5 4.2 copy-start.2
Sparse Core Ops, SparseCore 0:
  9.2 36.9 all-gather.1
  460.2 27.7 reduce-scatter.1
where the time goes:
time: 500 us; the launch traced here: 495 us
  local copies, waits for them, and re-layouts  213 us (43%)
  blocking collectives  195 us (39%)
  waiting for transfers between devices  28.6 us (6%)
  loops' own time  22.5 us (4%)
  other arithmetic  16 us (3%)
  between operations  14.1 us (3%)
  matrix products  5.83 us (1%)
    all_to_all x1, blocking collectives, local(): lax.all_to_all(buffers, 'pair', split_axis=0, concat_axis=0, tiled=True)  195 us
    gather x1, local copies, waits for them, and re-layouts, toeplitz_table(): chosen = jnp.take(tap_values, tap_index)  192 us
    reduce_scatter x1, waiting for transfers between devices, local(): result = lax.psum_scatter(result, 'tm', scatter_dimension=2, tiled=True)  27.9 us
    another operation x1, loops' own time, local(): buffers = lax.fori_loop(0, turn_count, one_slot, buffers)  22.5 us
  transfers between devices with their start and end apart: 2, of which 1 were waited for; matrix products, arithmetic and copies ran while one was open for 39% of the time, Pallas kernels for 0%

commit v1 on v0

--- a/solution.py
+++ b/solution.py
@@ -8,12 +8,12 @@
 
 def toeplitz_table(tap_values):
     tap_count = tap_values.shape[0]
-    row_index = jnp.arange(2 * tap_count, dtype=jnp.int32)[:, None]
-    col_index = jnp.arange(tap_count, dtype=jnp.int32)[None, :]
-    lag_index = tap_count + col_index - row_index
-    tap_index = jnp.clip(lag_index - 1, 0, tap_count - 1)
-    chosen = jnp.take(tap_values, tap_index)
-    return jnp.where((lag_index >= 1) & (lag_index <= tap_count), chosen, jnp.zeros_like(chosen))
+    rows = 2 * tap_count
+    period = rows + tap_count
+    zeros = jnp.zeros((rows,), tap_values.dtype)
+    base = jnp.concatenate([tap_values[tap_count - 1:], zeros, tap_values[: tap_count - 1]])
+    tiled = jnp.tile(base, rows)[: rows * (period - 1)].reshape(rows, period - 1)
+    return tiled[:, :tap_count]
 
 
 def delayed(signal, toeplitz):
@@ -83,17 +83,16 @@
     blocks = mode_count // block_size
     live_count = live_slots[0]
     targets = target_blocks.reshape(slot_count, entries)
-    gathered = lax.all_gather(mode_fields, "tm", axis=2, tiled=True)
-    window = jnp.concatenate([jnp.zeros((2, mode_count, tap_count), jnp.bfloat16), gathered], 2)
-    first_slot = lax.axis_index("tm")
-    my_slots = slot_count // tm_count
+    halo = lax.ppermute(
+        mode_fields[:, :, -tap_count:], "tm", [(k, k + 1) for k in range(tm_count - 1)]
+    )
+    window = jnp.concatenate([halo, mode_fields], 2)
     full_length = window.shape[2]
     length = full_length - tap_count
     blocked = jnp.transpose(window.reshape(2, blocks, block_size, full_length), (1, 0, 2, 3))
     buffers = jnp.zeros((blocks, 2, block_size, length), jnp.float32)
 
-    def one_slot(turn_index, buffers):
-        slot_index = first_slot + tm_count * turn_index
+    def one_slot(slot_index, buffers):
         partials = slot_partials(
             blocked,
             pair_blocks[0, slot_index],
@@ -109,13 +108,12 @@
             )
         return buffers
 
-    turn_count = jnp.clip((live_count - first_slot + tm_count - 1) // tm_count, 0, my_slots)
+    turn_count = jnp.clip(live_count, 0, slot_count)
     buffers = lax.fori_loop(0, turn_count, one_slot, buffers)
     owned = blocks // pair_count
     received = lax.all_to_all(buffers, "pair", split_axis=0, concat_axis=0, tiled=True)
     shared = received.reshape(pair_count, owned, 2, block_size, length).sum(axis=0)
     result = jnp.transpose(shared, (1, 0, 2, 3)).reshape(2, owned * block_size, length)
-    result = lax.psum_scatter(result, "tm", scatter_dimension=2, tiled=True)
     return result
 
 

time: 500 us -> 315 us (0.63)
  local copies, waits for them, and re-layouts: 213 us -> 54.3 us
  loops' own time: 22.5 us -> 160 us
  blocking collectives: 195 us -> 70.6 us
  waiting for transfers between devices: 28.6 us -> 0.01 us
  between operations: 14.1 us -> 0.77 us
  other arithmetic: 16 us -> 6.76 us
  matrix products: 5.83 us -> 13.2 us
    gather x1 -> x0, local copies, waits for them, and re-layouts: 192 us -> none  [toeplitz_table(): chosen = jnp.take(tap_values, tap_index)]
    another operation x1, loops' own time: 22.5 us -> 160 us  [local(): buffers = lax.fori_loop(0, turn_count, one_slot, buffers)]
    all_to_all x1, blocking collectives: 195 us -> 70.6 us  [local(): lax.all_to_all(buffers, 'pair', split_axis=0, concat_axis=0, tiled=True)]
    reduce_scatter x1 -> x0, waiting for transfers between devices: 27.9 us -> none  [local(): result = lax.psum_scatter(result, 'tm', scatter_dimension=2, tiled=True)]
    slice x2 -> x14, local copies, waits for them, and re-layouts: 1.79 us -> 12.5 us  [slot_partials(): matrix = values[entry_index].reshape(square, square)]
    dynamic_slice x2 -> x14, local copies, waits for them, and re-layouts: 1.3 us -> 9.33 us  [one_slot(): target = targets[slot_index, entry_index]]
    slice x2 -> x14, local copies, waits for them, and re-layouts: 1.16 us -> 8.39 us  [slot_partials(): light_field = blocked[light_ids[entry_index]][:, :, tap_count:]]
    slice x2 -> x14, local copies, waits for them, and re-layouts: 1.17 us -> 8.36 us  [slot_partials(): left_field = blocked[pair_ids[0]]]
  transfers between devices with their start and end apart: 2 -> 1, of which waited for: 1 -> 0; matrix products, arithmetic and copies ran while one was open for 39% -> 2% of each run, Pallas kernels for 0% -> 0%
where the time goes in v1:
time: 315 us; the launch traced here: 309 us
  loops' own time  160 us (51%)
  blocking collectives  70.6 us (22%)
  local copies, waits for them, and re-layouts  54.3 us (17%)
  matrix products  13.2 us (4%)
  other arithmetic  6.76 us (2%)
  starting transfers between devices  3.68 us (1%)
    another operation x1, loops' own time, local(): buffers = lax.fori_loop(0, turn_count, one_slot, buffers)  160 us
    all_to_all x1, blocking collectives, local(): lax.all_to_all(buffers, 'pair', split_axis=0, concat_axis=0, tiled=True)  70.6 us
    slice x14, local copies, waits for them, and re-layouts, slot_partials(): matrix = values[entry_index].reshape(square, square)  12.5 us
    dynamic_slice x14, local copies, waits for them, and re-layouts, one_slot(): target = targets[slot_index, entry_index]  9.33 us
    slice x14, local copies, waits for them, and re-layouts, slot_partials(): light_field = blocked[light_ids[entry_index]][:, :, tap_count:]  8.39 us
    slice x14, local copies, waits for them, and re-layouts, slot_partials(): left_field = blocked[pair_ids[0]]  8.36 us
  transfers between devices with their start and end apart: 1, of which 0 were waited for; matrix products, arithmetic and copies ran while one was open for 2% of the time, Pallas kernels for 0%

profile of v1, /device:TPU:11, one launch (start us, length us, event | category | flops | bytes accessed | tf_op | source)
XLA Modules:
  0.0 309.3 jit_solution(10777855166568516423)
XLA Ops:
  0.0 1.0 slice.93
  1.0 3.7 %collective-permute-start = (bf16[2,256,128]{2,1,0:T(8,128)(2,1)S(1)}, bf16[2,256,128]{2,1,0:T(8,128)(2,1)S(1)}, u32[]{:S(2)}, u32[]{:S(2)}) collective-permute-start(bf16[2,256,128]{2,1,0:T(8,128)(2,1)S(1)} %slice.93), channel_id=1, source_target_pairs={{0,32},{32,64},{64,96},{96,128},{128,160},{160,192},{192,224},{1,3... | collective-permute-start | bytes 393224 | tf_op jit(solution)/shard_map/ppermute | solution.py:86
  5.3 1.3 slice.94
  7.2 1.2 reduce.9
  8.6 1.4 pad_maximum_fusion.1
  11.4 0.7 slice-done
  12.1 225.9 %while.10 = (s32[]{:T(128)}, f32[32,2,8,512]{3,2,1,0:T(8,128)S(1)}, s32[]{:T(128)}, s32[16,2]{0,1:T(2,128)S(1)}, s32[1,16,2]{1,2,0:T(2,128)S(1)}, /*index=5*/bf1...) while((s32[]{:T(128)}, f32[32,2,8,512]{3,2,1,0:T(8,128)S(1)}, ...), condition=%wide.region_5.6_spmd, body=%wide.region_0.5_spmd.sunk | while | flops 51826704 | bytes 5120515 | solution.py:112
  12.1 0.7 constant_dynamic-slice_fusion.6
  20.9 0.6 fusion.64
  25.3 0.9 dynamic-slice_reduce_fusion.3
  28.2 0.7 constant_dynamic-slice_fusion.6
  37.1 0.6 fusion.64
  41.4 0.9 dynamic-slice_reduce_fusion.3
  44.4 0.7 constant_dynamic-slice_fusion.6
  53.2 0.6 fusion.64
  57.6 0.9 dynamic-slice_reduce_fusion.3
  60.5 0.7 constant_dynamic-slice_fusion.6
  69.4 0.6 fusion.64
  73.7 0.9 dynamic-slice_reduce_fusion.3
  76.7 0.7 constant_dynamic-slice_fusion.6
  85.5 0.6 fusion.64
  89.9 0.9 dynamic-slice_reduce_fusion.3
  92.8 0.7 constant_dynamic-slice_fusion.6
  101.6 0.6 fusion.64
  106.0 0.9 dynamic-slice_reduce_fusion.3
  108.9 0.7 constant_dynamic-slice_fusion.6
  117.8 0.6 fusion.64
  122.1 0.9 dynamic-slice_reduce_fusion.3
  125.1 0.7 constant_dynamic-slice_fusion.6
  133.9 0.6 fusion.64
  138.3 0.9 dynamic-slice_reduce_fusion.3
  141.2 0.7 constant_dynamic-slice_fusion.6
  150.1 0.6 fusion.64
  154.4 0.9 dynamic-slice_reduce_fusion.3
  157.3 0.7 constant_dynamic-slice_fusion.6
  166.2 0.6 fusion.64
  170.5 0.9 dynamic-slice_reduce_fusion.3
  173.5 0.7 constant_dynamic-slice_fusion.6
  182.3 0.6 fusion.64
  186.7 0.9 dynamic-slice_reduce_fusion.3
  189.6 0.7 constant_dynamic-slice_fusion.6
  202.8 0.9 dynamic-slice_reduce_fusion.3
  205.8 0.7 constant_dynamic-slice_fusion.6
  219.0 0.9 dynamic-slice_reduce_fusion.3
  221.9 0.7 constant_dynamic-slice_fusion.6
  235.1 0.9 dynamic-slice_reduce_fusion.3
  238.0 70.6 %all_to_all.5 = f32[32,2,8,512]{3,2,1,0:T(8,128)S(1)} all-to-all(f32[32,2,8,512]{3,2,1,0:T(8,128)S(1)} %get-tuple-element.53), channel_id=1, replica_groups=mesh['tm'=8,'pair'=32] {'pair'}, dimensions={0} | all-to-all | bytes 2097152 | tf_op jit(solution)/shard_map/all_to_all | solution.py:114
  308.6 0.7 reduce_sum.45
  (387 shorter events, 39.5 us)
Async XLA Ops:
  0.0 10.6 %copy-start.1 = (bf16[2,256,512]{2,1,0:T(8,128)(2,1)S(1)}, bf16[2,256,512]{2,1,0:T(8,128)(2,1)}, u32[]{:S(2)}) copy-start(bf16[2,256,512]{2,1,0:T(8,128)(2,1)} %param.9) | copy-start | bytes 1572868
  1.0 9.6 %collective-permute-start = (bf16[2,256,128]{2,1,0:T(8,128)(2,1)S(1)}, bf16[2,256,128]{2,1,0:T(8,128)(2,1)S(1)}, u32[]{:S(2)}, u32[]{:S(2)}) collective-permute-start(bf16[2,256,128]{2,1,0:T(8,128)(2,1)S(1)} %slice.93), channel_id=1, source_target_pairs={{0,32},{32,64},{64,96},{96,128},{128,160},{160,192},{192,224},{1,3... | collective-permute-start | bytes 393224 | tf_op jit(solution)/shard_map/ppermute | solution.py:86
  10.6 0.7 copy-start
  10.7 0.7 copy-start.2
  10.7 0.7 copy-start.3
  11.3 0.8 slice-start

commit v2 on v1

--- a/solution.py
+++ b/solution.py
@@ -2,6 +2,8 @@
 import jax.numpy as jnp
 from jax import lax
 from jax.sharding import PartitionSpec as P
+from jax.experimental import pallas as pl
+from jax.experimental.pallas import tpu as pltpu
 
 MB = 8
 
@@ -69,6 +71,54 @@
     return partials
 
 
+def slot_kernel(pairs_ref, lights_ref, targets_ref, live_ref, fields_ref, table_ref, values_ref, out_ref):
+    block_size = fields_ref.shape[2]
+    width = fields_ref.shape[3]
+    length = out_ref.shape[3]
+    tap_count = width - length
+    square = block_size * block_size
+    entries = values_ref.shape[1]
+    slot_count = values_ref.shape[0]
+    out_ref[...] = jnp.zeros(out_ref.shape, out_ref.dtype)
+    table = table_ref[...]
+
+    def body(slot_index, carry):
+        left = pairs_ref[2 * slot_index]
+        right = pairs_ref[2 * slot_index + 1]
+        left_real = fields_ref[0, left].astype(jnp.float32)[:, None]
+        left_imag = fields_ref[1, left].astype(jnp.float32)[:, None]
+        right_real = fields_ref[0, right].astype(jnp.float32)[None]
+        right_imag = fields_ref[1, right].astype(jnp.float32)[None]
+        real_part = (left_real * right_real + left_imag * right_imag).reshape(square, width)
+        imag_part = (left_imag * right_real - left_real * right_imag).reshape(square, width)
+        intensity = jnp.concatenate([real_part, imag_part], 0).astype(jnp.bfloat16)
+        pieces = []
+        for piece in range(length // tap_count):
+            window = intensity[:, piece * tap_count:piece * tap_count + 2 * tap_count]
+            pieces.append(jnp.dot(window, table, preferred_element_type=jnp.float32))
+        response = jnp.concatenate(pieces, 1).astype(jnp.bfloat16)
+        for entry_index in range(entries):
+            matrix = values_ref[slot_index, entry_index]
+            mixed_real = jnp.dot(matrix, response[:square], preferred_element_type=jnp.float32).reshape(
+                block_size, block_size, length
+            )
+            mixed_imag = jnp.dot(matrix, response[square:], preferred_element_type=jnp.float32).reshape(
+                block_size, block_size, length
+            )
+            light = lights_ref[entries * slot_index + entry_index]
+            light_real = fields_ref[0, light, :, tap_count:].astype(jnp.float32)[None]
+            light_imag = fields_ref[1, light, :, tap_count:].astype(jnp.float32)[None]
+            out_real = jnp.sum(light_real * mixed_real - light_imag * mixed_imag, axis=1)
+            out_imag = jnp.sum(light_real * mixed_imag + light_imag * mixed_real, axis=1)
+            target = targets_ref[entries * slot_index + entry_index]
+            out_ref[target, 0] += out_real
+            out_ref[target, 1] += out_imag
+        return carry
+
+    live = jnp.clip(live_ref[0], 0, slot_count)
+    lax.fori_loop(0, live, body, 0)
+
+
 def local(
     mode_fields, raman_taps, pair_blocks, light_blocks, target_blocks, raman_values, live_slots
 ):
@@ -89,27 +139,24 @@
     window = jnp.concatenate([halo, mode_fields], 2)
     full_length = window.shape[2]
     length = full_length - tap_count
-    blocked = jnp.transpose(window.reshape(2, blocks, block_size, full_length), (1, 0, 2, 3))
-    buffers = jnp.zeros((blocks, 2, block_size, length), jnp.float32)
-
-    def one_slot(slot_index, buffers):
-        partials = slot_partials(
-            blocked,
-            pair_blocks[0, slot_index],
-            light_blocks[0, slot_index],
-            raman_values[0, slot_index],
-            toeplitz,
-        )
-        for entry_index in range(entries):
-            target = targets[slot_index, entry_index]
-            current = lax.dynamic_index_in_dim(buffers, target, 0, True)
-            buffers = lax.dynamic_update_index_in_dim(
-                buffers, current + partials[entry_index][None], target, 0
-            )
-        return buffers
-
-    turn_count = jnp.clip(live_count, 0, slot_count)
-    buffers = lax.fori_loop(0, turn_count, one_slot, buffers)
+    fields = window.reshape(2, blocks, block_size, full_length)
+    values = raman_values[0].reshape(slot_count, entries, block_size * block_size, block_size * block_size)
+    smem = pl.BlockSpec(memory_space=pltpu.SMEM)
+    vmem = pl.BlockSpec(memory_space=pltpu.VMEM)
+    buffers = pl.pallas_call(
+        slot_kernel,
+        out_shape=jax.ShapeDtypeStruct((blocks, 2, block_size, length), jnp.float32),
+        in_specs=[smem, smem, smem, smem, vmem, vmem, vmem],
+        out_specs=vmem,
+    )(
+        pair_blocks[0].reshape(-1),
+        light_blocks[0].reshape(-1),
+        target_blocks.reshape(-1),
+        live_slots,
+        fields,
+        toeplitz,
+        values,
+    )
     owned = blocks // pair_count
     received = lax.all_to_all(buffers, "pair", split_axis=0, concat_axis=0, tiled=True)
     shared = received.reshape(pair_count, owned, 2, block_size, length).sum(axis=0)

time: 315 us -> 63.9 us (0.20); the launches traced: 309 us -> 63.4 us
  loops' own time: 160 us -> 0 us
  local copies, waits for them, and re-layouts: 54.3 us -> 7.3 us
  blocking collectives: 70.6 us -> 38.5 us
  matrix products: 13.2 us -> 0 us
  Pallas kernels: 0 us -> 10.3 us
  other arithmetic: 6.76 us -> 2.89 us
    another operation x1 -> x0, loops' own time: 160 us -> none  [local(): buffers = lax.fori_loop(0, turn_count, one_slot, buffers)]
    slice x98 -> x0, local copies, waits for them, and re-layouts: 32.2 us -> none  [the longest x14 12.5 us: slot_partials(): matrix = values[entry_index].reshape(square, square)]
    all_to_all x1, blocking collectives: 70.6 us -> 38.5 us  [local(): lax.all_to_all(buffers, 'pair', split_axis=0, concat_axis=0, tiled=True)]
    dot_general x70 -> x0, matrix products: 13.2 us -> none  [the longest x28 6.13 us: slot_partials(): jnp.dot(matrix, response[square:], preferred_element_type=jnp.float32)]
    dynamic_slice x28 -> x0, local copies, waits for them, and re-layouts: 10.4 us -> none  [the longest x14 9.33 us: one_slot(): target = targets[slot_index, entry_index]]
    pallas_call x0 -> x1, Pallas kernels: none -> 10.3 us  [local(): pl.pallas_call(slot_kernel, out_shape=jax.ShapeDtypeStruct((blocks, 2, bl...]
  transfers between devices with their start and end apart: 1 -> 1, of which waited for: 0 -> 0; matrix products, arithmetic and copies ran while one was open for 2% -> 12% of each run, Pallas kernels for 0% -> 0%
where the time goes in v2:
time: 63.9 us; the launch traced here: 63.4 us
  blocking collectives  38.5 us (60%)
  Pallas kernels  10.3 us (16%)
  local copies, waits for them, and re-layouts  7.3 us (11%)
  starting transfers between devices  3.68 us (6%)
  other arithmetic  2.89 us (5%)
  between operations  0.68 us (1%)
    all_to_all x1, blocking collectives, local(): lax.all_to_all(buffers, 'pair', split_axis=0, concat_axis=0, tiled=True)  38.5 us
    pallas_call x1, Pallas kernels, local(): pl.pallas_call(slot_kernel, out_shape=jax.ShapeDtypeStruct((blocks, 2, bl...  10.3 us
    ppermute x1, starting transfers between devices, local(): lax.ppermute(mode_fields[:, :, -tap_count:], 'tm', [(k, k + 1) for k in r...  3.68 us
    unnamed x6, local copies, waits for them, and re-layouts  1.52 us
    concatenate x1, other arithmetic, toeplitz_table(): jnp.concatenate([tap_values[tap_count - 1:], zeros, tap_values[:tap_count...  1.29 us
  transfers between devices with their start and end apart: 1, of which 0 were waited for; matrix products, arithmetic and copies ran while one was open for 12% of the time, Pallas kernels for 0%

profile of v2, /device:TPU:11, one launch (start us, length us, event | category | flops | bytes accessed | tf_op | source)
XLA Modules:
  0.0 63.4 jit_solution(2595383195598214015)
XLA Ops:
  0.0 0.0 copy-start
  0.0 0.0 copy-start.1
  0.0 1.0 %slice.15 = bf16[2,256,128]{2,1,0:T(8,128)(2,1)S(1)} slice(bf16[2,256,512]{2,1,0:T(8,128)(2,1)} %param.7), slice={[0:2], [0:256], [384:512]} | slice | bytes 262144 | tf_op jit(solution)/shard_map/slice | solution.py:137
  1.0 3.7 %collective-permute-start = (bf16[2,256,128]{2,1,0:T(8,128)(2,1)S(1)}, bf16[2,256,128]{2,1,0:T(8,128)(2,1)S(1)}, u32[]{:S(2)}, u32[]{:S(2)}) collective-permute-start(bf16[2,256,128]{2,1,0:T(8,128)(2,1)S(1)} %slice.15), channel_id=1, source_target_pairs={{0,32},{32,64},{64,96},{96,128},{128,160},{160,192},{192,224},{1,3... | collective-permute-start | bytes 393224 | tf_op jit(solution)/shard_map/ppermute | solution.py:136
  5.3 1.2 %slice.16 = bf16[1]{0:T(256)(128)(2,1)} slice(bf16[128]{0:T(256)(128)(2,1)} %param.8), slice={[127:128]} | slice | bytes 4 | tf_op jit(solution)/shard_map/slice | solution.py:16
  6.6 0.8 %copy.10 = s32[1,16,2]{2,1,0:T(8,128)S(1)} copy(s32[1,16,2]{1,2,0:T(2,128)} %param.9) | data formatting | bytes 256 | tf_op args[2]
  7.3 0.6 reshape_squeeze.9.pairs_ref
  7.9 0.8 %copy.11 = s32[1,16,2]{2,1,0:T(8,128)S(1)} copy(s32[1,16,2]{1,2,0:T(2,128)} %param.10) | data formatting | bytes 256 | tf_op args[3]
  8.7 0.6 reshape_squeeze.10.lights_ref
  9.3 1.3 %pad_maximum_fusion = bf16[384]{0:T(512)(128)(2,1)S(1)} fusion(bf16[127]{0:T(256)(128)(2,1)} %bitcast.6, bf16[256]{0:T(256)(128)(2,1)S(1)} %broadcast_in_dim.3, bf16[1]{0:T(256)(128)(2,1)} %slice.16), kind=kLoop, calls=%fused_computation.1 | loop fusion | flops 2304 | bytes 1536 | tf_op jit(solution)/shard_map/concatenate | solution.py:16
  10.6 0.1 tile.10
  10.7 0.5 reshape.15
  11.1 0.6 %slice.21.table_ref = bf16[256,128]{1,0:T(8,128)(2,1)} slice(bf16[256,383]{1,0:T(8,128)(2,1)S(1)} %reshape.15), slice={[0:256], [0:128]} | slice | bytes 131072 | tf_op jit(solution)/shard_map/slice | solution.py:18
  11.8 0.0 copy-done.1
  11.8 1.2 %reshape_squeeze.11.values_ref = bf16[16,2,64,64]{3,2,1,0:T(8,128)(2,1)} reshape(bf16[1,16,2,4096]{3,2,1,0:T(2,128)(2,1)S(1)} %copy-done.1) | data formatting | bytes 524288 | tf_op jit(solution)/shard_map/reshape;squeeze | solution.py:143
  13.0 0.0 collective-permute-done
  13.0 0.0 copy-done
  13.0 0.9 %maximum_bitcast_fusion.fields_ref = bf16[2,32,8,640]{3,2,1,0:T(8,128)(2,1)} fusion(bf16[2,256,512]{2,1,0:T(8,128)(2,1)S(1)} %copy-done, bf16[2,256,128]{2,1,0:T(8,128)(2,1)S(1)} %collective-permute-done), kind=kLoop, calls=%fused_computation | loop fusion | flops 1310720 | bytes 1310720 | tf_op jit(solution)/shard_map/reshape | solution.py:142
  13.9 10.3 %shard_map.73 = f32[32,2,8,512]{3,2,1,0:T(8,128)} custom-call(s32[32]{0:T(128)} %reshape_squeeze.9.pairs_ref, s32[32]{0:T(128)} %reshape_squeeze.10.lights_ref, s32[32]{0:T(128)} %bitcast.7, s32[1]{0:T(128)S(6)} %copy.12.live_ref, bf16[2,32,8,640]{3,2,1,0:T(8,128)(2,1)} %maximum_bitcast_fusion.fields_ref, bf16[256,128]{1,0:T(8,128)(2,1)} %slice.21.table_ref, ...), custom_call_target="tpu_custom_call" | custom-call | tf_op jit(solution)/shard_map/pallas_call | solution.py:146
  24.2 38.5 %all_to_all.5 = f32[32,2,8,512]{3,2,1,0:T(8,128)S(1)} all-to-all(f32[32,2,8,512]{3,2,1,0:T(8,128)} %shard_map.73), channel_id=1, replica_groups=mesh['tm'=8,'pair'=32] {'pair'}, dimensions={0} | all-to-all | bytes 2097152 | tf_op jit(solution)/shard_map/all_to_all | solution.py:161
  62.7 0.7 %reduce_sum.9 = f32[2,8,512]{2,1,0:T(8,128)} reduce(f32[32,2,8,512]{3,2,1,0:T(8,128)S(1)} %all_to_all.5, f32[]{:T(128)} %constant.1.clone.1), dimensions={0}, to_apply=%region_0.0 | reduce | flops 253952 | bytes 1081348 | tf_op jit(solution)/shard_map/reduce_sum | solution.py:162
  (2 shorter events, 0.0 us)
Async XLA Ops:
  0.0 13.0 %copy-start = (bf16[2,256,512]{2,1,0:T(8,128)(2,1)S(1)}, bf16[2,256,512]{2,1,0:T(8,128)(2,1)}, u32[]{:S(2)}) copy-start(bf16[2,256,512]{2,1,0:T(8,128)(2,1)} %param.7) | copy-start | bytes 1572868
  0.0 11.8 %copy-start.1 = (bf16[1,16,2,4096]{3,2,1,0:T(2,128)(2,1)S(1)}, bf16[1,16,2,4096]{3,2,1,0:T(2,128)(2,1)}, u32[]{:S(2)}) copy-start(bf16[1,16,2,4096]{3,2,1,0:T(2,128)(2,1)} %param.12) | copy-start | bytes 786436
  1.0 12.0 %collective-permute-start = (bf16[2,256,128]{2,1,0:T(8,128)(2,1)S(1)}, bf16[2,256,128]{2,1,0:T(8,128)(2,1)S(1)}, u32[]{:S(2)}, u32[]{:S(2)}) collective-permute-start(bf16[2,256,128]{2,1,0:T(8,128)(2,1)S(1)} %slice.15), channel_id=1, source_target_pairs={{0,32},{32,64},{64,96},{96,128},{128,160},{160,192},{192,224},{1,3... | collective-permute-start | bytes 393224 | tf_op jit(solution)/shard_map/ppermute | solution.py:136

commit v3 on v2

--- a/solution.py
+++ b/solution.py
@@ -131,8 +131,6 @@
     entries = light_blocks.shape[2]
     mode_count = mode_fields.shape[1]
     blocks = mode_count // block_size
-    live_count = live_slots[0]
-    targets = target_blocks.reshape(slot_count, entries)
     halo = lax.ppermute(
         mode_fields[:, :, -tap_count:], "tm", [(k, k + 1) for k in range(tm_count - 1)]
     )
@@ -158,8 +156,7 @@
         values,
     )
     owned = blocks // pair_count
-    received = lax.all_to_all(buffers, "pair", split_axis=0, concat_axis=0, tiled=True)
-    shared = received.reshape(pair_count, owned, 2, block_size, length).sum(axis=0)
+    shared = lax.psum_scatter(buffers, "pair", scatter_dimension=0, tiled=True)
     result = jnp.transpose(shared, (1, 0, 2, 3)).reshape(2, owned * block_size, length)
     return result
 

time: 63.9 us -> 254 us (3.97)
  the two profiles are of different devices: /device:TPU:11 before, /device:TPU:2 now
where the time goes in v3:
time: 254 us
  waiting for transfers between devices  219 us (86%)
  between operations  14.1 us (6%)
  Pallas kernels  9.79 us (4%)
  local copies, waits for them, and re-layouts  7.36 us (3%)
    reduce_scatter x1, waiting for transfers between devices, local(): shared = lax.psum_scatter(buffers, 'pair', scatter_dimension=0, tiled=True)  219 us
    pallas_call x1, Pallas kernels, local(): pl.pallas_call(slot_kernel, out_shape=jax.ShapeDtypeStruct((blocks, 2, bl...  9.79 us
  transfers between devices with their start and end apart: 2, of which 1 were waited for; matrix products, arithmetic and copies ran while one was open for 3% of the time, Pallas kernels for 0%

profile of v3, /device:TPU:2, one launch (start us, length us, event | category | flops | bytes accessed | tf_op | source)
XLA Modules:
  0.0 254.0 jit_solution(8782748422552459008)
XLA Ops:
  6.5 0.0 copy-start
  6.5 0.0 copy-start.1
  6.5 0.0 reduce-scatter.2.cloned.1.call-start
  6.5 1.0 slice.15
  7.5 1.9 collective-permute-start
  10.1 1.3 slice.16
  11.4 0.8 copy.10
  12.1 0.6 reshape_squeeze.9.pairs_ref
  12.7 0.8 copy.11
  13.5 0.6 reshape_squeeze.10.lights_ref
  14.1 1.3 pad_maximum_fusion
  15.5 0.1 tile.10
  15.6 0.5 reshape.12
  16.0 0.6 slice.21.table_ref
  16.7 0.0 copy-done.1
  16.7 1.2 reshape_squeeze.11.values_ref
  17.8 0.0 collective-permute-done
  17.8 0.0 copy-done
  17.8 0.9 maximum_bitcast_fusion.fields_ref
  18.8 9.8 %shard_map.73 = f32[32,2,8,512]{3,2,1,0:T(8,128)} custom-call(s32[32]{0:T(128)} %reshape_squeeze.9.pairs_ref, s32[32]{0:T(128)} %reshape_squeeze.10.lights_ref, s32[32]{0:T(128)} %bitcast.8, s32[1]{0:T(128)S(6)} %copy.12.live_ref, bf16[2,32,8,640]{3,2,1,0:T(8,128)(2,1)} %maximum_bitcast_fusion.fields_ref, bf16[256,128]{1,0:T(8,128)(2,1)} %slice.21.table_ref, ...), custom_call_target="tpu_custom_call" | custom-call | tf_op jit(solution)/shard_map/pallas_call | solution.py:144
  28.6 0.0 reduce-scatter.2.cloned.1.call-update
  28.6 218.6 %reduce-scatter.2.cloned.1.call-done = f32[1,2,8,512]{3,2,1,0:T(8,128)} async-done(((f32[32,2,8,512]{3,2,1,0:T(8,128)}), f32[1,2,8,512]{3,2,1,0:T(8,128)}) %reduce-scatter.2.cloned.1.call-update) | async-done | bytes 32784 | tf_op jit(solution)/shard_map/reduce_scatter | solution.py:159
  (2 shorter events, 0.0 us)
Async XLA Ops:
  6.5 11.3 %copy-start = (bf16[2,256,512]{2,1,0:T(8,128)(2,1)S(1)}, bf16[2,256,512]{2,1,0:T(8,128)(2,1)}, u32[]{:S(2)}) copy-start(bf16[2,256,512]{2,1,0:T(8,128)(2,1)} %param.7) | copy-start | bytes 1572868
  6.5 10.1 %copy-start.1 = (bf16[1,16,2,4096]{3,2,1,0:T(2,128)(2,1)S(1)}, bf16[1,16,2,4096]{3,2,1,0:T(2,128)(2,1)}, u32[]{:S(2)}) copy-start(bf16[1,16,2,4096]{3,2,1,0:T(2,128)(2,1)} %param.12) | copy-start | bytes 786436
  6.5 240.7 %reduce-scatter.2.cloned.1.call-start = ((), (), s32[]{:S(2)}) async-start(), calls=%async_computation.1 | async-start | bytes 1081344 | tf_op jit(solution)/shard_map/reduce_scatter | solution.py:159
  7.5 10.3 %collective-permute-start = (bf16[2,256,128]{2,1,0:T(8,128)(2,1)S(1)}, bf16[2,256,128]{2,1,0:T(8,128)(2,1)S(1)}, u32[]{:S(2)}, u32[]{:S(2)}) collective-permute-start(bf16[2,256,128]{2,1,0:T(8,128)(2,1)S(1)} %slice.15), channel_id=1, source_target_pairs={{0,32},{32,64},{64,96},{96,128},{128,160},{160,192},{192,224},{1,3... | collective-permute-start | bytes 393224 | tf_op jit(solution)/shard_map/ppermute | solution.py:134
Sparse Core Ops, SparseCore 0:
  28.7 218.4 reduce-scatter.1

commit v4 on v3

--- a/solution.py
+++ b/solution.py
@@ -117,6 +117,60 @@
 
     live = jnp.clip(live_ref[0], 0, slot_count)
     lax.fori_loop(0, live, body, 0)
+
+
+def exchange_kernel(buffers_ref, out_ref, recv_ref, send_sems, recv_sems):
+    pair_count = buffers_ref.shape[0]
+    me = lax.axis_index("pair")
+    row = lax.axis_index("tm")
+    mesh_ids = pl.DeviceIdType.MESH
+    barrier = pltpu.get_barrier_semaphore()
+
+    def greet(step, carry):
+        peer = lax.rem(me + step, pair_count)
+        pl.semaphore_signal(barrier, inc=1, device_id=(row, peer), device_id_type=mesh_ids)
+        return carry
+
+    lax.fori_loop(1, pair_count, greet, 0)
+    pl.semaphore_wait(barrier, pair_count - 1)
+
+    def outgoing(peer):
+        return pltpu.make_async_remote_copy(
+            src_ref=buffers_ref.at[peer],
+            dst_ref=recv_ref.at[me],
+            send_sem=send_sems.at[peer],
+            recv_sem=recv_sems.at[me],
+            device_id=(row, peer),
+            device_id_type=mesh_ids,
+        )
+
+    def send(step, carry):
+        outgoing(lax.rem(me + step, pair_count)).start()
+        return carry
+
+    lax.fori_loop(1, pair_count, send, 0)
+
+    def gather(step, total):
+        peer = lax.rem(me + pair_count - step, pair_count)
+        incoming = pltpu.make_async_remote_copy(
+            src_ref=buffers_ref.at[peer],
+            dst_ref=recv_ref.at[peer],
+            send_sem=send_sems.at[peer],
+            recv_sem=recv_sems.at[peer],
+            device_id=(row, peer),
+            device_id_type=mesh_ids,
+        )
+        incoming.wait_recv()
+        return total + recv_ref[peer]
+
+    total = lax.fori_loop(1, pair_count, gather, buffers_ref[me])
+
+    def finish(step, carry):
+        outgoing(lax.rem(me + step, pair_count)).wait_send()
+        return carry
+
+    lax.fori_loop(1, pair_count, finish, 0)
+    out_ref[...] = total
 
 
 def local(
@@ -156,7 +210,19 @@
         values,
     )
     owned = blocks // pair_count
-    shared = lax.psum_scatter(buffers, "pair", scatter_dimension=0, tiled=True)
+    grouped = buffers.reshape(pair_count, owned, 2, block_size, length)
+    shared = pl.pallas_call(
+        exchange_kernel,
+        out_shape=jax.ShapeDtypeStruct((owned, 2, block_size, length), jnp.float32),
+        in_specs=[vmem],
+        out_specs=vmem,
+        scratch_shapes=[
+            pltpu.VMEM(grouped.shape, jnp.float32),
+            pltpu.SemaphoreType.DMA((pair_count,)),
+            pltpu.SemaphoreType.DMA((pair_count,)),
+        ],
+        compiler_params=pltpu.CompilerParams(collective_id=0, has_side_effects=True),
+    )(grouped)
     result = jnp.transpose(shared, (1, 0, 2, 3)).reshape(2, owned * block_size, length)
     return result
 

time: 254 us -> 61.7 us (0.24)
  the two profiles are of different devices: /device:TPU:2 before, /device:TPU:11 now
where the time goes in v4:
time: 61.7 us; the launch traced here: 60.5 us
  Pallas kernels  45 us (73%)
  local copies, waits for them, and re-layouts  8.82 us (14%)
  starting transfers between devices  3.68 us (6%)
  other arithmetic  2.31 us (4%)
  between operations  0.69 us (1%)
    pallas_call x1, Pallas kernels, local(): pl.pallas_call(exchange_kernel, out_shape=jax.ShapeDtypeStruct((owned, 2,...  35.7 us
    pallas_call x1, Pallas kernels, local(): pl.pallas_call(slot_kernel, out_shape=jax.ShapeDtypeStruct((blocks, 2, bl...  9.29 us
    ppermute x1, starting transfers between devices, local(): lax.ppermute(mode_fields[:, :, -tap_count:], 'tm', [(k, k + 1) for k in r...  3.68 us
    unnamed x7, local copies, waits for them, and re-layouts  2.89 us
    concatenate x1, other arithmetic, toeplitz_table(): jnp.concatenate([tap_values[tap_count - 1:], zeros, tap_values[:tap_count...  1.36 us
    slice x1, local copies, waits for them, and re-layouts, toeplitz_table(): tap_values[tap_count - 1:]  1.3 us
  transfers between devices with their start and end apart: 1, of which 0 were waited for; matrix products, arithmetic and copies ran while one was open for 13% of the time, Pallas kernels for 0%

profile of v4, /device:TPU:11, one launch (start us, length us, event | category | flops | bytes accessed | tf_op | source)
XLA Modules:
  0.0 60.5 jit_solution(2390161006448305501)
XLA Ops:
  0.0 0.0 copy-start
  0.0 0.0 copy-start.1
  0.0 1.0 %slice.15 = bf16[2,256,128]{2,1,0:T(8,128)(2,1)S(1)} slice(bf16[2,256,512]{2,1,0:T(8,128)(2,1)} %param.7), slice={[0:2], [0:256], [384:512]} | slice | bytes 262144 | tf_op jit(solution)/shard_map/slice | solution.py:189
  1.0 3.7 %collective-permute-start = (bf16[2,256,128]{2,1,0:T(8,128)(2,1)S(1)}, bf16[2,256,128]{2,1,0:T(8,128)(2,1)S(1)}, u32[]{:S(2)}, u32[]{:S(2)}) collective-permute-start(bf16[2,256,128]{2,1,0:T(8,128)(2,1)S(1)} %slice.15), channel_id=1, source_target_pairs={{0,32},{32,64},{64,96},{96,128},{128,160},{160,192},{192,224},{1,3... | collective-permute-start | bytes 393224 | tf_op jit(solution)/shard_map/ppermute | solution.py:188
  5.3 1.3 %slice.16 = bf16[1]{0:T(256)(128)(2,1)} slice(bf16[128]{0:T(256)(128)(2,1)} %param.8), slice={[127:128]} | slice | bytes 4 | tf_op jit(solution)/shard_map/slice | solution.py:16
  6.6 0.8 %copy.10 = s32[1,16,2]{2,1,0:T(8,128)S(1)} copy(s32[1,16,2]{1,2,0:T(2,128)} %param.9) | data formatting | bytes 256 | tf_op args[2]
  7.4 0.6 reshape_squeeze.9.pairs_ref
  8.0 0.8 %copy.11 = s32[1,16,2]{2,1,0:T(8,128)S(1)} copy(s32[1,16,2]{1,2,0:T(2,128)} %param.10) | data formatting | bytes 256 | tf_op args[3]
  8.7 0.6 %reshape_squeeze.10.lights_ref = s32[32]{0:T(128)} reshape(s32[1,16,2]{2,1,0:T(8,128)S(1)} %copy.11) | data formatting | bytes 256 | tf_op jit(solution)/shard_map/reshape;squeeze | solution.py:205
  9.4 1.4 %pad_maximum_fusion = bf16[384]{0:T(512)(128)(2,1)S(1)} fusion(bf16[127]{0:T(256)(128)(2,1)} %bitcast.10, bf16[256]{0:T(256)(128)(2,1)S(1)} %broadcast_in_dim.3, bf16[1]{0:T(256)(128)(2,1)} %slice.16), kind=kLoop, calls=%fused_computation.1 | loop fusion | flops 2304 | bytes 1536 | tf_op jit(solution)/shard_map/concatenate | solution.py:16
  10.8 0.1 tile.10
  10.9 0.5 reshape.15
  11.3 0.6 %slice.21.table_ref = bf16[256,128]{1,0:T(8,128)(2,1)} slice(bf16[256,383]{1,0:T(8,128)(2,1)S(1)} %reshape.15), slice={[0:256], [0:128]} | slice | bytes 131072 | tf_op jit(solution)/shard_map/slice | solution.py:18
  12.0 0.0 copy-done.1
  12.0 1.2 %reshape_squeeze.11.values_ref = bf16[16,2,64,64]{3,2,1,0:T(8,128)(2,1)} reshape(bf16[1,16,2,4096]{3,2,1,0:T(2,128)(2,1)S(1)} %copy-done.1) | data formatting | bytes 524288 | tf_op jit(solution)/shard_map/reshape;squeeze | solution.py:195
  13.2 0.0 collective-permute-done
  13.2 0.0 copy-done
  13.2 0.9 %maximum_bitcast_fusion.fields_ref = bf16[2,32,8,640]{3,2,1,0:T(8,128)(2,1)} fusion(bf16[2,256,512]{2,1,0:T(8,128)(2,1)S(1)} %copy-done, bf16[2,256,128]{2,1,0:T(8,128)(2,1)S(1)} %collective-permute-done), kind=kLoop, calls=%fused_computation | loop fusion | flops 1310720 | bytes 1310720 | tf_op jit(solution)/shard_map/reshape | solution.py:194
  14.1 9.3 %shard_map.73 = f32[32,2,8,512]{3,2,1,0:T(8,128)} custom-call(s32[32]{0:T(128)} %reshape_squeeze.9.pairs_ref, s32[32]{0:T(128)} %reshape_squeeze.10.lights_ref, s32[32]{0:T(128)} %bitcast.11, s32[1]{0:T(128)S(6)} %copy.13.live_ref, bf16[2,32,8,640]{3,2,1,0:T(8,128)(2,1)} %maximum_bitcast_fusion.fields_ref, bf16[256,128]{1,0:T(8,128)(2,1)} %slice.21.table_ref, ...), custom_call_target="tpu_custom_call" | custom-call | tf_op jit(solution)/shard_map/pallas_call | solution.py:198
  23.4 35.7 %shard_map.74 = f32[1,2,8,512]{3,2,1,0:T(8,128)} custom-call(f32[32,1,2,8,512]{4,3,2,1,0:T(8,128)} %bitcast.7), custom_call_target="tpu_custom_call" | custom-call | tf_op jit(solution)/shard_map/pallas_call | solution.py:214
  59.1 1.4 %copy.14 = f32[2,8,512]{2,1,0:T(8,128)} copy(f32[2,8,512]{2,1,0:T(8,128)} %bitcast.9) | data formatting | bytes 65536
  (2 shorter events, 0.0 us)
Async XLA Ops:
  0.0 13.2 %copy-start = (bf16[2,256,512]{2,1,0:T(8,128)(2,1)S(1)}, bf16[2,256,512]{2,1,0:T(8,128)(2,1)}, u32[]{:S(2)}) copy-start(bf16[2,256,512]{2,1,0:T(8,128)(2,1)} %param.7) | copy-start | bytes 1572868
  0.0 12.0 %copy-start.1 = (bf16[1,16,2,4096]{3,2,1,0:T(2,128)(2,1)S(1)}, bf16[1,16,2,4096]{3,2,1,0:T(2,128)(2,1)}, u32[]{:S(2)}) copy-start(bf16[1,16,2,4096]{3,2,1,0:T(2,128)(2,1)} %param.12) | copy-start | bytes 786436
  1.0 12.2 %collective-permute-start = (bf16[2,256,128]{2,1,0:T(8,128)(2,1)S(1)}, bf16[2,256,128]{2,1,0:T(8,128)(2,1)S(1)}, u32[]{:S(2)}, u32[]{:S(2)}) collective-permute-start(bf16[2,256,128]{2,1,0:T(8,128)(2,1)S(1)} %slice.15), channel_id=1, source_target_pairs={{0,32},{32,64},{64,96},{96,128},{128,160},{160,192},{192,224},{1,3... | collective-permute-start | bytes 393224 | tf_op jit(solution)/shard_map/ppermute | solution.py:188

commit v5 on v4

--- a/solution.py
+++ b/solution.py
@@ -71,7 +71,7 @@
     return partials
 
 
-def slot_kernel(pairs_ref, lights_ref, targets_ref, live_ref, fields_ref, table_ref, values_ref, out_ref):
+def slot_kernel(pairs_ref, lights_ref, targets_ref, live_ref, fields_ref, table_ref, values_ref, out_ref, acc_ref):
     block_size = fields_ref.shape[2]
     width = fields_ref.shape[3]
     length = out_ref.shape[3]
@@ -79,7 +79,7 @@
     square = block_size * block_size
     entries = values_ref.shape[1]
     slot_count = values_ref.shape[0]
-    out_ref[...] = jnp.zeros(out_ref.shape, out_ref.dtype)
+    acc_ref[...] = jnp.zeros(acc_ref.shape, acc_ref.dtype)
     table = table_ref[...]
 
     def body(slot_index, carry):
@@ -111,12 +111,13 @@
             out_real = jnp.sum(light_real * mixed_real - light_imag * mixed_imag, axis=1)
             out_imag = jnp.sum(light_real * mixed_imag + light_imag * mixed_real, axis=1)
             target = targets_ref[entries * slot_index + entry_index]
-            out_ref[target, 0] += out_real
-            out_ref[target, 1] += out_imag
+            acc_ref[target, 0] += out_real
+            acc_ref[target, 1] += out_imag
         return carry
 
     live = jnp.clip(live_ref[0], 0, slot_count)
     lax.fori_loop(0, live, body, 0)
+    out_ref[...] = acc_ref[...].astype(out_ref.dtype)
 
 
 def exchange_kernel(buffers_ref, out_ref, recv_ref, send_sems, recv_sems):
@@ -161,9 +162,9 @@
             device_id_type=mesh_ids,
         )
         incoming.wait_recv()
-        return total + recv_ref[peer]
-
-    total = lax.fori_loop(1, pair_count, gather, buffers_ref[me])
+        return total + recv_ref[peer].astype(jnp.float32)
+
+    total = lax.fori_loop(1, pair_count, gather, buffers_ref[me].astype(jnp.float32))
 
     def finish(step, carry):
         outgoing(lax.rem(me + step, pair_count)).wait_send()
@@ -197,9 +198,10 @@
     vmem = pl.BlockSpec(memory_space=pltpu.VMEM)
     buffers = pl.pallas_call(
         slot_kernel,
-        out_shape=jax.ShapeDtypeStruct((blocks, 2, block_size, length), jnp.float32),
+        out_shape=jax.ShapeDtypeStruct((blocks, 2, block_size, length), jnp.bfloat16),
         in_specs=[smem, smem, smem, smem, vmem, vmem, vmem],
         out_specs=vmem,
+        scratch_shapes=[pltpu.VMEM((blocks, 2, block_size, length), jnp.float32)],
     )(
         pair_blocks[0].reshape(-1),
         light_blocks[0].reshape(-1),
@@ -217,7 +219,7 @@
         in_specs=[vmem],
         out_specs=vmem,
         scratch_shapes=[
-            pltpu.VMEM(grouped.shape, jnp.float32),
+            pltpu.VMEM(grouped.shape, grouped.dtype),
             pltpu.SemaphoreType.DMA((pair_count,)),
             pltpu.SemaphoreType.DMA((pair_count,)),
         ],

time: 61.7 us -> 50.8 us (0.82)
  the two profiles are of different devices: /device:TPU:11 before, /device:TPU:1 now
where the time goes in v5:
time: 50.8 us; the launch traced here: 50.5 us
  Pallas kernels  34.2 us (67%)
  local copies, waits for them, and re-layouts  8.8 us (17%)
  starting transfers between devices  4.51 us (9%)
  other arithmetic  2.27 us (4%)
  between operations  0.7 us (1%)
    pallas_call x1, Pallas kernels, local(): pl.pallas_call(exchange_kernel, out_shape=jax.ShapeDtypeStruct((owned, 2,...  24 us
    pallas_call x1, Pallas kernels, local(): pl.pallas_call(slot_kernel, out_shape=jax.ShapeDtypeStruct((blocks, 2, bl...  10.1 us
    ppermute x1, starting transfers between devices, local(): lax.ppermute(mode_fields[:, :, -tap_count:], 'tm', [(k, k + 1) for k in r...  4.51 us
    unnamed x7, local copies, waits for them, and re-layouts  2.89 us
    concatenate x1, other arithmetic, toeplitz_table(): jnp.concatenate([tap_values[tap_count - 1:], zeros, tap_values[:tap_count...  1.36 us
    slice x1, local copies, waits for them, and re-layouts, toeplitz_table(): tap_values[tap_count - 1:]  1.3 us
    another operation x1, local copies, waits for them, and re-layouts, local(): raman_values[0]  1.21 us
  transfers between devices with their start and end apart: 1, of which 0 were waited for; matrix products, arithmetic and copies ran while one was open for 16% of the time, Pallas kernels for 0%

profile of v5, /device:TPU:1, one launch (start us, length us, event | category | flops | bytes accessed | tf_op | source)
XLA Modules:
  0.0 50.5 jit_solution(13179339500001684594)
XLA Ops:
  0.0 0.0 copy-start.1
  0.0 1.0 %slice.15 = bf16[2,256,128]{2,1,0:T(8,128)(2,1)S(1)} slice(bf16[2,256,512]{2,1,0:T(8,128)(2,1)} %param.7), slice={[0:2], [0:256], [384:512]} | slice | bytes 262144 | tf_op jit(solution)/shard_map/slice | solution.py:190
  1.0 4.5 %collective-permute-start = (bf16[2,256,128]{2,1,0:T(8,128)(2,1)S(1)}, bf16[2,256,128]{2,1,0:T(8,128)(2,1)S(1)}, u32[]{:S(2)}, u32[]{:S(2)}) collective-permute-start(bf16[2,256,128]{2,1,0:T(8,128)(2,1)S(1)} %slice.15), channel_id=1, source_target_pairs={{0,32},{32,64},{64,96},{96,128},{128,160},{160,192},{192,224},{1,3... | collective-permute-start | bytes 393224 | tf_op jit(solution)/shard_map/ppermute | solution.py:189
  6.1 1.3 %slice.16 = bf16[1]{0:T(256)(128)(2,1)} slice(bf16[128]{0:T(256)(128)(2,1)} %param.8), slice={[127:128]} | slice | bytes 4 | tf_op jit(solution)/shard_map/slice | solution.py:16
  7.4 0.8 %copy.10 = s32[1,16,2]{2,1,0:T(8,128)S(1)} copy(s32[1,16,2]{1,2,0:T(2,128)} %param.9) | data formatting | bytes 256 | tf_op args[2]
  8.2 0.6 %reshape_squeeze.9.pairs_ref = s32[32]{0:T(128)} reshape(s32[1,16,2]{2,1,0:T(8,128)S(1)} %copy.10) | data formatting | bytes 256 | tf_op jit(solution)/shard_map/reshape;squeeze | solution.py:206
  8.8 0.8 %copy.11 = s32[1,16,2]{2,1,0:T(8,128)S(1)} copy(s32[1,16,2]{1,2,0:T(2,128)} %param.10) | data formatting | bytes 256 | tf_op args[3]
  9.5 0.6 %reshape_squeeze.10.lights_ref = s32[32]{0:T(128)} reshape(s32[1,16,2]{2,1,0:T(8,128)S(1)} %copy.11) | data formatting | bytes 256 | tf_op jit(solution)/shard_map/reshape;squeeze | solution.py:207
  10.2 1.4 %pad_maximum_fusion = bf16[384]{0:T(512)(128)(2,1)S(1)} fusion(bf16[127]{0:T(256)(128)(2,1)} %bitcast.10, bf16[256]{0:T(256)(128)(2,1)S(1)} %broadcast_in_dim.3, bf16[1]{0:T(256)(128)(2,1)} %slice.16), kind=kLoop, calls=%fused_computation.1 | loop fusion | flops 2304 | bytes 1536 | tf_op jit(solution)/shard_map/concatenate | solution.py:16
  11.5 0.1 tile.10
  11.6 0.0 copy-start
  11.7 0.5 reshape.15
  12.1 0.6 %slice.21.table_ref = bf16[256,128]{1,0:T(8,128)(2,1)} slice(bf16[256,383]{1,0:T(8,128)(2,1)S(1)} %reshape.15), slice={[0:256], [0:128]} | slice | bytes 131072 | tf_op jit(solution)/shard_map/slice | solution.py:18
  12.8 0.0 copy-done.1
  12.8 1.2 %reshape_squeeze.11.values_ref = bf16[16,2,64,64]{3,2,1,0:T(8,128)(2,1)} reshape(bf16[1,16,2,4096]{3,2,1,0:T(2,128)(2,1)S(1)} %copy-done.1) | data formatting | bytes 524288 | tf_op jit(solution)/shard_map/reshape;squeeze | solution.py:196
  14.0 0.0 collective-permute-done
  14.0 0.0 copy-done
  14.0 0.9 %maximum_bitcast_fusion.fields_ref = bf16[2,32,8,640]{3,2,1,0:T(8,128)(2,1)} fusion(bf16[2,256,512]{2,1,0:T(8,128)(2,1)S(1)} %copy-done, bf16[2,256,128]{2,1,0:T(8,128)(2,1)S(1)} %collective-permute-done), kind=kLoop, calls=%fused_computation | loop fusion | flops 1310720 | bytes 1310720 | tf_op jit(solution)/shard_map/reshape | solution.py:195
  14.9 10.1 %shard_map.73 = bf16[32,2,8,512]{3,2,1,0:T(8,128)(2,1)} custom-call(s32[32]{0:T(128)} %reshape_squeeze.9.pairs_ref, s32[32]{0:T(128)} %reshape_squeeze.10.lights_ref, s32[32]{0:T(128)} %bitcast.11, s32[1]{0:T(128)S(6)} %copy.13.live_ref, bf16[2,32,8,640]{3,2,1,0:T(8,128)(2,1)} %maximum_bitcast_fusion.fields_ref, bf16[256,128]{1,0:T(8,128)(2,1)} %slice.21.table_ref, ...), custom_call_target="tpu_custom_call" | custom-call | tf_op jit(solution)/shard_map/pallas_call | solution.py:199
  25.0 24.0 %shard_map.74 = f32[1,2,8,512]{3,2,1,0:T(8,128)} custom-call(bf16[32,1,2,8,512]{4,3,2,1,0:T(8,128)(2,1)} %bitcast.7), custom_call_target="tpu_custom_call" | custom-call | tf_op jit(solution)/shard_map/pallas_call | solution.py:216
  49.1 1.4 %copy.14 = f32[2,8,512]{2,1,0:T(8,128)} copy(f32[2,8,512]{2,1,0:T(8,128)} %bitcast.9) | data formatting | bytes 65536
  (2 shorter events, 0.0 us)
Async XLA Ops:
  0.0 12.8 %copy-start.1 = (bf16[1,16,2,4096]{3,2,1,0:T(2,128)(2,1)S(1)}, bf16[1,16,2,4096]{3,2,1,0:T(2,128)(2,1)}, u32[]{:S(2)}) copy-start(bf16[1,16,2,4096]{3,2,1,0:T(2,128)(2,1)} %param.12) | copy-start | bytes 786436
  1.0 13.0 %collective-permute-start = (bf16[2,256,128]{2,1,0:T(8,128)(2,1)S(1)}, bf16[2,256,128]{2,1,0:T(8,128)(2,1)S(1)}, u32[]{:S(2)}, u32[]{:S(2)}) collective-permute-start(bf16[2,256,128]{2,1,0:T(8,128)(2,1)S(1)} %slice.15), channel_id=1, source_target_pairs={{0,32},{32,64},{64,96},{96,128},{128,160},{160,192},{192,224},{1,3... | collective-permute-start | bytes 393224 | tf_op jit(solution)/shard_map/ppermute | solution.py:189
  11.6 2.3 %copy-start = (bf16[2,256,512]{2,1,0:T(8,128)(2,1)S(1)}, bf16[2,256,512]{2,1,0:T(8,128)(2,1)}, u32[]{:S(2)}) copy-start(bf16[2,256,512]{2,1,0:T(8,128)(2,1)} %param.7) | copy-start | bytes 1572868

commit v6 on v3

v6 whole, which is shorter than its diff:
```python
import functools

import jax
import jax.numpy as jnp
from jax import lax
from jax.sharding import PartitionSpec as P
from jax.experimental import pallas as pl
from jax.experimental.pallas import tpu as pltpu

MB = 8


def toeplitz_table(tap_values):
    tap_count = tap_values.shape[0]
    rows = 2 * tap_count
    period = rows + tap_count
    zeros = jnp.zeros((rows,), tap_values.dtype)
    base = jnp.concatenate([tap_values[tap_count - 1:], zeros, tap_values[: tap_count - 1]])
    tiled = jnp.tile(base, rows)[: rows * (period - 1)].reshape(rows, period - 1)
    return tiled[:, :tap_count]


def fused_kernel(
    slot_count, entries,
    ints_ref, halo_ref, fields_ref, table_ref, values_ref, out_ref,
    partials_ref, send_ref, recv_ref, send_sems, recv_sems,
):
    block_size = fields_ref.shape[2]
    length = fields_ref.shape[3]
    tap_count = halo_ref.shape[3]
    width = length + tap_count
    square = block_size * block_size
    pair_count = send_ref.shape[0]
    owned = send_ref.shape[1]
    light_base = 2 * slot_count
    pick_base = light_base + entries * slot_count
    zero_row = slot_count * entries
    me = lax.axis_index("pair")
    row = lax.axis_index("tm")
    mesh_ids = pl.DeviceIdType.MESH
    barrier = pltpu.get_barrier_semaphore()

    def greet(step, carry):
        peer = lax.rem(me + step, pair_count)
        pl.semaphore_signal(barrier, inc=1, device_id=(row, peer), device_id_type=mesh_ids)
        return carry

    lax.fori_loop(1, pair_count, greet, 0)

    partials_ref[zero_row] = jnp.zeros(partials_ref.shape[1:], partials_ref.dtype)
    table = table_ref[...]

    def window(part, block):
        return jnp.concatenate([halo_ref[part, block], fields_ref[part, block]], 1).astype(jnp.float32)

    def body(slot_index, carry):
        left = ints_ref[2 * slot_index]
        right = ints_ref[2 * slot_index + 1]
        left_real = window(0, left)[:, None]
        left_imag = window(1, left)[:, None]
        right_real = window(0, right)[None]
        right_imag = window(1, right)[None]
        real_part = (left_real * right_real + left_imag * right_imag).reshape(square, width)
        imag_part = (left_imag * right_real - left_real * right_imag).reshape(square, width)
        intensity = jnp.concatenate([real_part, imag_part], 0).astype(jnp.bfloat16)
        pieces = []
        for piece in range(length // tap_count):
            span = intensity[:, piece * tap_count:piece * tap_count + 2 * tap_count]
            pieces.append(jnp.dot(span, table, preferred_element_type=jnp.float32))
        response = jnp.concatenate(pieces, 1).astype(jnp.bfloat16)
        for entry_index in range(entries):
            matrix = values_ref[slot_index, entry_index]
            mixed_real = jnp.dot(matrix, response[:square], preferred_element_type=jnp.float32).reshape(
                block_size, block_size, length
            )
            mixed_imag = jnp.dot(matrix, response[square:], preferred_element_type=jnp.float32).reshape(
                block_size, block_size, length
            )
            light = ints_ref[light_base + entries * slot_index + entry_index]
            light_real = fields_ref[0, light].astype(jnp.float32)[None]
            light_imag = fields_ref[1, light].astype(jnp.float32)[None]
            out_real = jnp.sum(light_real * mixed_real - light_imag * mixed_imag, axis=1)
            out_imag = jnp.sum(light_real * mixed_imag + light_imag * mixed_real, axis=1)
            partials_ref[entries * slot_index + entry_index, 0] = out_real
            partials_ref[entries * slot_index + entry_index, 1] = out_imag
        return carry

    lax.fori_loop(0, slot_count, body, 0)

    def block_sum(peer, part):
        block = peer * owned + part
        first = ints_ref[pick_base + 2 * block]
        second = ints_ref[pick_base + 2 * block + 1]
        return partials_ref[first] + partials_ref[second]

    pl.semaphore_wait(barrier, pair_count - 1)

    def outgoing(peer):
        return pltpu.make_async_remote_copy(
            src_ref=send_ref.at[peer],
            dst_ref=recv_ref.at[me],
            send_sem=send_sems.at[peer],
            recv_sem=recv_sems.at[me],
            device_id=(row, peer),
            device_id_type=mesh_ids,
        )

    def send(step, carry):
        peer = lax.rem(me + step, pair_count)
        for part in range(owned):
            send_ref[peer, part] = block_sum(peer, part).astype(send_ref.dtype)
        outgoing(peer).start()
        return carry

    lax.fori_loop(1, pair_count, send, 0)

    def gather(step, total):
        peer = lax.rem(me + pair_count - step, pair_count)
        incoming = pltpu.make_async_remote_copy(
            src_ref=send_ref.at[peer],
            dst_ref=recv_ref.at[peer],
            send_sem=send_sems.at[peer],
            recv_sem=recv_sems.at[peer],
            device_id=(row, peer),
            device_id_type=mesh_ids,
        )
        incoming.wait_recv()
        return total + recv_ref[peer].astype(jnp.float32)

    own = jnp.stack([block_sum(me, part) for part in range(owned)])
    total = lax.fori_loop(1, pair_count, gather, own)

    def finish(step, carry):
        outgoing(lax.rem(me + step, pair_count)).wait_send()
        return carry

    lax.fori_loop(1, pair_count, finish, 0)
    out_ref[...] = total


def local(
    mode_fields, raman_taps, pair_blocks, light_blocks, target_blocks, raman_values, live_slots
):
    toeplitz = toeplitz_table(raman_taps)
    tap_count = toeplitz.shape[1]
    block_size = MB
    tm_count = lax.axis_size("tm")
    pair_count = lax.axis_size("pair")
    slot_count = pair_blocks.shape[1]
    entries = light_blocks.shape[2]
    mode_count = mode_fields.shape[1]
    length = mode_fields.shape[2]
    blocks = mode_count // block_size
    owned = blocks // pair_count
    rows = slot_count * entries
    halo = lax.ppermute(
        mode_fields[:, :, -tap_count:], "tm", [(k, k + 1) for k in range(tm_count - 1)]
    )
    halo = halo.reshape(2, blocks, block_size, tap_count)
    fields = mode_fields.reshape(2, blocks, block_size, length)
    square = block_size * block_size
    values = raman_values[0].reshape(slot_count, entries, square, square)
    row_index = jnp.arange(rows, dtype=jnp.int32)
    live_rows = row_index // entries < live_slots[0]
    feeds = (target_blocks.reshape(1, rows) == jnp.arange(blocks, dtype=jnp.int32)[:, None]) & live_rows[None]
    count = jnp.sum(feeds.astype(jnp.int32), axis=1)
    first = jnp.where(count >= 1, jnp.argmax(feeds, axis=1).astype(jnp.int32), rows)
    last = rows - 1 - jnp.argmax(feeds[:, ::-1], axis=1).astype(jnp.int32)
    second = jnp.where(count >= 2, last, rows)
    ints = jnp.concatenate(
        [pair_blocks.reshape(-1), light_blocks.reshape(-1), jnp.stack([first, second], 1).reshape(-1)]
    )
    smem = pl.BlockSpec(memory_space=pltpu.SMEM)
    vmem = pl.BlockSpec(memory_space=pltpu.VMEM)
    exchange_shape = (pair_count, owned, 2, block_size, length)
    shared = pl.pallas_call(
        functools.partial(fused_kernel, slot_count, entries),
        out_shape=jax.ShapeDtypeStruct((owned, 2, block_size, length), jnp.float32),
        in_specs=[smem, vmem, vmem, vmem, vmem],
        out_specs=vmem,
        scratch_shapes=[
            pltpu.VMEM((rows + 1, 2, block_size, length), jnp.float32),
            pltpu.VMEM(exchange_shape, jnp.bfloat16),
            pltpu.VMEM(exchange_shape, jnp.bfloat16),
            pltpu.SemaphoreType.DMA((pair_count,)),
            pltpu.SemaphoreType.DMA((pair_count,)),
        ],
        compiler_params=pltpu.CompilerParams(collective_id=0, has_side_effects=True),
    )(ints, halo, fields, toeplitz, values)
    result = jnp.transpose(shared, (1, 0, 2, 3)).reshape(2, owned * block_size, length)
    return result


def solution(mesh):
    return jax.shard_map(
        local,
        mesh=mesh,
        in_specs=(
            P(None, None, "tm"),
            P(),
            P("pair", None, None),
            P("pair", None, None),
            P("pair", None),
            P("pair", None, None, None),
            P("pair"),
        ),
        out_specs=P(None, "pair", "tm"),
        check_vma=False,
    )
```

time: 254 us -> 46.9 us (0.18)
  the two profiles are of different devices: /device:TPU:2 before, /device:TPU:11 now
where the time goes in v6:
time: 46.9 us; the launch traced here: 46.7 us
  Pallas kernels  31 us (66%)
  local copies, waits for them, and re-layouts  8.5 us (18%)
  starting transfers between devices  3.68 us (8%)
  other arithmetic  2.77 us (6%)
  between operations  0.74 us (2%)
    pallas_call x1, Pallas kernels, local(): pl.pallas_call(functools.partial(fused_kernel, slot_count, entries), out_...  31 us
    unnamed x15, local copies, waits for them, and re-layouts  4.09 us
    ppermute x1, starting transfers between devices, local(): lax.ppermute(mode_fields[:, :, -tap_count:], 'tm', [(k, k + 1) for k in r...  3.68 us
    another operation x2, other arithmetic, local(): jnp.argmax(feeds, axis=1).astype(jnp.int32)  1.27 us
    another operation x1, local copies, waits for them, and re-layouts, local(): values = raman_values[0].reshape(slot_count, entries, square, square)  1.16 us
  transfers between devices with their start and end apart: 1, of which 0 were waited for; matrix products, arithmetic and copies ran while one was open for 14% of the time, Pallas kernels for 0%

profile of v6, /device:TPU:11, one launch (start us, length us, event | category | flops | bytes accessed | tf_op | source)
XLA Modules:
  0.0 46.7 jit_solution(16378703342692206312)
XLA Ops:
  0.0 0.9 %slice.15 = bf16[2,256,128]{2,1,0:T(8,128)(2,1)S(1)} slice(bf16[2,256,512]{2,1,0:T(8,128)(2,1)} %param.7), slice={[0:2], [0:256], [384:512]} | slice | bytes 262144 | tf_op jit(solution)/shard_map/slice | solution.py:157
  0.9 3.7 %collective-permute-start = (bf16[2,256,128]{2,1,0:T(8,128)(2,1)S(1)}, bf16[2,256,128]{2,1,0:T(8,128)(2,1)S(1)}, u32[]{:S(2)}, u32[]{:S(2)}) collective-permute-start(bf16[2,256,128]{2,1,0:T(8,128)(2,1)S(1)} %slice.15), channel_id=1, source_target_pairs={{0,32},{32,64},{64,96},{96,128},{128,160},{160,192},{192,224},{1,3... | collective-permute-start | bytes 393224 | tf_op jit(solution)/shard_map/ppermute | solution.py:156
  5.3 0.0 copy-start.2
  5.3 0.6 %copy-done.2 = s32[32,1]{0,1:T(1,128)S(1)} copy-done((s32[32,1]{0,1:T(1,128)S(1)}, s32[32,1]{0,1:T(1,128)}, u32[]{:S(2)}) %copy-start.2) | copy-done | bytes 152
  5.9 0.1 convert_reduce_fusion
  6.0 0.6 %iota_reduce_fusion.1 = (pred[32]{0:T(512)(128)(4,1)}, s32[32]{0:T(128)S(1)}) fusion(pred[32]{0:T(512)(128)(4,1)S(1)} %fusion.1, s32[32]{0:T(128)S(1)} %bitcast.17), kind=kLoop, calls=%fused_computation.1 | loop fusion | flops 8992 | bytes 320 | tf_op jit(solution)/shard_map/local/reduce | solution.py:167
  6.7 0.0 copy-start.5
  6.7 0.6 %copy-done.5 = bf16[128]{0:T(256)(128)(2,1)S(1)} copy-done((bf16[128]{0:T(256)(128)(2,1)S(1)}, bf16[128]{0:T(256)(128)(2,1)}, u32[]{:S(2)}) %copy-start.5) | copy-done | bytes 280
  7.3 0.7 %slice.16 = bf16[1]{0:T(256)(128)(2,1)} slice(bf16[128]{0:T(256)(128)(2,1)S(1)} %copy-done.5), slice={[127:128]} | slice | bytes 4 | tf_op jit(solution)/shard_map/slice | solution.py:18
  8.0 0.1 rev.3
  8.1 0.6 %iota_reduce_fusion = (pred[32]{0:T(512)(128)(4,1)}, s32[32]{0:T(128)S(1)}) fusion(pred[32,32]{1,0:T(8,128)(4,1)S(1)} %rev.3), kind=kLoop, calls=%fused_computation | loop fusion | flops 6944 | bytes 1184 | tf_op jit(solution)/shard_map/local/reduce | solution.py:167
  8.7 0.0 copy-start.3
  8.8 0.8 %pad_maximum_fusion = bf16[384]{0:T(512)(128)(2,1)S(1)} fusion(bf16[127]{0:T(256)(128)(2,1)S(1)} %bitcast.19, bf16[256]{0:T(256)(128)(2,1)S(1)} %broadcast_in_dim.11, bf16[1]{0:T(256)(128)(2,1)} %slice.16), kind=kLoop, calls=%fused_computation.9 | loop fusion | flops 2304 | bytes 1536 | tf_op jit(solution)/shard_map/concatenate | solution.py:18
  9.5 0.0 copy-done.3
  9.5 0.1 copy.14
  9.6 0.0 copy-start.4
  9.6 0.1 reshape.35
  9.7 0.6 %copy-done.4 = s32[1,16,2]{1,2,0:T(2,128)S(1)} copy-done((s32[1,16,2]{1,2,0:T(2,128)S(1)}, s32[1,16,2]{1,2,0:T(2,128)}, u32[]{:S(2)}) %copy-start.4) | copy-done | bytes 152
  10.3 0.1 copy.15
  10.4 0.1 reshape.36
  10.5 0.1 copy.16
  10.6 0.1 reshape.37
  10.7 0.1 tile.10
  10.8 0.0 copy-start
  10.8 0.5 %reshape.40 = bf16[256,383]{1,0:T(8,128)(2,1)S(1)} reshape(bf16[98048]{0:T(1024)(128)(2,1)S(1)} %bitcast.13) | data formatting | bytes 392192 | tf_op jit(solution)/shard_map/reshape | solution.py:19
  11.3 0.6 %slice.21.table_ref = bf16[256,128]{1,0:T(8,128)(2,1)} slice(bf16[256,383]{1,0:T(8,128)(2,1)S(1)} %reshape.40), slice={[0:256], [0:128]} | slice | bytes 131072 | tf_op jit(solution)/shard_map/slice | solution.py:20
  11.9 0.0 copy-done
  11.9 1.2 %reshape_squeeze.3.values_ref = bf16[16,2,64,64]{3,2,1,0:T(8,128)(2,1)} reshape(bf16[1,16,2,4096]{3,2,1,0:T(2,128)(2,1)S(1)} %copy-done) | data formatting | bytes 524288 | tf_op jit(solution)/shard_map/reshape;squeeze | solution.py:162
  13.1 0.6 %pad_add_fusion.1.ints_ref = s32[128]{0:T(128)} fusion(s32[64]{0:T(128)S(1)} %reshape.37, s32[32]{0:T(128)S(1)} %reshape.36, s32[32]{0:T(128)S(1)} %reshape.35), kind=kLoop, calls=%fused_computation.16 | loop fusion | flops 256 | bytes 1024 | tf_op jit(solution)/shard_map/concatenate | solution.py:170
  13.7 0.0 collective-permute-done
  13.7 0.0 copy-start.1
  13.7 0.7 %copy-done.1 = bf16[2,256,128]{2,1,0:T(8,128)(2,1)} copy-done((bf16[2,256,128]{2,1,0:T(8,128)(2,1)}, bf16[2,256,128]{2,1,0:T(8,128)(2,1)S(1)}, u32[]{:S(2)}) %copy-start.1) | copy-done | bytes 131096
  14.3 31.0 %shard_map.73 = f32[1,2,8,512]{3,2,1,0:T(8,128)} custom-call(s32[128]{0:T(128)} %pad_add_fusion.1.ints_ref, bf16[2,32,8,128]{3,2,1,0:T(8,128)(2,1)} %bitcast.14, bf16[2,32,8,512]{3,2,1,0:T(8,128)(2,1)} %bitcast.12, bf16[256,128]{1,0:T(8,128)(2,1)} %slice.21.table_ref, bf16[16,2,64,64]{3,2,1,0:T(8,128)(2,1)} %reshape_squeeze.3.values_ref), custom_call_target="tpu_custom_call" | custom-call | tf_op jit(solution)/shard_map/pallas_call | solution.py:176
  45.3 1.4 %copy.19 = f32[2,8,512]{2,1,0:T(8,128)} copy(f32[2,8,512]{2,1,0:T(8,128)} %bitcast.15) | data formatting | bytes 65536
  (6 shorter events, 0.1 us)
Async XLA Ops:
  0.9 12.7 %collective-permute-start = (bf16[2,256,128]{2,1,0:T(8,128)(2,1)S(1)}, bf16[2,256,128]{2,1,0:T(8,128)(2,1)S(1)}, u32[]{:S(2)}, u32[]{:S(2)}) collective-permute-start(bf16[2,256,128]{2,1,0:T(8,128)(2,1)S(1)} %slice.15), channel_id=1, source_target_pairs={{0,32},{32,64},{64,96},{96,128},{128,160},{160,192},{192,224},{1,3... | collective-permute-start | bytes 393224 | tf_op jit(solution)/shard_map/ppermute | solution.py:156
  5.3 0.7 %copy-start.2 = (s32[32,1]{0,1:T(1,128)S(1)}, s32[32,1]{0,1:T(1,128)}, u32[]{:S(2)}) copy-start(s32[32,1]{0,1:T(1,128)} %param.11) | copy-start | bytes 388
  6.7 0.7 %copy-start.5 = (bf16[128]{0:T(256)(128)(2,1)S(1)}, bf16[128]{0:T(256)(128)(2,1)}, u32[]{:S(2)}) copy-start(bf16[128]{0:T(256)(128)(2,1)} %param.8) | copy-start | bytes 772
  8.7 0.8 %copy-start.3 = (s32[1,16,2]{1,2,0:T(2,128)S(1)}, s32[1,16,2]{1,2,0:T(2,128)}, u32[]{:S(2)}) copy-start(s32[1,16,2]{1,2,0:T(2,128)} %param.9) | copy-start | bytes 388
  9.6 0.7 %copy-start.4 = (s32[1,16,2]{1,2,0:T(2,128)S(1)}, s32[1,16,2]{1,2,0:T(2,128)}, u32[]{:S(2)}) copy-start(s32[1,16,2]{1,2,0:T(2,128)} %param.10) | copy-start | bytes 388
  10.8 1.1 %copy-start = (bf16[1,16,2,4096]{3,2,1,0:T(2,128)(2,1)S(1)}, bf16[1,16,2,4096]{3,2,1,0:T(2,128)(2,1)}, u32[]{:S(2)}) copy-start(bf16[1,16,2,4096]{3,2,1,0:T(2,128)(2,1)} %param.12) | copy-start | bytes 786436
  13.7 0.7 %copy-start.1 = (bf16[2,256,128]{2,1,0:T(8,128)(2,1)}, bf16[2,256,128]{2,1,0:T(8,128)(2,1)S(1)}, u32[]{:S(2)}) copy-start(bf16[2,256,128]{2,1,0:T(8,128)(2,1)S(1)} %collective-permute-done) | copy-start | bytes 393220

commit v7 on v6

--- a/solution.py
+++ b/solution.py
@@ -8,6 +8,7 @@
 from jax.experimental.pallas import tpu as pltpu
 
 MB = 8
+Y_IN_PAIR = 4
 
 
 def toeplitz_table(tap_values):
@@ -23,15 +24,15 @@
 def fused_kernel(
     slot_count, entries,
     ints_ref, halo_ref, fields_ref, table_ref, values_ref, out_ref,
-    partials_ref, send_ref, recv_ref, send_sems, recv_sems,
+    partials_ref, send_ref, recv_ref, stage_ref, final_ref,
+    send_sems, recv_sems, stage_send_sems, stage_recv_sems,
 ):
     block_size = fields_ref.shape[2]
     length = fields_ref.shape[3]
     tap_count = halo_ref.shape[3]
     width = length + tap_count
     square = block_size * block_size
-    pair_count = send_ref.shape[0]
-    owned = send_ref.shape[1]
+    owned = send_ref.shape[2]
     light_base = 2 * slot_count
     pick_base = light_base + entries * slot_count
     zero_row = slot_count * entries
@@ -40,12 +41,21 @@
     mesh_ids = pl.DeviceIdType.MESH
     barrier = pltpu.get_barrier_semaphore()
 
-    def greet(step, carry):
-        peer = lax.rem(me + step, pair_count)
+    y_count = send_ref.shape[0]
+    z_count = stage_ref.shape[0]
+
+    def greet_y(step, carry):
+        peer = (me // y_count) * y_count + lax.rem(lax.rem(me, y_count) + step, y_count)
         pl.semaphore_signal(barrier, inc=1, device_id=(row, peer), device_id_type=mesh_ids)
         return carry
 
-    lax.fori_loop(1, pair_count, greet, 0)
+    def greet_z(step, carry):
+        peer = lax.rem(me // y_count + step, z_count) * y_count + lax.rem(me, y_count)
+        pl.semaphore_signal(barrier, inc=1, device_id=(row, peer), device_id_type=mesh_ids)
+        return carry
+
+    lax.fori_loop(1, y_count, greet_y, 0)
+    lax.fori_loop(1, z_count, greet_z, 0)
 
     partials_ref[zero_row] = jnp.zeros(partials_ref.shape[1:], partials_ref.dtype)
     table = table_ref[...]
@@ -93,48 +103,92 @@
         second = ints_ref[pick_base + 2 * block + 1]
         return partials_ref[first] + partials_ref[second]
 
-    pl.semaphore_wait(barrier, pair_count - 1)
-
-    def outgoing(peer):
+    group = send_ref.shape[0]
+    rings = stage_ref.shape[0]
+    my_y = lax.rem(me, group)
+    my_z = me // group
+    pl.semaphore_wait(barrier, group - 1 + rings - 1)
+
+    def outgoing_y(peer_y):
         return pltpu.make_async_remote_copy(
-            src_ref=send_ref.at[peer],
-            dst_ref=recv_ref.at[me],
-            send_sem=send_sems.at[peer],
-            recv_sem=recv_sems.at[me],
-            device_id=(row, peer),
-            device_id_type=mesh_ids,
-        )
-
-    def send(step, carry):
-        peer = lax.rem(me + step, pair_count)
+            src_ref=send_ref.at[peer_y],
+            dst_ref=recv_ref.at[my_y],
+            send_sem=send_sems.at[peer_y],
+            recv_sem=recv_sems.at[my_y],
+            device_id=(row, my_z * group + peer_y),
+            device_id_type=mesh_ids,
+        )
+
+    def send_y(step, carry):
+        peer_y = lax.rem(my_y + step, group)
+        for ring in range(rings):
+            for part in range(owned):
+                send_ref[peer_y, ring, part] = block_sum(ring * group + peer_y, part).astype(send_ref.dtype)
+        outgoing_y(peer_y).start()
+        return carry
+
+    lax.fori_loop(1, group, send_y, 0)
+    for ring in range(rings):
         for part in range(owned):
-            send_ref[peer, part] = block_sum(peer, part).astype(send_ref.dtype)
-        outgoing(peer).start()
-        return carry
-
-    lax.fori_loop(1, pair_count, send, 0)
-
-    def gather(step, total):
-        peer = lax.rem(me + pair_count - step, pair_count)
+            stage_ref[ring, part] = block_sum(ring * group + my_y, part)
+
+    def gather_y(step, carry):
+        peer_y = lax.rem(my_y + group - step, group)
         incoming = pltpu.make_async_remote_copy(
-            src_ref=send_ref.at[peer],
-            dst_ref=recv_ref.at[peer],
-            send_sem=send_sems.at[peer],
-            recv_sem=recv_sems.at[peer],
-            device_id=(row, peer),
+            src_ref=send_ref.at[peer_y],
+            dst_ref=recv_ref.at[peer_y],
+            send_sem=send_sems.at[peer_y],
+            recv_sem=recv_sems.at[peer_y],
+            device_id=(row, my_z * group + peer_y),
             device_id_type=mesh_ids,
         )
         incoming.wait_recv()
-        return total + recv_ref[peer].astype(jnp.float32)
-
-    own = jnp.stack([block_sum(me, part) for part in range(owned)])
-    total = lax.fori_loop(1, pair_count, gather, own)
-
-    def finish(step, carry):
-        outgoing(lax.rem(me + step, pair_count)).wait_send()
-        return carry
-
-    lax.fori_loop(1, pair_count, finish, 0)
+        stage_ref[...] += recv_ref[peer_y].astype(jnp.float32)
+        return carry
+
+    lax.fori_loop(1, group, gather_y, 0)
+
+    def outgoing_z(peer_z):
+        return pltpu.make_async_remote_copy(
+            src_ref=stage_ref.at[peer_z],
+            dst_ref=final_ref.at[my_z],
+            send_sem=stage_send_sems.at[peer_z],
+            recv_sem=stage_recv_sems.at[my_z],
+            device_id=(row, peer_z * group + my_y),
+            device_id_type=mesh_ids,
+        )
+
+    def send_z(step, carry):
+        outgoing_z(lax.rem(my_z + step, rings)).start()
+        return carry
+
+    lax.fori_loop(1, rings, send_z, 0)
+
+    def gather_z(step, total):
+        peer_z = lax.rem(my_z + rings - step, rings)
+        incoming = pltpu.make_async_remote_copy(
+            src_ref=stage_ref.at[peer_z],
+            dst_ref=final_ref.at[peer_z],
+            send_sem=stage_send_sems.at[peer_z],
+            recv_sem=stage_recv_sems.at[peer_z],
+            device_id=(row, peer_z * group + my_y),
+            device_id_type=mesh_ids,
+        )
+        incoming.wait_recv()
+        return total + final_ref[peer_z]
+
+    total = lax.fori_loop(1, rings, gather_z, stage_ref[my_z])
+
+    def finish_y(step, carry):
+        outgoing_y(lax.rem(my_y + step, group)).wait_send()
+        return carry
+
+    def finish_z(step, carry):
+        outgoing_z(lax.rem(my_z + step, rings)).wait_send()
+        return carry
+
+    lax.fori_loop(1, group, finish_y, 0)
+    lax.fori_loop(1, rings, finish_z, 0)
     out_ref[...] = total
 
 
@@ -163,16 +217,17 @@
     row_index = jnp.arange(rows, dtype=jnp.int32)
     live_rows = row_index // entries < live_slots[0]
     feeds = (target_blocks.reshape(1, rows) == jnp.arange(blocks, dtype=jnp.int32)[:, None]) & live_rows[None]
-    count = jnp.sum(feeds.astype(jnp.int32), axis=1)
-    first = jnp.where(count >= 1, jnp.argmax(feeds, axis=1).astype(jnp.int32), rows)
-    last = rows - 1 - jnp.argmax(feeds[:, ::-1], axis=1).astype(jnp.int32)
-    second = jnp.where(count >= 2, last, rows)
+    first = jnp.min(jnp.where(feeds, row_index[None], rows), axis=1)
+    last = jnp.max(jnp.where(feeds, row_index[None], -1), axis=1)
+    second = jnp.where(last > first, last, rows)
     ints = jnp.concatenate(
         [pair_blocks.reshape(-1), light_blocks.reshape(-1), jnp.stack([first, second], 1).reshape(-1)]
     )
     smem = pl.BlockSpec(memory_space=pltpu.SMEM)
     vmem = pl.BlockSpec(memory_space=pltpu.VMEM)
-    exchange_shape = (pair_count, owned, 2, block_size, length)
+    z_count = pair_count // Y_IN_PAIR
+    exchange_shape = (Y_IN_PAIR, z_count, owned, 2, block_size, length)
+    stage_shape = (z_count, owned, 2, block_size, length)
     shared = pl.pallas_call(
         functools.partial(fused_kernel, slot_count, entries),
         out_shape=jax.ShapeDtypeStruct((owned, 2, block_size, length), jnp.float32),
@@ -182,8 +237,12 @@
             pltpu.VMEM((rows + 1, 2, block_size, length), jnp.float32),
             pltpu.VMEM(exchange_shape, jnp.bfloat16),
             pltpu.VMEM(exchange_shape, jnp.bfloat16),
-            pltpu.SemaphoreType.DMA((pair_count,)),
-            pltpu.SemaphoreType.DMA((pair_count,)),
+            pltpu.VMEM(stage_shape, jnp.float32),
+            pltpu.VMEM(stage_shape, jnp.float32),
+            pltpu.SemaphoreType.DMA((Y_IN_PAIR,)),
+            pltpu.SemaphoreType.DMA((Y_IN_PAIR,)),
+            pltpu.SemaphoreType.DMA((z_count,)),
+            pltpu.SemaphoreType.DMA((z_count,)),
         ],
         compiler_params=pltpu.CompilerParams(collective_id=0, has_side_effects=True),
     )(ints, halo, fields, toeplitz, values)

time: 46.9 us -> 46.9 us (level)
  the two profiles are of different devices: /device:TPU:11 before, /device:TPU:1 now
where the time goes in v7:
time: 46.9 us; the launch traced here: 46.7 us
  Pallas kernels  32.2 us (69%)
  local copies, waits for them, and re-layouts  7.77 us (17%)
  starting transfers between devices  4.51 us (10%)
  other arithmetic  1.44 us (3%)
  between operations  0.75 us (2%)
    pallas_call x1, Pallas kernels, local(): pl.pallas_call(functools.partial(fused_kernel, slot_count, entries), out_...  32.2 us
    ppermute x1, starting transfers between devices, local(): lax.ppermute(mode_fields[:, :, -tap_count:], 'tm', [(k, k + 1) for k in r...  4.51 us
    unnamed x15, local copies, waits for them, and re-layouts  3.45 us
    another operation x1, local copies, waits for them, and re-layouts, local(): values = raman_values[0].reshape(slot_count, entries, square, square)  1.16 us
  transfers between devices with their start and end apart: 1, of which 0 were waited for; matrix products, arithmetic and copies ran while one was open for 11% of the time, Pallas kernels for 0%

profile of v7, /device:TPU:1, one launch (start us, length us, event | category | flops | bytes accessed | tf_op | source)
XLA Modules:
  0.0 46.7 jit_solution(14296951583612419385)
XLA Ops:
  0.0 0.9 %slice.15 = bf16[2,256,128]{2,1,0:T(8,128)(2,1)S(1)} slice(bf16[2,256,512]{2,1,0:T(8,128)(2,1)} %param.7), slice={[0:2], [0:256], [384:512]} | slice | bytes 262144 | tf_op jit(solution)/shard_map/slice | solution.py:211
  0.9 0.0 copy-start.4
  0.9 4.5 %collective-permute-start = (bf16[2,256,128]{2,1,0:T(8,128)(2,1)S(1)}, bf16[2,256,128]{2,1,0:T(8,128)(2,1)S(1)}, u32[]{:S(2)}, u32[]{:S(2)}) collective-permute-start(bf16[2,256,128]{2,1,0:T(8,128)(2,1)S(1)} %slice.15), channel_id=1, source_target_pairs={{0,32},{32,64},{64,96},{96,128},{128,160},{160,192},{192,224},{1,3... | collective-permute-start | bytes 393224 | tf_op jit(solution)/shard_map/ppermute | solution.py:210
  6.1 0.0 copy-done.4
  6.1 0.6 %slice.16 = bf16[1]{0:T(256)(128)(2,1)} slice(bf16[128]{0:T(256)(128)(2,1)S(1)} %copy-done.4), slice={[127:128]} | slice | bytes 4 | tf_op jit(solution)/shard_map/slice | solution.py:19
  6.8 0.0 copy-start.5
  6.8 0.7 %copy-done.5 = s32[32,1]{0,1:T(1,128)S(1)} copy-done((s32[32,1]{0,1:T(1,128)S(1)}, s32[32,1]{0,1:T(1,128)}, u32[]{:S(2)}) %copy-start.5) | copy-done | bytes 152
  7.4 0.1 select_reduce_fusion.1
  7.6 0.0 copy-start.2
  7.6 0.7 %pad_maximum_fusion = bf16[384]{0:T(512)(128)(2,1)S(1)} fusion(bf16[127]{0:T(256)(128)(2,1)S(1)} %bitcast.17, bf16[256]{0:T(256)(128)(2,1)S(1)} %broadcast_in_dim.36, bf16[1]{0:T(256)(128)(2,1)} %slice.16), kind=kLoop, calls=%fused_computation.7 | loop fusion | flops 2304 | bytes 1536 | tf_op jit(solution)/shard_map/concatenate | solution.py:19
  8.3 0.0 copy-done.2
  8.3 0.1 copy.14
  8.4 0.0 copy-start.3
  8.4 0.1 reshape.49
  8.5 0.6 %copy-done.3 = s32[1,16,2]{1,2,0:T(2,128)S(1)} copy-done((s32[1,16,2]{1,2,0:T(2,128)S(1)}, s32[1,16,2]{1,2,0:T(2,128)}, u32[]{:S(2)}) %copy-start.3) | copy-done | bytes 152
  9.1 0.1 copy.15
  9.1 0.1 reshape.50
  9.2 0.1 copy.16
  9.3 0.1 reshape.51
  9.5 0.1 tile.10
  9.6 0.0 copy-start
  9.6 0.5 %reshape.54 = bf16[256,383]{1,0:T(8,128)(2,1)S(1)} reshape(bf16[98048]{0:T(1024)(128)(2,1)S(1)} %bitcast.13) | data formatting | bytes 392192 | tf_op jit(solution)/shard_map/reshape | solution.py:20
  10.1 0.6 %slice.21.table_ref = bf16[256,128]{1,0:T(8,128)(2,1)} slice(bf16[256,383]{1,0:T(8,128)(2,1)S(1)} %reshape.54), slice={[0:256], [0:128]} | slice | bytes 131072 | tf_op jit(solution)/shard_map/slice | solution.py:21
  10.7 0.0 copy-done
  10.7 1.2 %reshape_squeeze.3.values_ref = bf16[16,2,64,64]{3,2,1,0:T(8,128)(2,1)} reshape(bf16[1,16,2,4096]{3,2,1,0:T(2,128)(2,1)S(1)} %copy-done) | data formatting | bytes 524288 | tf_op jit(solution)/shard_map/reshape;squeeze | solution.py:216
  11.9 0.6 %pad_add_fusion.1.ints_ref = s32[128]{0:T(128)} fusion(s32[64]{0:T(128)S(1)} %reshape.51, s32[32]{0:T(128)S(1)} %reshape.50, s32[32]{0:T(128)S(1)} %reshape.49), kind=kLoop, calls=%fused_computation.12 | loop fusion | flops 256 | bytes 1024 | tf_op jit(solution)/shard_map/concatenate | solution.py:223
  12.4 0.0 collective-permute-done
  12.4 0.0 copy-start.1
  12.4 0.6 %copy-done.1 = bf16[2,256,128]{2,1,0:T(8,128)(2,1)} copy-done((bf16[2,256,128]{2,1,0:T(8,128)(2,1)}, bf16[2,256,128]{2,1,0:T(8,128)(2,1)S(1)}, u32[]{:S(2)}) %copy-start.1) | copy-done | bytes 131096
  13.1 32.2 %shard_map.73 = f32[1,2,8,512]{3,2,1,0:T(8,128)} custom-call(s32[128]{0:T(128)} %pad_add_fusion.1.ints_ref, bf16[2,32,8,128]{3,2,1,0:T(8,128)(2,1)} %bitcast.14, bf16[2,32,8,512]{3,2,1,0:T(8,128)(2,1)} %bitcast.12, bf16[256,128]{1,0:T(8,128)(2,1)} %slice.21.table_ref, bf16[16,2,64,64]{3,2,1,0:T(8,128)(2,1)} %reshape_squeeze.3.values_ref), custom_call_target="tpu_custom_call" | custom-call | tf_op jit(solution)/shard_map/pallas_call | solution.py:231
  45.3 1.4 %copy.19 = f32[2,8,512]{2,1,0:T(8,128)} copy(f32[2,8,512]{2,1,0:T(8,128)} %bitcast.15) | data formatting | bytes 65536
  (5 shorter events, 0.0 us)
Async XLA Ops:
  0.9 5.2 %copy-start.4 = (bf16[128]{0:T(256)(128)(2,1)S(1)}, bf16[128]{0:T(256)(128)(2,1)}, u32[]{:S(2)}) copy-start(bf16[128]{0:T(256)(128)(2,1)} %param.8) | copy-start | bytes 772
  0.9 11.5 %collective-permute-start = (bf16[2,256,128]{2,1,0:T(8,128)(2,1)S(1)}, bf16[2,256,128]{2,1,0:T(8,128)(2,1)S(1)}, u32[]{:S(2)}, u32[]{:S(2)}) collective-permute-start(bf16[2,256,128]{2,1,0:T(8,128)(2,1)S(1)} %slice.15), channel_id=1, source_target_pairs={{0,32},{32,64},{64,96},{96,128},{128,160},{160,192},{192,224},{1,3... | collective-permute-start | bytes 393224 | tf_op jit(solution)/shard_map/ppermute | solution.py:210
  6.8 0.7 %copy-start.5 = (s32[32,1]{0,1:T(1,128)S(1)}, s32[32,1]{0,1:T(1,128)}, u32[]{:S(2)}) copy-start(s32[32,1]{0,1:T(1,128)} %param.11) | copy-start | bytes 388
  7.6 0.7 %copy-start.2 = (s32[1,16,2]{1,2,0:T(2,128)S(1)}, s32[1,16,2]{1,2,0:T(2,128)}, u32[]{:S(2)}) copy-start(s32[1,16,2]{1,2,0:T(2,128)} %param.9) | copy-start | bytes 388
  8.4 0.7 %copy-start.3 = (s32[1,16,2]{1,2,0:T(2,128)S(1)}, s32[1,16,2]{1,2,0:T(2,128)}, u32[]{:S(2)}) copy-start(s32[1,16,2]{1,2,0:T(2,128)} %param.10) | copy-start | bytes 388
  9.6 1.1 %copy-start = (bf16[1,16,2,4096]{3,2,1,0:T(2,128)(2,1)S(1)}, bf16[1,16,2,4096]{3,2,1,0:T(2,128)(2,1)}, u32[]{:S(2)}) copy-start(bf16[1,16,2,4096]{3,2,1,0:T(2,128)(2,1)} %param.12) | copy-start | bytes 786436
  12.4 0.6 %copy-start.1 = (bf16[2,256,128]{2,1,0:T(8,128)(2,1)}, bf16[2,256,128]{2,1,0:T(8,128)(2,1)S(1)}, u32[]{:S(2)}) copy-start(bf16[2,256,128]{2,1,0:T(8,128)(2,1)S(1)} %collective-permute-done) | copy-start | bytes 393220

commit v8 on v6

--- a/solution.py
+++ b/solution.py
@@ -163,10 +163,9 @@
     row_index = jnp.arange(rows, dtype=jnp.int32)
     live_rows = row_index // entries < live_slots[0]
     feeds = (target_blocks.reshape(1, rows) == jnp.arange(blocks, dtype=jnp.int32)[:, None]) & live_rows[None]
-    count = jnp.sum(feeds.astype(jnp.int32), axis=1)
-    first = jnp.where(count >= 1, jnp.argmax(feeds, axis=1).astype(jnp.int32), rows)
-    last = rows - 1 - jnp.argmax(feeds[:, ::-1], axis=1).astype(jnp.int32)
-    second = jnp.where(count >= 2, last, rows)
+    first = jnp.min(jnp.where(feeds, row_index[None], rows), axis=1)
+    last = jnp.max(jnp.where(feeds, row_index[None], -1), axis=1)
+    second = jnp.where(last > first, last, rows)
     ints = jnp.concatenate(
         [pair_blocks.reshape(-1), light_blocks.reshape(-1), jnp.stack([first, second], 1).reshape(-1)]
     )

time: 46.9 us -> 44.9 us (0.957)
  other arithmetic: 2.77 us -> 1.44 us
  local copies, waits for them, and re-layouts: 8.5 us -> 7.77 us
    another operation x2 -> x0, other arithmetic: 1.27 us -> none  [local(): jnp.argmax(feeds, axis=1).astype(jnp.int32)]
    unnamed x15, local copies, waits for them, and re-layouts: 4.09 us -> 3.45 us
  transfers between devices with their start and end apart: 1 -> 1, of which waited for: 0 -> 0; matrix products, arithmetic and copies ran while one was open for 14% -> 11% of each run, Pallas kernels for 0% -> 0%
where the time goes in v8:
time: 44.9 us; the launch traced here: 44.6 us
  Pallas kernels  31 us (69%)
  local copies, waits for them, and re-layouts  7.77 us (17%)
  starting transfers between devices  3.68 us (8%)
  other arithmetic  1.44 us (3%)
  between operations  0.75 us (2%)
    pallas_call x1, Pallas kernels, local(): pl.pallas_call(functools.partial(fused_kernel, slot_count, entries), out_...  31 us
    ppermute x1, starting transfers between devices, local(): lax.ppermute(mode_fields[:, :, -tap_count:], 'tm', [(k, k + 1) for k in r...  3.68 us
    unnamed x15, local copies, waits for them, and re-layouts  3.45 us
    another operation x1, local copies, waits for them, and re-layouts, local(): values = raman_values[0].reshape(slot_count, entries, square, square)  1.16 us
    slice x1, local copies, waits for them, and re-layouts, local(): mode_fields[:, :, -tap_count:]  0.91 us
  transfers between devices with their start and end apart: 1, of which 0 were waited for; matrix products, arithmetic and copies ran while one was open for 11% of the time, Pallas kernels for 0%

profile of v8, /device:TPU:11, one launch (start us, length us, event | category | flops | bytes accessed | tf_op | source)
XLA Modules:
  0.0 44.6 jit_solution(867948189666661212)
XLA Ops:
  0.0 0.9 %slice.15 = bf16[2,256,128]{2,1,0:T(8,128)(2,1)S(1)} slice(bf16[2,256,512]{2,1,0:T(8,128)(2,1)} %param.7), slice={[0:2], [0:256], [384:512]} | slice | bytes 262144 | tf_op jit(solution)/shard_map/slice | solution.py:157
  0.9 0.0 copy-start.4
  0.9 3.7 %collective-permute-start = (bf16[2,256,128]{2,1,0:T(8,128)(2,1)S(1)}, bf16[2,256,128]{2,1,0:T(8,128)(2,1)S(1)}, u32[]{:S(2)}, u32[]{:S(2)}) collective-permute-start(bf16[2,256,128]{2,1,0:T(8,128)(2,1)S(1)} %slice.15), channel_id=1, source_target_pairs={{0,32},{32,64},{64,96},{96,128},{128,160},{160,192},{192,224},{1,3... | collective-permute-start | bytes 393224 | tf_op jit(solution)/shard_map/ppermute | solution.py:156
  5.3 0.0 copy-done.4
  5.3 0.6 %slice.16 = bf16[1]{0:T(256)(128)(2,1)} slice(bf16[128]{0:T(256)(128)(2,1)S(1)} %copy-done.4), slice={[127:128]} | slice | bytes 4 | tf_op jit(solution)/shard_map/slice | solution.py:18
  5.9 0.0 copy-start.5
  5.9 0.7 %copy-done.5 = s32[32,1]{0,1:T(1,128)S(1)} copy-done((s32[32,1]{0,1:T(1,128)S(1)}, s32[32,1]{0,1:T(1,128)}, u32[]{:S(2)}) %copy-start.5) | copy-done | bytes 152
  6.6 0.1 select_reduce_fusion.1
  6.7 0.0 copy-start.2
  6.8 0.7 %pad_maximum_fusion = bf16[384]{0:T(512)(128)(2,1)S(1)} fusion(bf16[127]{0:T(256)(128)(2,1)S(1)} %bitcast.17, bf16[256]{0:T(256)(128)(2,1)S(1)} %broadcast_in_dim.36, bf16[1]{0:T(256)(128)(2,1)} %slice.16), kind=kLoop, calls=%fused_computation.7 | loop fusion | flops 2304 | bytes 1536 | tf_op jit(solution)/shard_map/concatenate | solution.py:18
  7.5 0.0 copy-done.2
  7.5 0.1 copy.14
  7.6 0.0 copy-start.3
  7.6 0.1 reshape.49
  7.6 0.6 %copy-done.3 = s32[1,16,2]{1,2,0:T(2,128)S(1)} copy-done((s32[1,16,2]{1,2,0:T(2,128)S(1)}, s32[1,16,2]{1,2,0:T(2,128)}, u32[]{:S(2)}) %copy-start.3) | copy-done | bytes 152
  8.2 0.1 copy.15
  8.3 0.1 reshape.50
  8.4 0.1 copy.16
  8.5 0.1 reshape.51
  8.6 0.1 tile.10
  8.7 0.0 copy-start
  8.7 0.5 %reshape.54 = bf16[256,383]{1,0:T(8,128)(2,1)S(1)} reshape(bf16[98048]{0:T(1024)(128)(2,1)S(1)} %bitcast.13) | data formatting | bytes 392192 | tf_op jit(solution)/shard_map/reshape | solution.py:19
  9.2 0.6 %slice.21.table_ref = bf16[256,128]{1,0:T(8,128)(2,1)} slice(bf16[256,383]{1,0:T(8,128)(2,1)S(1)} %reshape.54), slice={[0:256], [0:128]} | slice | bytes 131072 | tf_op jit(solution)/shard_map/slice | solution.py:20
  9.9 0.0 copy-done
  9.9 1.2 %reshape_squeeze.3.values_ref = bf16[16,2,64,64]{3,2,1,0:T(8,128)(2,1)} reshape(bf16[1,16,2,4096]{3,2,1,0:T(2,128)(2,1)S(1)} %copy-done) | data formatting | bytes 524288 | tf_op jit(solution)/shard_map/reshape;squeeze | solution.py:162
  11.0 0.6 %pad_add_fusion.1.ints_ref = s32[128]{0:T(128)} fusion(s32[64]{0:T(128)S(1)} %reshape.51, s32[32]{0:T(128)S(1)} %reshape.50, s32[32]{0:T(128)S(1)} %reshape.49), kind=kLoop, calls=%fused_computation.12 | loop fusion | flops 256 | bytes 1024 | tf_op jit(solution)/shard_map/concatenate | solution.py:169
  11.6 0.0 collective-permute-done
  11.6 0.0 copy-start.1
  11.6 0.6 %copy-done.1 = bf16[2,256,128]{2,1,0:T(8,128)(2,1)} copy-done((bf16[2,256,128]{2,1,0:T(8,128)(2,1)}, bf16[2,256,128]{2,1,0:T(8,128)(2,1)S(1)}, u32[]{:S(2)}) %copy-start.1) | copy-done | bytes 131096
  12.3 31.0 %shard_map.73 = f32[1,2,8,512]{3,2,1,0:T(8,128)} custom-call(s32[128]{0:T(128)} %pad_add_fusion.1.ints_ref, bf16[2,32,8,128]{3,2,1,0:T(8,128)(2,1)} %bitcast.14, bf16[2,32,8,512]{3,2,1,0:T(8,128)(2,1)} %bitcast.12, bf16[256,128]{1,0:T(8,128)(2,1)} %slice.21.table_ref, bf16[16,2,64,64]{3,2,1,0:T(8,128)(2,1)} %reshape_squeeze.3.values_ref), custom_call_target="tpu_custom_call" | custom-call | tf_op jit(solution)/shard_map/pallas_call | solution.py:175
  43.2 1.4 %copy.19 = f32[2,8,512]{2,1,0:T(8,128)} copy(f32[2,8,512]{2,1,0:T(8,128)} %bitcast.15) | data formatting | bytes 65536
  (5 shorter events, 0.0 us)
Async XLA Ops:
  0.9 4.3 %copy-start.4 = (bf16[128]{0:T(256)(128)(2,1)S(1)}, bf16[128]{0:T(256)(128)(2,1)}, u32[]{:S(2)}) copy-start(bf16[128]{0:T(256)(128)(2,1)} %param.8) | copy-start | bytes 772
  0.9 10.7 %collective-permute-start = (bf16[2,256,128]{2,1,0:T(8,128)(2,1)S(1)}, bf16[2,256,128]{2,1,0:T(8,128)(2,1)S(1)}, u32[]{:S(2)}, u32[]{:S(2)}) collective-permute-start(bf16[2,256,128]{2,1,0:T(8,128)(2,1)S(1)} %slice.15), channel_id=1, source_target_pairs={{0,32},{32,64},{64,96},{96,128},{128,160},{160,192},{192,224},{1,3... | collective-permute-start | bytes 393224 | tf_op jit(solution)/shard_map/ppermute | solution.py:156
  5.9 0.7 %copy-start.5 = (s32[32,1]{0,1:T(1,128)S(1)}, s32[32,1]{0,1:T(1,128)}, u32[]{:S(2)}) copy-start(s32[32,1]{0,1:T(1,128)} %param.11) | copy-start | bytes 388
  6.7 0.7 %copy-start.2 = (s32[1,16,2]{1,2,0:T(2,128)S(1)}, s32[1,16,2]{1,2,0:T(2,128)}, u32[]{:S(2)}) copy-start(s32[1,16,2]{1,2,0:T(2,128)} %param.9) | copy-start | bytes 388
  7.6 0.7 %copy-start.3 = (s32[1,16,2]{1,2,0:T(2,128)S(1)}, s32[1,16,2]{1,2,0:T(2,128)}, u32[]{:S(2)}) copy-start(s32[1,16,2]{1,2,0:T(2,128)} %param.10) | copy-start | bytes 388
  8.7 1.1 %copy-start = (bf16[1,16,2,4096]{3,2,1,0:T(2,128)(2,1)S(1)}, bf16[1,16,2,4096]{3,2,1,0:T(2,128)(2,1)}, u32[]{:S(2)}) copy-start(bf16[1,16,2,4096]{3,2,1,0:T(2,128)(2,1)} %param.12) | copy-start | bytes 786436
  11.6 0.6 %copy-start.1 = (bf16[2,256,128]{2,1,0:T(8,128)(2,1)}, bf16[2,256,128]{2,1,0:T(8,128)(2,1)S(1)}, u32[]{:S(2)}) copy-start(bf16[2,256,128]{2,1,0:T(8,128)(2,1)S(1)} %collective-permute-done) | copy-start | bytes 393220

commit v9 on v8

v9 whole, which is shorter than its diff:
```python
import functools

import jax
import jax.numpy as jnp
from jax import lax
from jax.sharding import PartitionSpec as P
from jax.experimental import pallas as pl
from jax.experimental.pallas import tpu as pltpu

MB = 8


def toeplitz_table(tap_values):
    tap_count = tap_values.shape[0]
    rows = 2 * tap_count
    period = rows + tap_count
    zeros = jnp.zeros((rows,), tap_values.dtype)
    base = jnp.concatenate([tap_values[tap_count - 1:], zeros, tap_values[: tap_count - 1]])
    tiled = jnp.tile(base, rows)[: rows * (period - 1)].reshape(rows, period - 1)
    return tiled[:, :tap_count]


def fused_kernel(
    slot_count, entries, halves,
    ints_ref, halo_ref, fields_ref, table_ref, values_ref, out_ref,
    partials_ref, send_ref, recv_ref, send_sems, recv_sems,
):
    block_size = fields_ref.shape[2]
    length = fields_ref.shape[3]
    span_length = length // halves
    tap_count = halo_ref.shape[3]
    width = span_length + tap_count
    square = block_size * block_size
    pair_count = send_ref.shape[1]
    owned = send_ref.shape[2]
    light_base = 2 * slot_count
    pick_base = light_base + entries * slot_count
    zero_row = slot_count * entries
    me = lax.axis_index("pair")
    row = lax.axis_index("tm")
    mesh_ids = pl.DeviceIdType.MESH
    barrier = pltpu.get_barrier_semaphore()

    def greet(step, carry):
        peer = lax.rem(me + step, pair_count)
        pl.semaphore_signal(barrier, inc=1, device_id=(row, peer), device_id_type=mesh_ids)
        return carry

    lax.fori_loop(1, pair_count, greet, 0)

    table = table_ref[...]

    def window(part, block, half):
        if half == 0:
            head = halo_ref[part, block]
        else:
            head = fields_ref[part, block, :, pl.ds(half * span_length - tap_count, tap_count)]
        tail = fields_ref[part, block, :, pl.ds(half * span_length, span_length)]
        return jnp.concatenate([head, tail], 1).astype(jnp.float32)

    def compute(half):
        partials_ref[half, zero_row] = jnp.zeros(partials_ref.shape[2:], partials_ref.dtype)

        def body(slot_index, carry):
            left = ints_ref[2 * slot_index]
            right = ints_ref[2 * slot_index + 1]
            left_real = window(0, left, half)[:, None]
            left_imag = window(1, left, half)[:, None]
            right_real = window(0, right, half)[None]
            right_imag = window(1, right, half)[None]
            real_part = (left_real * right_real + left_imag * right_imag).reshape(square, width)
            imag_part = (left_imag * right_real - left_real * right_imag).reshape(square, width)
            intensity = jnp.concatenate([real_part, imag_part], 0).astype(jnp.bfloat16)
            pieces = []
            for piece in range(span_length // tap_count):
                span = intensity[:, piece * tap_count:piece * tap_count + 2 * tap_count]
                pieces.append(jnp.dot(span, table, preferred_element_type=jnp.float32))
            response = jnp.concatenate(pieces, 1).astype(jnp.bfloat16)
            for entry_index in range(entries):
                matrix = values_ref[slot_index, entry_index]
                mixed_real = jnp.dot(matrix, response[:square], preferred_element_type=jnp.float32).reshape(
                    block_size, block_size, span_length
                )
                mixed_imag = jnp.dot(matrix, response[square:], preferred_element_type=jnp.float32).reshape(
                    block_size, block_size, span_length
                )
                light = ints_ref[light_base + entries * slot_index + entry_index]
                columns = pl.ds(half * span_length, span_length)
                light_real = fields_ref[0, light, :, columns].astype(jnp.float32)[None]
                light_imag = fields_ref[1, light, :, columns].astype(jnp.float32)[None]
                out_real = jnp.sum(light_real * mixed_real - light_imag * mixed_imag, axis=1)
                out_imag = jnp.sum(light_real * mixed_imag + light_imag * mixed_real, axis=1)
                partials_ref[half, entries * slot_index + entry_index, 0] = out_real
                partials_ref[half, entries * slot_index + entry_index, 1] = out_imag
            return carry

        lax.fori_loop(0, slot_count, body, 0)

    def block_sum(half, peer, part):
        block = peer * owned + part
        first = ints_ref[pick_base + 2 * block]
        second = ints_ref[pick_base + 2 * block + 1]
        return partials_ref[half, first] + partials_ref[half, second]

    def copy_of(half, peer, source):
        return pltpu.make_async_remote_copy(
            src_ref=send_ref.at[half, peer],
            dst_ref=recv_ref.at[half, source],
            send_sem=send_sems.at[half, peer],
            recv_sem=recv_sems.at[half, source],
            device_id=(row, peer),
            device_id_type=mesh_ids,
        )

    def send_half(half):
        def send(step, carry):
            peer = lax.rem(me + step, pair_count)
            for part in range(owned):
                send_ref[half, peer, part] = block_sum(half, peer, part).astype(send_ref.dtype)
            copy_of(half, peer, me).start()
            return carry

        lax.fori_loop(1, pair_count, send, 0)

    for half in range(halves):
        compute(half)
        if half == 0:
            pl.semaphore_wait(barrier, pair_count - 1)
        send_half(half)

    for half in range(halves):
        def gather(step, total):
            peer = lax.rem(me + pair_count - step, pair_count)
            copy_of(half, peer, peer).wait_recv()
            return total + recv_ref[half, peer].astype(jnp.float32)

        own = jnp.stack([block_sum(half, me, part) for part in range(owned)])
        total = lax.fori_loop(1, pair_count, gather, own)
        out_ref[:, :, :, pl.ds(half * span_length, span_length)] = total

    for half in range(halves):
        def finish(step, carry):
            copy_of(half, lax.rem(me + step, pair_count), me).wait_send()
            return carry

        lax.fori_loop(1, pair_count, finish, 0)


def local(
    mode_fields, raman_taps, pair_blocks, light_blocks, target_blocks, raman_values, live_slots
):
    toeplitz = toeplitz_table(raman_taps)
    tap_count = toeplitz.shape[1]
    block_size = MB
    tm_count = lax.axis_size("tm")
    pair_count = lax.axis_size("pair")
    slot_count = pair_blocks.shape[1]
    entries = light_blocks.shape[2]
    mode_count = mode_fields.shape[1]
    length = mode_fields.shape[2]
    blocks = mode_count // block_size
    owned = blocks // pair_count
    rows = slot_count * entries
    halo = lax.ppermute(
        mode_fields[:, :, -tap_count:], "tm", [(k, k + 1) for k in range(tm_count - 1)]
    )
    halo = halo.reshape(2, blocks, block_size, tap_count)
    fields = mode_fields.reshape(2, blocks, block_size, length)
    square = block_size * block_size
    values = raman_values[0].reshape(slot_count, entries, square, square)
    row_index = jnp.arange(rows, dtype=jnp.int32)
    live_rows = row_index // entries < live_slots[0]
    feeds = (target_blocks.reshape(1, rows) == jnp.arange(blocks, dtype=jnp.int32)[:, None]) & live_rows[None]
    first = jnp.min(jnp.where(feeds, row_index[None], rows), axis=1)
    last = jnp.max(jnp.where(feeds, row_index[None], -1), axis=1)
    second = jnp.where(last > first, last, rows)
    ints = jnp.concatenate(
        [pair_blocks.reshape(-1), light_blocks.reshape(-1), jnp.stack([first, second], 1).reshape(-1)]
    )
    smem = pl.BlockSpec(memory_space=pltpu.SMEM)
    vmem = pl.BlockSpec(memory_space=pltpu.VMEM)
    halves = 2
    span_length = length // halves
    exchange_shape = (halves, pair_count, owned, 2, block_size, span_length)
    shared = pl.pallas_call(
        functools.partial(fused_kernel, slot_count, entries, halves),
        out_shape=jax.ShapeDtypeStruct((owned, 2, block_size, length), jnp.float32),
        in_specs=[smem, vmem, vmem, vmem, vmem],
        out_specs=vmem,
        scratch_shapes=[
            pltpu.VMEM((halves, rows + 1, 2, block_size, span_length), jnp.float32),
            pltpu.VMEM(exchange_shape, jnp.bfloat16),
            pltpu.VMEM(exchange_shape, jnp.bfloat16),
            pltpu.SemaphoreType.DMA((halves, pair_count)),
            pltpu.SemaphoreType.DMA((halves, pair_count)),
        ],
        compiler_params=pltpu.CompilerParams(collective_id=0, has_side_effects=True),
    )(ints, halo, fields, toeplitz, values)
    result = jnp.transpose(shared, (1, 0, 2, 3)).reshape(2, owned * block_size, length)
    return result


def solution(mesh):
    return jax.shard_map(
        local,
        mesh=mesh,
        in_specs=(
            P(None, None, "tm"),
            P(),
            P("pair", None, None),
            P("pair", None, None),
            P("pair", None),
            P("pair", None, None, None),
            P("pair"),
        ),
        out_specs=P(None, "pair", "tm"),
        check_vma=False,
    )
```

time: 44.9 us -> 46.6 us (1.038)
  the two profiles are of different devices: /device:TPU:11 before, /device:TPU:1 now
where the time goes in v9:
time: 46.6 us; the launch traced here: 46.3 us
  Pallas kernels  31.8 us (68%)
  local copies, waits for them, and re-layouts  7.77 us (17%)
  starting transfers between devices  4.51 us (10%)
  other arithmetic  1.44 us (3%)
  between operations  0.75 us (2%)
    pallas_call x1, Pallas kernels, local(): pl.pallas_call(functools.partial(fused_kernel, slot_count, entries, halve...  31.8 us
    ppermute x1, starting transfers between devices, local(): lax.ppermute(mode_fields[:, :, -tap_count:], 'tm', [(k, k + 1) for k in r...  4.51 us
    unnamed x15, local copies, waits for them, and re-layouts  3.45 us
    another operation x1, local copies, waits for them, and re-layouts, local(): values = raman_values[0].reshape(slot_count, entries, square, square)  1.16 us
  transfers between devices with their start and end apart: 1, of which 0 were waited for; matrix products, arithmetic and copies ran while one was open for 11% of the time, Pallas kernels for 0%

profile of v9, /device:TPU:1, one launch (start us, length us, event | category | flops | bytes accessed | tf_op | source)
XLA Modules:
  0.0 46.3 jit_solution(1867330076672784668)
XLA Ops:
  0.0 0.9 %slice.15 = bf16[2,256,128]{2,1,0:T(8,128)(2,1)S(1)} slice(bf16[2,256,512]{2,1,0:T(8,128)(2,1)} %param.7), slice={[0:2], [0:256], [384:512]} | slice | bytes 262144 | tf_op jit(solution)/shard_map/slice | solution.py:165
  0.9 0.0 copy-start.4
  0.9 4.5 %collective-permute-start = (bf16[2,256,128]{2,1,0:T(8,128)(2,1)S(1)}, bf16[2,256,128]{2,1,0:T(8,128)(2,1)S(1)}, u32[]{:S(2)}, u32[]{:S(2)}) collective-permute-start(bf16[2,256,128]{2,1,0:T(8,128)(2,1)S(1)} %slice.15), channel_id=1, source_target_pairs={{0,32},{32,64},{64,96},{96,128},{128,160},{160,192},{192,224},{1,3... | collective-permute-start | bytes 393224 | tf_op jit(solution)/shard_map/ppermute | solution.py:164
  6.1 0.0 copy-done.4
  6.1 0.6 %slice.16 = bf16[1]{0:T(256)(128)(2,1)} slice(bf16[128]{0:T(256)(128)(2,1)S(1)} %copy-done.4), slice={[127:128]} | slice | bytes 4 | tf_op jit(solution)/shard_map/slice | solution.py:18
  6.8 0.0 copy-start.5
  6.8 0.7 %copy-done.5 = s32[32,1]{0,1:T(1,128)S(1)} copy-done((s32[32,1]{0,1:T(1,128)S(1)}, s32[32,1]{0,1:T(1,128)}, u32[]{:S(2)}) %copy-start.5) | copy-done | bytes 152
  7.4 0.1 select_reduce_fusion.1
  7.6 0.0 copy-start.2
  7.6 0.7 %pad_maximum_fusion = bf16[384]{0:T(512)(128)(2,1)S(1)} fusion(bf16[127]{0:T(256)(128)(2,1)S(1)} %bitcast.17, bf16[256]{0:T(256)(128)(2,1)S(1)} %broadcast_in_dim.36, bf16[1]{0:T(256)(128)(2,1)} %slice.16), kind=kLoop, calls=%fused_computation.7 | loop fusion | flops 2304 | bytes 1536 | tf_op jit(solution)/shard_map/concatenate | solution.py:18
  8.3 0.0 copy-done.2
  8.3 0.1 copy.14
  8.4 0.0 copy-start.3
  8.4 0.1 reshape.49
  8.5 0.6 %copy-done.3 = s32[1,16,2]{1,2,0:T(2,128)S(1)} copy-done((s32[1,16,2]{1,2,0:T(2,128)S(1)}, s32[1,16,2]{1,2,0:T(2,128)}, u32[]{:S(2)}) %copy-start.3) | copy-done | bytes 152
  9.1 0.1 copy.15
  9.1 0.1 reshape.50
  9.2 0.1 copy.16
  9.3 0.1 reshape.51
  9.5 0.1 tile.10
  9.6 0.0 copy-start
  9.6 0.5 %reshape.54 = bf16[256,383]{1,0:T(8,128)(2,1)S(1)} reshape(bf16[98048]{0:T(1024)(128)(2,1)S(1)} %bitcast.13) | data formatting | bytes 392192 | tf_op jit(solution)/shard_map/reshape | solution.py:19
  10.1 0.6 %slice.21.table_ref = bf16[256,128]{1,0:T(8,128)(2,1)} slice(bf16[256,383]{1,0:T(8,128)(2,1)S(1)} %reshape.54), slice={[0:256], [0:128]} | slice | bytes 131072 | tf_op jit(solution)/shard_map/slice | solution.py:20
  10.7 0.0 copy-done
  10.7 1.2 %reshape_squeeze.3.values_ref = bf16[16,2,64,64]{3,2,1,0:T(8,128)(2,1)} reshape(bf16[1,16,2,4096]{3,2,1,0:T(2,128)(2,1)S(1)} %copy-done) | data formatting | bytes 524288 | tf_op jit(solution)/shard_map/reshape;squeeze | solution.py:170
  11.9 0.6 %pad_add_fusion.1.ints_ref = s32[128]{0:T(128)} fusion(s32[64]{0:T(128)S(1)} %reshape.51, s32[32]{0:T(128)S(1)} %reshape.50, s32[32]{0:T(128)S(1)} %reshape.49), kind=kLoop, calls=%fused_computation.12 | loop fusion | flops 256 | bytes 1024 | tf_op jit(solution)/shard_map/concatenate | solution.py:177
  12.4 0.0 collective-permute-done
  12.4 0.0 copy-start.1
  12.4 0.6 %copy-done.1 = bf16[2,256,128]{2,1,0:T(8,128)(2,1)} copy-done((bf16[2,256,128]{2,1,0:T(8,128)(2,1)}, bf16[2,256,128]{2,1,0:T(8,128)(2,1)S(1)}, u32[]{:S(2)}) %copy-start.1) | copy-done | bytes 131096
  13.1 31.8 %shard_map.73 = f32[1,2,8,512]{3,2,1,0:T(8,128)} custom-call(s32[128]{0:T(128)} %pad_add_fusion.1.ints_ref, bf16[2,32,8,128]{3,2,1,0:T(8,128)(2,1)} %bitcast.14, bf16[2,32,8,512]{3,2,1,0:T(8,128)(2,1)} %bitcast.12, bf16[256,128]{1,0:T(8,128)(2,1)} %slice.21.table_ref, bf16[16,2,64,64]{3,2,1,0:T(8,128)(2,1)} %reshape_squeeze.3.values_ref), custom_call_target="tpu_custom_call" | custom-call | tf_op jit(solution)/shard_map/pallas_call | solution.py:185
  44.9 1.4 %copy.19 = f32[2,8,512]{2,1,0:T(8,128)} copy(f32[2,8,512]{2,1,0:T(8,128)} %bitcast.15) | data formatting | bytes 65536
  (5 shorter events, 0.0 us)
Async XLA Ops:
  0.9 5.2 %copy-start.4 = (bf16[128]{0:T(256)(128)(2,1)S(1)}, bf16[128]{0:T(256)(128)(2,1)}, u32[]{:S(2)}) copy-start(bf16[128]{0:T(256)(128)(2,1)} %param.8) | copy-start | bytes 772
  0.9 11.5 %collective-permute-start = (bf16[2,256,128]{2,1,0:T(8,128)(2,1)S(1)}, bf16[2,256,128]{2,1,0:T(8,128)(2,1)S(1)}, u32[]{:S(2)}, u32[]{:S(2)}) collective-permute-start(bf16[2,256,128]{2,1,0:T(8,128)(2,1)S(1)} %slice.15), channel_id=1, source_target_pairs={{0,32},{32,64},{64,96},{96,128},{128,160},{160,192},{192,224},{1,3... | collective-permute-start | bytes 393224 | tf_op jit(solution)/shard_map/ppermute | solution.py:164
  6.8 0.7 %copy-start.5 = (s32[32,1]{0,1:T(1,128)S(1)}, s32[32,1]{0,1:T(1,128)}, u32[]{:S(2)}) copy-start(s32[32,1]{0,1:T(1,128)} %param.11) | copy-start | bytes 388
  7.6 0.7 %copy-start.2 = (s32[1,16,2]{1,2,0:T(2,128)S(1)}, s32[1,16,2]{1,2,0:T(2,128)}, u32[]{:S(2)}) copy-start(s32[1,16,2]{1,2,0:T(2,128)} %param.9) | copy-start | bytes 388
  8.4 0.7 %copy-start.3 = (s32[1,16,2]{1,2,0:T(2,128)S(1)}, s32[1,16,2]{1,2,0:T(2,128)}, u32[]{:S(2)}) copy-start(s32[1,16,2]{1,2,0:T(2,128)} %param.10) | copy-start | bytes 388
  9.6 1.1 %copy-start = (bf16[1,16,2,4096]{3,2,1,0:T(2,128)(2,1)S(1)}, bf16[1,16,2,4096]{3,2,1,0:T(2,128)(2,1)}, u32[]{:S(2)}) copy-start(bf16[1,16,2,4096]{3,2,1,0:T(2,128)(2,1)} %param.12) | copy-start | bytes 786436
  12.4 0.6 %copy-start.1 = (bf16[2,256,128]{2,1,0:T(8,128)(2,1)}, bf16[2,256,128]{2,1,0:T(8,128)(2,1)S(1)}, u32[]{:S(2)}) copy-start(bf16[2,256,128]{2,1,0:T(8,128)(2,1)S(1)} %collective-permute-done) | copy-start | bytes 393220

commit v10 on v8

--- a/solution.py
+++ b/solution.py
@@ -8,16 +8,6 @@
 from jax.experimental.pallas import tpu as pltpu
 
 MB = 8
-
-
-def toeplitz_table(tap_values):
-    tap_count = tap_values.shape[0]
-    rows = 2 * tap_count
-    period = rows + tap_count
-    zeros = jnp.zeros((rows,), tap_values.dtype)
-    base = jnp.concatenate([tap_values[tap_count - 1:], zeros, tap_values[: tap_count - 1]])
-    tiled = jnp.tile(base, rows)[: rows * (period - 1)].reshape(rows, period - 1)
-    return tiled[:, :tap_count]
 
 
 def fused_kernel(
@@ -48,7 +38,12 @@
     lax.fori_loop(1, pair_count, greet, 0)
 
     partials_ref[zero_row] = jnp.zeros(partials_ref.shape[1:], partials_ref.dtype)
-    table = table_ref[...]
+    tap_count = halo_ref.shape[3]
+    taps = table_ref[...].astype(jnp.float32)
+    padded = jnp.concatenate([taps, jnp.zeros((1, 2 * tap_count), jnp.float32)], 1)
+    spread = jnp.broadcast_to(padded, (2 * tap_count, 3 * tap_count))
+    rolled = pltpu.roll(spread, 2 * tap_count + 1, 1, stride=1, stride_axis=0)
+    table = rolled[:, :tap_count].astype(jnp.bfloat16)
 
     def window(part, block):
         return jnp.concatenate([halo_ref[part, block], fields_ref[part, block]], 1).astype(jnp.float32)
@@ -141,8 +136,7 @@
 def local(
     mode_fields, raman_taps, pair_blocks, light_blocks, target_blocks, raman_values, live_slots
 ):
-    toeplitz = toeplitz_table(raman_taps)
-    tap_count = toeplitz.shape[1]
+    tap_count = raman_taps.shape[0]
     block_size = MB
     tm_count = lax.axis_size("tm")
     pair_count = lax.axis_size("pair")
@@ -185,7 +179,7 @@
             pltpu.SemaphoreType.DMA((pair_count,)),
         ],
         compiler_params=pltpu.CompilerParams(collective_id=0, has_side_effects=True),
-    )(ints, halo, fields, toeplitz, values)
+    )(ints, halo, fields, raman_taps.reshape(1, tap_count), values)
     result = jnp.transpose(shared, (1, 0, 2, 3)).reshape(2, owned * block_size, length)
     return result
 

time: 44.9 us -> 43 us (0.958)
  local copies, waits for them, and re-layouts: 7.77 us -> 6.57 us
  other arithmetic: 1.44 us -> 0.73 us
    slice x2 -> x0, local copies, waits for them, and re-layouts: 1.28 us -> none  [the longest x1 0.65 us: toeplitz_table(): tap_values[tap_count - 1:]]
    concatenate x1 -> x0, other arithmetic: 0.71 us -> none  [toeplitz_table(): jnp.concatenate([tap_values[tap_count - 1:], zeros, tap_values[:tap_count...]
    unnamed x15 -> x13, local copies, waits for them, and re-layouts: 3.45 us -> 4.1 us
    reshape x1 -> x0, local copies, waits for them, and re-layouts: 0.47 us -> none  [toeplitz_table(): tiled = jnp.tile(base, rows)[:rows * (period - 1)].reshape(rows, period - 1)]
  transfers between devices with their start and end apart: 1 -> 1, of which waited for: 0 -> 0; matrix products, arithmetic and copies ran while one was open for 11% -> 6% of each run, Pallas kernels for 0% -> 0%
where the time goes in v10:
time: 43 us; the launch traced here: 42.7 us
  Pallas kernels  31 us (72%)
  local copies, waits for them, and re-layouts  6.57 us (15%)
  starting transfers between devices  3.68 us (9%)
  other arithmetic  0.73 us (2%)
  between operations  0.72 us (2%)
    pallas_call x1, Pallas kernels, local(): pl.pallas_call(functools.partial(fused_kernel, slot_count, entries), out_...  31 us
    unnamed x13, local copies, waits for them, and re-layouts  4.1 us
    ppermute x1, starting transfers between devices, local(): lax.ppermute(mode_fields[:, :, -tap_count:], 'tm', [(k, k + 1) for k in r...  3.68 us
    another operation x1, local copies, waits for them, and re-layouts, local(): values = raman_values[0].reshape(slot_count, entries, square, square)  1.15 us
    slice x1, local copies, waits for them, and re-layouts, local(): mode_fields[:, :, -tap_count:]  0.96 us
  transfers between devices with their start and end apart: 1, of which 0 were waited for; matrix products, arithmetic and copies ran while one was open for 6% of the time, Pallas kernels for 0%

profile of v10, /device:TPU:11, one launch (start us, length us, event | category | flops | bytes accessed | tf_op | source)
XLA Modules:
  0.0 42.7 jit_solution(18400777938551328341)
XLA Ops:
  0.0 0.0 copy-start
  0.0 1.0 %slice.3 = bf16[2,256,128]{2,1,0:T(8,128)(2,1)S(1)} slice(bf16[2,256,512]{2,1,0:T(8,128)(2,1)} %param.7), slice={[0:2], [0:256], [384:512]} | slice | bytes 262144 | tf_op jit(solution)/shard_map/slice | solution.py:151
  1.0 3.7 %collective-permute-start = (bf16[2,256,128]{2,1,0:T(8,128)(2,1)S(1)}, bf16[2,256,128]{2,1,0:T(8,128)(2,1)S(1)}, u32[]{:S(2)}, u32[]{:S(2)}) collective-permute-start(bf16[2,256,128]{2,1,0:T(8,128)(2,1)S(1)} %slice.3), channel_id=1, source_target_pairs={{0,32},{32,64},{64,96},{96,128},{128,160},{160,192},{192,224},{1,3... | collective-permute-start | bytes 393224 | tf_op jit(solution)/shard_map/ppermute | solution.py:150
  5.3 0.0 copy-start.4
  5.3 0.6 %copy-done.4 = s32[32,1]{0,1:T(1,128)S(1)} copy-done((s32[32,1]{0,1:T(1,128)S(1)}, s32[32,1]{0,1:T(1,128)}, u32[]{:S(2)}) %copy-start.4) | copy-done | bytes 152
  6.0 0.1 select_reduce_fusion.1
  6.1 0.0 copy-start.2
  6.1 0.7 %copy-done.2 = s32[1,16,2]{1,2,0:T(2,128)S(1)} copy-done((s32[1,16,2]{1,2,0:T(2,128)S(1)}, s32[1,16,2]{1,2,0:T(2,128)}, u32[]{:S(2)}) %copy-start.2) | copy-done | bytes 152
  6.8 0.1 copy.14
  6.9 0.0 copy-start.3
  6.9 0.1 reshape.48
  7.0 0.6 %copy-done.3 = s32[1,16,2]{1,2,0:T(2,128)S(1)} copy-done((s32[1,16,2]{1,2,0:T(2,128)S(1)}, s32[1,16,2]{1,2,0:T(2,128)}, u32[]{:S(2)}) %copy-start.3) | copy-done | bytes 152
  7.5 0.1 copy.15
  7.6 0.1 reshape.49
  7.7 0.1 copy.16
  7.8 0.1 reshape.50
  7.9 0.0 copy-done
  7.9 1.1 %reshape_squeeze.3.values_ref = bf16[16,2,64,64]{3,2,1,0:T(8,128)(2,1)} reshape(bf16[1,16,2,4096]{3,2,1,0:T(2,128)(2,1)S(1)} %copy-done) | data formatting | bytes 524288 | tf_op jit(solution)/shard_map/reshape;squeeze | solution.py:156
  9.1 0.6 %pad_add_fusion.1.ints_ref = s32[128]{0:T(128)} fusion(s32[64]{0:T(128)S(1)} %reshape.50, s32[32]{0:T(128)S(1)} %reshape.49, s32[32]{0:T(128)S(1)} %reshape.48), kind=kLoop, calls=%fused_computation.11 | loop fusion | flops 256 | bytes 1024 | tf_op jit(solution)/shard_map/concatenate | solution.py:163
  9.7 0.0 collective-permute-done
  9.7 0.0 copy-start.1
  9.7 0.7 %copy-done.1 = bf16[2,256,128]{2,1,0:T(8,128)(2,1)} copy-done((bf16[2,256,128]{2,1,0:T(8,128)(2,1)}, bf16[2,256,128]{2,1,0:T(8,128)(2,1)S(1)}, u32[]{:S(2)}) %copy-start.1) | copy-done | bytes 131096
  10.3 31.0 %shard_map.73 = f32[1,2,8,512]{3,2,1,0:T(8,128)} custom-call(s32[128]{0:T(128)} %pad_add_fusion.1.ints_ref, bf16[2,32,8,128]{3,2,1,0:T(8,128)(2,1)} %bitcast.13, bf16[2,32,8,512]{3,2,1,0:T(8,128)(2,1)} %bitcast.11, bf16[1,128]{1,0:T(2,128)(2,1)} %bitcast.15, bf16[16,2,64,64]{3,2,1,0:T(8,128)(2,1)} %reshape_squeeze.3.values_ref), custom_call_target="tpu_custom_call" | custom-call | tf_op jit(solution)/shard_map/pallas_call | solution.py:169
  41.4 1.4 %copy.19 = f32[2,8,512]{2,1,0:T(8,128)} copy(f32[2,8,512]{2,1,0:T(8,128)} %bitcast.12) | data formatting | bytes 65536
  (3 shorter events, 0.0 us)
Async XLA Ops:
  0.0 7.9 %copy-start = (bf16[1,16,2,4096]{3,2,1,0:T(2,128)(2,1)S(1)}, bf16[1,16,2,4096]{3,2,1,0:T(2,128)(2,1)}, u32[]{:S(2)}) copy-start(bf16[1,16,2,4096]{3,2,1,0:T(2,128)(2,1)} %param.12) | copy-start | bytes 786436
  1.0 8.7 %collective-permute-start = (bf16[2,256,128]{2,1,0:T(8,128)(2,1)S(1)}, bf16[2,256,128]{2,1,0:T(8,128)(2,1)S(1)}, u32[]{:S(2)}, u32[]{:S(2)}) collective-permute-start(bf16[2,256,128]{2,1,0:T(8,128)(2,1)S(1)} %slice.3), channel_id=1, source_target_pairs={{0,32},{32,64},{64,96},{96,128},{128,160},{160,192},{192,224},{1,3... | collective-permute-start | bytes 393224 | tf_op jit(solution)/shard_map/ppermute | solution.py:150
  5.3 0.7 %copy-start.4 = (s32[32,1]{0,1:T(1,128)S(1)}, s32[32,1]{0,1:T(1,128)}, u32[]{:S(2)}) copy-start(s32[32,1]{0,1:T(1,128)} %param.11) | copy-start | bytes 388
  6.1 0.7 %copy-start.2 = (s32[1,16,2]{1,2,0:T(2,128)S(1)}, s32[1,16,2]{1,2,0:T(2,128)}, u32[]{:S(2)}) copy-start(s32[1,16,2]{1,2,0:T(2,128)} %param.9) | copy-start | bytes 388
  6.9 0.7 %copy-start.3 = (s32[1,16,2]{1,2,0:T(2,128)S(1)}, s32[1,16,2]{1,2,0:T(2,128)}, u32[]{:S(2)}) copy-start(s32[1,16,2]{1,2,0:T(2,128)} %param.10) | copy-start | bytes 388
  9.7 0.7 %copy-start.1 = (bf16[2,256,128]{2,1,0:T(8,128)(2,1)}, bf16[2,256,128]{2,1,0:T(8,128)(2,1)S(1)}, u32[]{:S(2)}) copy-start(bf16[2,256,128]{2,1,0:T(8,128)(2,1)S(1)} %collective-permute-done) | copy-start | bytes 393220

commit v11 on v10

--- a/solution.py
+++ b/solution.py
@@ -12,7 +12,7 @@
 
 def fused_kernel(
     slot_count, entries,
-    ints_ref, halo_ref, fields_ref, table_ref, values_ref, out_ref,
+    pairs_ref, lights_ref, picks_ref, halo_ref, fields_ref, table_ref, values_ref, out_ref,
     partials_ref, send_ref, recv_ref, send_sems, recv_sems,
 ):
     block_size = fields_ref.shape[2]
@@ -22,8 +22,6 @@
     square = block_size * block_size
     pair_count = send_ref.shape[0]
     owned = send_ref.shape[1]
-    light_base = 2 * slot_count
-    pick_base = light_base + entries * slot_count
     zero_row = slot_count * entries
     me = lax.axis_index("pair")
     row = lax.axis_index("tm")
@@ -49,8 +47,8 @@
         return jnp.concatenate([halo_ref[part, block], fields_ref[part, block]], 1).astype(jnp.float32)
 
     def body(slot_index, carry):
-        left = ints_ref[2 * slot_index]
-        right = ints_ref[2 * slot_index + 1]
+        left = pairs_ref[0, slot_index, 0]
+        right = pairs_ref[0, slot_index, 1]
         left_real = window(0, left)[:, None]
         left_imag = window(1, left)[:, None]
         right_real = window(0, right)[None]
@@ -71,7 +69,7 @@
             mixed_imag = jnp.dot(matrix, response[square:], preferred_element_type=jnp.float32).reshape(
                 block_size, block_size, length
             )
-            light = ints_ref[light_base + entries * slot_index + entry_index]
+            light = lights_ref[0, slot_index, entry_index]
             light_real = fields_ref[0, light].astype(jnp.float32)[None]
             light_imag = fields_ref[1, light].astype(jnp.float32)[None]
             out_real = jnp.sum(light_real * mixed_real - light_imag * mixed_imag, axis=1)
@@ -84,8 +82,8 @@
 
     def block_sum(peer, part):
         block = peer * owned + part
-        first = ints_ref[pick_base + 2 * block]
-        second = ints_ref[pick_base + 2 * block + 1]
+        first = picks_ref[block, 0]
+        second = picks_ref[block, 1]
         return partials_ref[first] + partials_ref[second]
 
     pl.semaphore_wait(barrier, pair_count - 1)
@@ -160,16 +158,14 @@
     first = jnp.min(jnp.where(feeds, row_index[None], rows), axis=1)
     last = jnp.max(jnp.where(feeds, row_index[None], -1), axis=1)
     second = jnp.where(last > first, last, rows)
-    ints = jnp.concatenate(
-        [pair_blocks.reshape(-1), light_blocks.reshape(-1), jnp.stack([first, second], 1).reshape(-1)]
-    )
+    picks = jnp.stack([first, second], 1)
     smem = pl.BlockSpec(memory_space=pltpu.SMEM)
     vmem = pl.BlockSpec(memory_space=pltpu.VMEM)
     exchange_shape = (pair_count, owned, 2, block_size, length)
     shared = pl.pallas_call(
         functools.partial(fused_kernel, slot_count, entries),
         out_shape=jax.ShapeDtypeStruct((owned, 2, block_size, length), jnp.float32),
-        in_specs=[smem, vmem, vmem, vmem, vmem],
+        in_specs=[smem, smem, smem, vmem, vmem, vmem, vmem],
         out_specs=vmem,
         scratch_shapes=[
             pltpu.VMEM((rows + 1, 2, block_size, length), jnp.float32),
@@ -179,7 +175,7 @@
             pltpu.SemaphoreType.DMA((pair_count,)),
         ],
         compiler_params=pltpu.CompilerParams(collective_id=0, has_side_effects=True),
-    )(ints, halo, fields, raman_taps.reshape(1, tap_count), values)
+    )(pair_blocks, light_blocks, picks, halo, fields, raman_taps.reshape(1, tap_count), values)
     result = jnp.transpose(shared, (1, 0, 2, 3)).reshape(2, owned * block_size, length)
     return result
 

time: 43 us -> 43.4 us (level)
  local copies, waits for them, and re-layouts: 6.57 us -> 7.5 us
  other arithmetic: 0.73 us -> 0.14 us
    another operation x1, local copies, waits for them, and re-layouts: 0.09 us -> 0.69 us  [local(): picks = jnp.stack([first, second], 1)]
    unnamed x13, local copies, waits for them, and re-layouts: 4.1 us -> 4.7 us
    concatenate x1 -> x0, other arithmetic: 0.59 us -> none  [local(): jnp.concatenate([pair_blocks.reshape(-1), light_blocks.reshape(-1), jnp.s...]
  transfers between devices with their start and end apart: 1 -> 1, of which waited for: 0 -> 0; matrix products, arithmetic and copies ran while one was open for 6% -> 8% of each run, Pallas kernels for 0% -> 0%
where the time goes in v11:
time: 43.4 us; the launch traced here: 43.1 us
  Pallas kernels  31.1 us (72%)
  local copies, waits for them, and re-layouts  7.5 us (17%)
  starting transfers between devices  3.68 us (8%)
  between operations  0.7 us (2%)
    pallas_call x1, Pallas kernels, local(): pl.pallas_call(functools.partial(fused_kernel, slot_count, entries), out_...  31.1 us
    unnamed x13, local copies, waits for them, and re-layouts  4.7 us
    ppermute x1, starting transfers between devices, local(): lax.ppermute(mode_fields[:, :, -tap_count:], 'tm', [(k, k + 1) for k in r...  3.68 us
    another operation x1, local copies, waits for them, and re-layouts, local(): values = raman_values[0].reshape(slot_count, entries, square, square)  1.15 us
    slice x1, local copies, waits for them, and re-layouts, local(): mode_fields[:, :, -tap_count:]  0.96 us
  transfers between devices with their start and end apart: 1, of which 0 were waited for; matrix products, arithmetic and copies ran while one was open for 8% of the time, Pallas kernels for 0%

profile of v11, /device:TPU:11, one launch (start us, length us, event | category | flops | bytes accessed | tf_op | source)
XLA Modules:
  0.0 43.1 jit_solution(8805295070404389706)
XLA Ops:
  0.0 0.0 copy-start
  0.0 1.0 %slice.3 = bf16[2,256,128]{2,1,0:T(8,128)(2,1)S(1)} slice(bf16[2,256,512]{2,1,0:T(8,128)(2,1)} %param.7), slice={[0:2], [0:256], [384:512]} | slice | bytes 262144 | tf_op jit(solution)/shard_map/slice | solution.py:149
  1.0 3.7 %collective-permute-start = (bf16[2,256,128]{2,1,0:T(8,128)(2,1)S(1)}, bf16[2,256,128]{2,1,0:T(8,128)(2,1)S(1)}, u32[]{:S(2)}, u32[]{:S(2)}) collective-permute-start(bf16[2,256,128]{2,1,0:T(8,128)(2,1)S(1)} %slice.3), channel_id=1, source_target_pairs={{0,32},{32,64},{64,96},{96,128},{128,160},{160,192},{192,224},{1,3... | collective-permute-start | bytes 393224 | tf_op jit(solution)/shard_map/ppermute | solution.py:148
  5.3 0.0 copy-start.4
  5.3 0.6 %copy-done.4 = s32[32,1]{0,1:T(1,128)S(1)} copy-done((s32[32,1]{0,1:T(1,128)S(1)}, s32[32,1]{0,1:T(1,128)}, u32[]{:S(2)}) %copy-start.4) | copy-done | bytes 152
  6.0 0.1 select_reduce_fusion.1
  6.1 0.0 copy-start.2
  6.1 0.7 %copy-done.2 = s32[1,16,2]{1,2,0:T(2,128)S(1)} copy-done((s32[1,16,2]{1,2,0:T(2,128)S(1)}, s32[1,16,2]{1,2,0:T(2,128)}, u32[]{:S(2)}) %copy-start.2) | copy-done | bytes 152
  6.8 0.0 copy-start.3
  6.8 0.7 %copy.17.pairs_ref = s32[1,16,2]{2,1,0:T(8,128)} copy(s32[1,16,2]{1,2,0:T(2,128)S(1)} %copy-done.2) | data formatting | bytes 256 | tf_op args[2]
  7.4 0.0 copy-done.3
  7.4 0.7 %copy.18.lights_ref = s32[1,16,2]{2,1,0:T(8,128)} copy(s32[1,16,2]{1,2,0:T(2,128)S(1)} %copy-done.3) | data formatting | bytes 256 | tf_op args[3]
  8.1 0.7 %copy.19.picks_ref = s32[32,2]{1,0:T(8,128)} copy(s32[32,2]{0,1:T(2,128)S(1)} %pad_add_fusion) | data formatting | bytes 512 | tf_op jit(solution)/shard_map/stack | solution.py:161
  8.8 0.0 copy-done
  8.8 1.1 %reshape_squeeze.3.values_ref = bf16[16,2,64,64]{3,2,1,0:T(8,128)(2,1)} reshape(bf16[1,16,2,4096]{3,2,1,0:T(2,128)(2,1)S(1)} %copy-done) | data formatting | bytes 524288 | tf_op jit(solution)/shard_map/reshape;squeeze | solution.py:154
  10.0 0.0 collective-permute-done
  10.0 0.0 copy-start.1
  10.0 0.7 %copy-done.1 = bf16[2,256,128]{2,1,0:T(8,128)(2,1)} copy-done((bf16[2,256,128]{2,1,0:T(8,128)(2,1)}, bf16[2,256,128]{2,1,0:T(8,128)(2,1)S(1)}, u32[]{:S(2)}) %copy-start.1) | copy-done | bytes 131096
  10.6 31.1 %shard_map.73 = f32[1,2,8,512]{3,2,1,0:T(8,128)} custom-call(s32[1,16,2]{2,1,0:T(8,128)} %copy.17.pairs_ref, s32[1,16,2]{2,1,0:T(8,128)} %copy.18.lights_ref, s32[32,2]{1,0:T(8,128)} %copy.19.picks_ref, bf16[2,32,8,128]{3,2,1,0:T(8,128)(2,1)} %bitcast.12, bf16[2,32,8,512]{3,2,1,0:T(8,128)(2,1)} %bitcast.11, bf16[1,128]{1,0:T(2,128)(2,1)} %bitcast.15, ...), custom_call_target="tpu_custom_call" | custom-call | tf_op jit(solution)/shard_map/pallas_call | solution.py:165
  41.7 1.4 %copy.22 = f32[2,8,512]{2,1,0:T(8,128)} copy(f32[2,8,512]{2,1,0:T(8,128)} %bitcast.13) | data formatting | bytes 65536
  (3 shorter events, 0.0 us)
Async XLA Ops:
  0.0 8.8 %copy-start = (bf16[1,16,2,4096]{3,2,1,0:T(2,128)(2,1)S(1)}, bf16[1,16,2,4096]{3,2,1,0:T(2,128)(2,1)}, u32[]{:S(2)}) copy-start(bf16[1,16,2,4096]{3,2,1,0:T(2,128)(2,1)} %param.12) | copy-start | bytes 786436
  1.0 9.0 %collective-permute-start = (bf16[2,256,128]{2,1,0:T(8,128)(2,1)S(1)}, bf16[2,256,128]{2,1,0:T(8,128)(2,1)S(1)}, u32[]{:S(2)}, u32[]{:S(2)}) collective-permute-start(bf16[2,256,128]{2,1,0:T(8,128)(2,1)S(1)} %slice.3), channel_id=1, source_target_pairs={{0,32},{32,64},{64,96},{96,128},{128,160},{160,192},{192,224},{1,3... | collective-permute-start | bytes 393224 | tf_op jit(solution)/shard_map/ppermute | solution.py:148
  5.3 0.7 %copy-start.4 = (s32[32,1]{0,1:T(1,128)S(1)}, s32[32,1]{0,1:T(1,128)}, u32[]{:S(2)}) copy-start(s32[32,1]{0,1:T(1,128)} %param.11) | copy-start | bytes 388
  6.1 0.7 %copy-start.2 = (s32[1,16,2]{1,2,0:T(2,128)S(1)}, s32[1,16,2]{1,2,0:T(2,128)}, u32[]{:S(2)}) copy-start(s32[1,16,2]{1,2,0:T(2,128)} %param.9) | copy-start | bytes 388
  6.8 0.7 %copy-start.3 = (s32[1,16,2]{1,2,0:T(2,128)S(1)}, s32[1,16,2]{1,2,0:T(2,128)}, u32[]{:S(2)}) copy-start(s32[1,16,2]{1,2,0:T(2,128)} %param.10) | copy-start | bytes 388
  10.0 0.7 %copy-start.1 = (bf16[2,256,128]{2,1,0:T(8,128)(2,1)}, bf16[2,256,128]{2,1,0:T(8,128)(2,1)S(1)}, u32[]{:S(2)}) copy-start(bf16[2,256,128]{2,1,0:T(8,128)(2,1)S(1)} %collective-permute-done) | copy-start | bytes 393220

commit v12 on v10

--- a/solution.py
+++ b/solution.py
@@ -80,7 +80,7 @@
             partials_ref[entries * slot_index + entry_index, 1] = out_imag
         return carry
 
-    lax.fori_loop(0, slot_count, body, 0)
+    lax.fori_loop(0, slot_count, body, 0, unroll=2)
 
     def block_sum(peer, part):
         block = peer * owned + part

time: 43 us -> 41.6 us (0.967)
  Pallas kernels: 31 us -> 29.7 us
    pallas_call x1, Pallas kernels: 31 us -> 29.7 us  [local(): pl.pallas_call(functools.partial(fused_kernel, slot_count, entries), out_...]
where the time goes in v12:
time: 41.6 us; the launch traced here: 41.4 us
  Pallas kernels  29.7 us (71%)
  local copies, waits for them, and re-layouts  6.57 us (16%)
  starting transfers between devices  3.68 us (9%)
  other arithmetic  0.73 us (2%)
  between operations  0.72 us (2%)
    pallas_call x1, Pallas kernels, local(): pl.pallas_call(functools.partial(fused_kernel, slot_count, entries), out_...  29.7 us
    unnamed x13, local copies, waits for them, and re-layouts  4.1 us
    ppermute x1, starting transfers between devices, local(): lax.ppermute(mode_fields[:, :, -tap_count:], 'tm', [(k, k + 1) for k in r...  3.68 us
    another operation x1, local copies, waits for them, and re-layouts, local(): values = raman_values[0].reshape(slot_count, entries, square, square)  1.15 us
    slice x1, local copies, waits for them, and re-layouts, local(): mode_fields[:, :, -tap_count:]  0.96 us
  transfers between devices with their start and end apart: 1, of which 0 were waited for; matrix products, arithmetic and copies ran while one was open for 6% of the time, Pallas kernels for 0%

profile of v12, /device:TPU:11, one launch (start us, length us, event | category | flops | bytes accessed | tf_op | source)
XLA Modules:
  0.0 41.4 jit_solution(16031718735254264246)
XLA Ops:
  0.0 0.0 copy-start
  0.0 1.0 %slice.3 = bf16[2,256,128]{2,1,0:T(8,128)(2,1)S(1)} slice(bf16[2,256,512]{2,1,0:T(8,128)(2,1)} %param.7), slice={[0:2], [0:256], [384:512]} | slice | bytes 262144 | tf_op jit(solution)/shard_map/slice | solution.py:151
  1.0 3.7 %collective-permute-start = (bf16[2,256,128]{2,1,0:T(8,128)(2,1)S(1)}, bf16[2,256,128]{2,1,0:T(8,128)(2,1)S(1)}, u32[]{:S(2)}, u32[]{:S(2)}) collective-permute-start(bf16[2,256,128]{2,1,0:T(8,128)(2,1)S(1)} %slice.3), channel_id=1, source_target_pairs={{0,32},{32,64},{64,96},{96,128},{128,160},{160,192},{192,224},{1,3... | collective-permute-start | bytes 393224 | tf_op jit(solution)/shard_map/ppermute | solution.py:150
  5.3 0.0 copy-start.4
  5.3 0.6 %copy-done.4 = s32[32,1]{0,1:T(1,128)S(1)} copy-done((s32[32,1]{0,1:T(1,128)S(1)}, s32[32,1]{0,1:T(1,128)}, u32[]{:S(2)}) %copy-start.4) | copy-done | bytes 152
  6.0 0.1 select_reduce_fusion.1
  6.1 0.0 copy-start.2
  6.1 0.7 %copy-done.2 = s32[1,16,2]{1,2,0:T(2,128)S(1)} copy-done((s32[1,16,2]{1,2,0:T(2,128)S(1)}, s32[1,16,2]{1,2,0:T(2,128)}, u32[]{:S(2)}) %copy-start.2) | copy-done | bytes 152
  6.8 0.1 copy.14
  6.9 0.0 copy-start.3
  6.9 0.1 reshape.48
  7.0 0.6 %copy-done.3 = s32[1,16,2]{1,2,0:T(2,128)S(1)} copy-done((s32[1,16,2]{1,2,0:T(2,128)S(1)}, s32[1,16,2]{1,2,0:T(2,128)}, u32[]{:S(2)}) %copy-start.3) | copy-done | bytes 152
  7.5 0.1 copy.15
  7.6 0.1 reshape.49
  7.7 0.1 copy.16
  7.8 0.1 reshape.50
  7.9 0.0 copy-done
  7.9 1.1 %reshape_squeeze.3.values_ref = bf16[16,2,64,64]{3,2,1,0:T(8,128)(2,1)} reshape(bf16[1,16,2,4096]{3,2,1,0:T(2,128)(2,1)S(1)} %copy-done) | data formatting | bytes 524288 | tf_op jit(solution)/shard_map/reshape;squeeze | solution.py:156
  9.1 0.6 %pad_add_fusion.1.ints_ref = s32[128]{0:T(128)} fusion(s32[64]{0:T(128)S(1)} %reshape.50, s32[32]{0:T(128)S(1)} %reshape.49, s32[32]{0:T(128)S(1)} %reshape.48), kind=kLoop, calls=%fused_computation.11 | loop fusion | flops 256 | bytes 1024 | tf_op jit(solution)/shard_map/concatenate | solution.py:163
  9.7 0.0 collective-permute-done
  9.7 0.0 copy-start.1
  9.7 0.7 %copy-done.1 = bf16[2,256,128]{2,1,0:T(8,128)(2,1)} copy-done((bf16[2,256,128]{2,1,0:T(8,128)(2,1)}, bf16[2,256,128]{2,1,0:T(8,128)(2,1)S(1)}, u32[]{:S(2)}) %copy-start.1) | copy-done | bytes 131096
  10.3 29.7 %shard_map.73 = f32[1,2,8,512]{3,2,1,0:T(8,128)} custom-call(s32[128]{0:T(128)} %pad_add_fusion.1.ints_ref, bf16[2,32,8,128]{3,2,1,0:T(8,128)(2,1)} %bitcast.13, bf16[2,32,8,512]{3,2,1,0:T(8,128)(2,1)} %bitcast.11, bf16[1,128]{1,0:T(2,128)(2,1)} %bitcast.15, bf16[16,2,64,64]{3,2,1,0:T(8,128)(2,1)} %reshape_squeeze.3.values_ref), custom_call_target="tpu_custom_call" | custom-call | tf_op jit(solution)/shard_map/pallas_call | solution.py:169
  40.0 1.4 %copy.19 = f32[2,8,512]{2,1,0:T(8,128)} copy(f32[2,8,512]{2,1,0:T(8,128)} %bitcast.12) | data formatting | bytes 65536
  (3 shorter events, 0.0 us)
Async XLA Ops:
  0.0 7.9 %copy-start = (bf16[1,16,2,4096]{3,2,1,0:T(2,128)(2,1)S(1)}, bf16[1,16,2,4096]{3,2,1,0:T(2,128)(2,1)}, u32[]{:S(2)}) copy-start(bf16[1,16,2,4096]{3,2,1,0:T(2,128)(2,1)} %param.12) | copy-start | bytes 786436
  1.0 8.7 %collective-permute-start = (bf16[2,256,128]{2,1,0:T(8,128)(2,1)S(1)}, bf16[2,256,128]{2,1,0:T(8,128)(2,1)S(1)}, u32[]{:S(2)}, u32[]{:S(2)}) collective-permute-start(bf16[2,256,128]{2,1,0:T(8,128)(2,1)S(1)} %slice.3), channel_id=1, source_target_pairs={{0,32},{32,64},{64,96},{96,128},{128,160},{160,192},{192,224},{1,3... | collective-permute-start | bytes 393224 | tf_op jit(solution)/shard_map/ppermute | solution.py:150
  5.3 0.7 %copy-start.4 = (s32[32,1]{0,1:T(1,128)S(1)}, s32[32,1]{0,1:T(1,128)}, u32[]{:S(2)}) copy-start(s32[32,1]{0,1:T(1,128)} %param.11) | copy-start | bytes 388
  6.1 0.7 %copy-start.2 = (s32[1,16,2]{1,2,0:T(2,128)S(1)}, s32[1,16,2]{1,2,0:T(2,128)}, u32[]{:S(2)}) copy-start(s32[1,16,2]{1,2,0:T(2,128)} %param.9) | copy-start | bytes 388
  6.9 0.7 %copy-start.3 = (s32[1,16,2]{1,2,0:T(2,128)S(1)}, s32[1,16,2]{1,2,0:T(2,128)}, u32[]{:S(2)}) copy-start(s32[1,16,2]{1,2,0:T(2,128)} %param.10) | copy-start | bytes 388
  9.7 0.7 %copy-start.1 = (bf16[2,256,128]{2,1,0:T(8,128)(2,1)}, bf16[2,256,128]{2,1,0:T(8,128)(2,1)S(1)}, u32[]{:S(2)}) copy-start(bf16[2,256,128]{2,1,0:T(8,128)(2,1)S(1)} %collective-permute-done) | copy-start | bytes 393220

commit v13 on v12

--- a/solution.py
+++ b/solution.py
@@ -80,7 +80,7 @@
             partials_ref[entries * slot_index + entry_index, 1] = out_imag
         return carry
 
-    lax.fori_loop(0, slot_count, body, 0, unroll=2)
+    lax.fori_loop(0, slot_count, body, 0, unroll=4)
 
     def block_sum(peer, part):
         block = peer * owned + part

time: 41.6 us -> 41 us (0.986)
  Pallas kernels: 29.7 us -> 29 us
    pallas_call x1, Pallas kernels: 29.7 us -> 29 us  [local(): pl.pallas_call(functools.partial(fused_kernel, slot_count, entries), out_...]
where the time goes in v13:
time: 41 us; the launch traced here: 40.7 us
  Pallas kernels  29 us (71%)
  local copies, waits for them, and re-layouts  6.57 us (16%)
  starting transfers between devices  3.68 us (9%)
  other arithmetic  0.73 us (2%)
  between operations  0.72 us (2%)
    pallas_call x1, Pallas kernels, local(): pl.pallas_call(functools.partial(fused_kernel, slot_count, entries), out_...  29 us
    unnamed x13, local copies, waits for them, and re-layouts  4.1 us
    ppermute x1, starting transfers between devices, local(): lax.ppermute(mode_fields[:, :, -tap_count:], 'tm', [(k, k + 1) for k in r...  3.68 us
    another operation x1, local copies, waits for them, and re-layouts, local(): values = raman_values[0].reshape(slot_count, entries, square, square)  1.15 us
    slice x1, local copies, waits for them, and re-layouts, local(): mode_fields[:, :, -tap_count:]  0.96 us
  transfers between devices with their start and end apart: 1, of which 0 were waited for; matrix products, arithmetic and copies ran while one was open for 6% of the time, Pallas kernels for 0%

profile of v13, /device:TPU:11, one launch (start us, length us, event | category | flops | bytes accessed | tf_op | source)
XLA Modules:
  0.0 40.7 jit_solution(11821718745954550008)
XLA Ops:
  0.0 0.0 copy-start
  0.0 1.0 %slice.3 = bf16[2,256,128]{2,1,0:T(8,128)(2,1)S(1)} slice(bf16[2,256,512]{2,1,0:T(8,128)(2,1)} %param.7), slice={[0:2], [0:256], [384:512]} | slice | bytes 262144 | tf_op jit(solution)/shard_map/slice | solution.py:151
  1.0 3.7 %collective-permute-start = (bf16[2,256,128]{2,1,0:T(8,128)(2,1)S(1)}, bf16[2,256,128]{2,1,0:T(8,128)(2,1)S(1)}, u32[]{:S(2)}, u32[]{:S(2)}) collective-permute-start(bf16[2,256,128]{2,1,0:T(8,128)(2,1)S(1)} %slice.3), channel_id=1, source_target_pairs={{0,32},{32,64},{64,96},{96,128},{128,160},{160,192},{192,224},{1,3... | collective-permute-start | bytes 393224 | tf_op jit(solution)/shard_map/ppermute | solution.py:150
  5.3 0.0 copy-start.4
  5.3 0.6 %copy-done.4 = s32[32,1]{0,1:T(1,128)S(1)} copy-done((s32[32,1]{0,1:T(1,128)S(1)}, s32[32,1]{0,1:T(1,128)}, u32[]{:S(2)}) %copy-start.4) | copy-done | bytes 152
  6.0 0.1 select_reduce_fusion.1
  6.1 0.0 copy-start.2
  6.1 0.7 %copy-done.2 = s32[1,16,2]{1,2,0:T(2,128)S(1)} copy-done((s32[1,16,2]{1,2,0:T(2,128)S(1)}, s32[1,16,2]{1,2,0:T(2,128)}, u32[]{:S(2)}) %copy-start.2) | copy-done | bytes 152
  6.8 0.1 copy.14
  6.9 0.0 copy-start.3
  6.9 0.1 reshape.48
  7.0 0.6 %copy-done.3 = s32[1,16,2]{1,2,0:T(2,128)S(1)} copy-done((s32[1,16,2]{1,2,0:T(2,128)S(1)}, s32[1,16,2]{1,2,0:T(2,128)}, u32[]{:S(2)}) %copy-start.3) | copy-done | bytes 152
  7.5 0.1 copy.15
  7.6 0.1 reshape.49
  7.7 0.1 copy.16
  7.8 0.1 reshape.50
  7.9 0.0 copy-done
  7.9 1.1 %reshape_squeeze.3.values_ref = bf16[16,2,64,64]{3,2,1,0:T(8,128)(2,1)} reshape(bf16[1,16,2,4096]{3,2,1,0:T(2,128)(2,1)S(1)} %copy-done) | data formatting | bytes 524288 | tf_op jit(solution)/shard_map/reshape;squeeze | solution.py:156
  9.1 0.6 %pad_add_fusion.1.ints_ref = s32[128]{0:T(128)} fusion(s32[64]{0:T(128)S(1)} %reshape.50, s32[32]{0:T(128)S(1)} %reshape.49, s32[32]{0:T(128)S(1)} %reshape.48), kind=kLoop, calls=%fused_computation.11 | loop fusion | flops 256 | bytes 1024 | tf_op jit(solution)/shard_map/concatenate | solution.py:163
  9.7 0.0 collective-permute-done
  9.7 0.0 copy-start.1
  9.7 0.7 %copy-done.1 = bf16[2,256,128]{2,1,0:T(8,128)(2,1)} copy-done((bf16[2,256,128]{2,1,0:T(8,128)(2,1)}, bf16[2,256,128]{2,1,0:T(8,128)(2,1)S(1)}, u32[]{:S(2)}) %copy-start.1) | copy-done | bytes 131096
  10.3 29.0 %shard_map.73 = f32[1,2,8,512]{3,2,1,0:T(8,128)} custom-call(s32[128]{0:T(128)} %pad_add_fusion.1.ints_ref, bf16[2,32,8,128]{3,2,1,0:T(8,128)(2,1)} %bitcast.13, bf16[2,32,8,512]{3,2,1,0:T(8,128)(2,1)} %bitcast.11, bf16[1,128]{1,0:T(2,128)(2,1)} %bitcast.15, bf16[16,2,64,64]{3,2,1,0:T(8,128)(2,1)} %reshape_squeeze.3.values_ref), custom_call_target="tpu_custom_call" | custom-call | tf_op jit(solution)/shard_map/pallas_call | solution.py:169
  39.3 1.4 %copy.19 = f32[2,8,512]{2,1,0:T(8,128)} copy(f32[2,8,512]{2,1,0:T(8,128)} %bitcast.12) | data formatting | bytes 65536
  (3 shorter events, 0.0 us)
Async XLA Ops:
  0.0 7.9 %copy-start = (bf16[1,16,2,4096]{3,2,1,0:T(2,128)(2,1)S(1)}, bf16[1,16,2,4096]{3,2,1,0:T(2,128)(2,1)}, u32[]{:S(2)}) copy-start(bf16[1,16,2,4096]{3,2,1,0:T(2,128)(2,1)} %param.12) | copy-start | bytes 786436
  1.0 8.7 %collective-permute-start = (bf16[2,256,128]{2,1,0:T(8,128)(2,1)S(1)}, bf16[2,256,128]{2,1,0:T(8,128)(2,1)S(1)}, u32[]{:S(2)}, u32[]{:S(2)}) collective-permute-start(bf16[2,256,128]{2,1,0:T(8,128)(2,1)S(1)} %slice.3), channel_id=1, source_target_pairs={{0,32},{32,64},{64,96},{96,128},{128,160},{160,192},{192,224},{1,3... | collective-permute-start | bytes 393224 | tf_op jit(solution)/shard_map/ppermute | solution.py:150
  5.3 0.7 %copy-start.4 = (s32[32,1]{0,1:T(1,128)S(1)}, s32[32,1]{0,1:T(1,128)}, u32[]{:S(2)}) copy-start(s32[32,1]{0,1:T(1,128)} %param.11) | copy-start | bytes 388
  6.1 0.7 %copy-start.2 = (s32[1,16,2]{1,2,0:T(2,128)S(1)}, s32[1,16,2]{1,2,0:T(2,128)}, u32[]{:S(2)}) copy-start(s32[1,16,2]{1,2,0:T(2,128)} %param.9) | copy-start | bytes 388
  6.9 0.7 %copy-start.3 = (s32[1,16,2]{1,2,0:T(2,128)S(1)}, s32[1,16,2]{1,2,0:T(2,128)}, u32[]{:S(2)}) copy-start(s32[1,16,2]{1,2,0:T(2,128)} %param.10) | copy-start | bytes 388
  9.7 0.7 %copy-start.1 = (bf16[2,256,128]{2,1,0:T(8,128)(2,1)}, bf16[2,256,128]{2,1,0:T(8,128)(2,1)S(1)}, u32[]{:S(2)}) copy-start(bf16[2,256,128]{2,1,0:T(8,128)(2,1)S(1)} %collective-permute-done) | copy-start | bytes 393220

commit v14 on v13

--- a/solution.py
+++ b/solution.py
@@ -107,7 +107,7 @@
         outgoing(peer).start()
         return carry
 
-    lax.fori_loop(1, pair_count, send, 0)
+    lax.fori_loop(1, pair_count, send, 0, unroll=4)
 
     def gather(step, total):
         peer = lax.rem(me + pair_count - step, pair_count)
@@ -123,7 +123,7 @@
         return total + recv_ref[peer].astype(jnp.float32)
 
     own = jnp.stack([block_sum(me, part) for part in range(owned)])
-    total = lax.fori_loop(1, pair_count, gather, own)
+    total = lax.fori_loop(1, pair_count, gather, own, unroll=4)
 
     def finish(step, carry):
         outgoing(lax.rem(me + step, pair_count)).wait_send()

time: 41 us -> 41 us (level)
  no operation moved by 1% of the time
where the time goes in v14:
time: 41 us; the launch traced here: 40.7 us
  Pallas kernels  29 us (71%)
  local copies, waits for them, and re-layouts  6.57 us (16%)
  starting transfers between devices  3.68 us (9%)
  other arithmetic  0.73 us (2%)
  between operations  0.72 us (2%)
    pallas_call x1, Pallas kernels, local(): pl.pallas_call(functools.partial(fused_kernel, slot_count, entries), out_...  29 us
    unnamed x13, local copies, waits for them, and re-layouts  4.1 us
    ppermute x1, starting transfers between devices, local(): lax.ppermute(mode_fields[:, :, -tap_count:], 'tm', [(k, k + 1) for k in r...  3.68 us
    another operation x1, local copies, waits for them, and re-layouts, local(): values = raman_values[0].reshape(slot_count, entries, square, square)  1.15 us
    slice x1, local copies, waits for them, and re-layouts, local(): mode_fields[:, :, -tap_count:]  0.96 us
  transfers between devices with their start and end apart: 1, of which 0 were waited for; matrix products, arithmetic and copies ran while one was open for 6% of the time, Pallas kernels for 0%

profile of v14, /device:TPU:11, one launch (start us, length us, event | category | flops | bytes accessed | tf_op | source)
XLA Modules:
  0.0 40.7 jit_solution(16390784697370493506)
XLA Ops:
  0.0 0.0 copy-start
  0.0 1.0 %slice.3 = bf16[2,256,128]{2,1,0:T(8,128)(2,1)S(1)} slice(bf16[2,256,512]{2,1,0:T(8,128)(2,1)} %param.7), slice={[0:2], [0:256], [384:512]} | slice | bytes 262144 | tf_op jit(solution)/shard_map/slice | solution.py:151
  1.0 3.7 %collective-permute-start = (bf16[2,256,128]{2,1,0:T(8,128)(2,1)S(1)}, bf16[2,256,128]{2,1,0:T(8,128)(2,1)S(1)}, u32[]{:S(2)}, u32[]{:S(2)}) collective-permute-start(bf16[2,256,128]{2,1,0:T(8,128)(2,1)S(1)} %slice.3), channel_id=1, source_target_pairs={{0,32},{32,64},{64,96},{96,128},{128,160},{160,192},{192,224},{1,3... | collective-permute-start | bytes 393224 | tf_op jit(solution)/shard_map/ppermute | solution.py:150
  5.3 0.0 copy-start.4
  5.3 0.6 %copy-done.4 = s32[32,1]{0,1:T(1,128)S(1)} copy-done((s32[32,1]{0,1:T(1,128)S(1)}, s32[32,1]{0,1:T(1,128)}, u32[]{:S(2)}) %copy-start.4) | copy-done | bytes 152
  6.0 0.1 select_reduce_fusion.1
  6.1 0.0 copy-start.2
  6.1 0.7 %copy-done.2 = s32[1,16,2]{1,2,0:T(2,128)S(1)} copy-done((s32[1,16,2]{1,2,0:T(2,128)S(1)}, s32[1,16,2]{1,2,0:T(2,128)}, u32[]{:S(2)}) %copy-start.2) | copy-done | bytes 152
  6.8 0.1 copy.14
  6.9 0.0 copy-start.3
  6.9 0.1 reshape.48
  7.0 0.6 %copy-done.3 = s32[1,16,2]{1,2,0:T(2,128)S(1)} copy-done((s32[1,16,2]{1,2,0:T(2,128)S(1)}, s32[1,16,2]{1,2,0:T(2,128)}, u32[]{:S(2)}) %copy-start.3) | copy-done | bytes 152
  7.5 0.1 copy.15
  7.6 0.1 reshape.49
  7.7 0.1 copy.16
  7.8 0.1 reshape.50
  7.9 0.0 copy-done
  7.9 1.1 %reshape_squeeze.3.values_ref = bf16[16,2,64,64]{3,2,1,0:T(8,128)(2,1)} reshape(bf16[1,16,2,4096]{3,2,1,0:T(2,128)(2,1)S(1)} %copy-done) | data formatting | bytes 524288 | tf_op jit(solution)/shard_map/reshape;squeeze | solution.py:156
  9.1 0.6 %pad_add_fusion.1.ints_ref = s32[128]{0:T(128)} fusion(s32[64]{0:T(128)S(1)} %reshape.50, s32[32]{0:T(128)S(1)} %reshape.49, s32[32]{0:T(128)S(1)} %reshape.48), kind=kLoop, calls=%fused_computation.11 | loop fusion | flops 256 | bytes 1024 | tf_op jit(solution)/shard_map/concatenate | solution.py:163
  9.7 0.0 collective-permute-done
  9.7 0.0 copy-start.1
  9.7 0.7 %copy-done.1 = bf16[2,256,128]{2,1,0:T(8,128)(2,1)} copy-done((bf16[2,256,128]{2,1,0:T(8,128)(2,1)}, bf16[2,256,128]{2,1,0:T(8,128)(2,1)S(1)}, u32[]{:S(2)}) %copy-start.1) | copy-done | bytes 131096
  10.3 29.0 %shard_map.73 = f32[1,2,8,512]{3,2,1,0:T(8,128)} custom-call(s32[128]{0:T(128)} %pad_add_fusion.1.ints_ref, bf16[2,32,8,128]{3,2,1,0:T(8,128)(2,1)} %bitcast.13, bf16[2,32,8,512]{3,2,1,0:T(8,128)(2,1)} %bitcast.11, bf16[1,128]{1,0:T(2,128)(2,1)} %bitcast.15, bf16[16,2,64,64]{3,2,1,0:T(8,128)(2,1)} %reshape_squeeze.3.values_ref), custom_call_target="tpu_custom_call" | custom-call | tf_op jit(solution)/shard_map/pallas_call | solution.py:169
  39.3 1.4 %copy.19 = f32[2,8,512]{2,1,0:T(8,128)} copy(f32[2,8,512]{2,1,0:T(8,128)} %bitcast.12) | data formatting | bytes 65536
  (3 shorter events, 0.0 us)
Async XLA Ops:
  0.0 7.9 %copy-start = (bf16[1,16,2,4096]{3,2,1,0:T(2,128)(2,1)S(1)}, bf16[1,16,2,4096]{3,2,1,0:T(2,128)(2,1)}, u32[]{:S(2)}) copy-start(bf16[1,16,2,4096]{3,2,1,0:T(2,128)(2,1)} %param.12) | copy-start | bytes 786436
  1.0 8.7 %collective-permute-start = (bf16[2,256,128]{2,1,0:T(8,128)(2,1)S(1)}, bf16[2,256,128]{2,1,0:T(8,128)(2,1)S(1)}, u32[]{:S(2)}, u32[]{:S(2)}) collective-permute-start(bf16[2,256,128]{2,1,0:T(8,128)(2,1)S(1)} %slice.3), channel_id=1, source_target_pairs={{0,32},{32,64},{64,96},{96,128},{128,160},{160,192},{192,224},{1,3... | collective-permute-start | bytes 393224 | tf_op jit(solution)/shard_map/ppermute | solution.py:150
  5.3 0.7 %copy-start.4 = (s32[32,1]{0,1:T(1,128)S(1)}, s32[32,1]{0,1:T(1,128)}, u32[]{:S(2)}) copy-start(s32[32,1]{0,1:T(1,128)} %param.11) | copy-start | bytes 388
  6.1 0.7 %copy-start.2 = (s32[1,16,2]{1,2,0:T(2,128)S(1)}, s32[1,16,2]{1,2,0:T(2,128)}, u32[]{:S(2)}) copy-start(s32[1,16,2]{1,2,0:T(2,128)} %param.9) | copy-start | bytes 388
  6.9 0.7 %copy-start.3 = (s32[1,16,2]{1,2,0:T(2,128)S(1)}, s32[1,16,2]{1,2,0:T(2,128)}, u32[]{:S(2)}) copy-start(s32[1,16,2]{1,2,0:T(2,128)} %param.10) | copy-start | bytes 388
  9.7 0.7 %copy-start.1 = (bf16[2,256,128]{2,1,0:T(8,128)(2,1)}, bf16[2,256,128]{2,1,0:T(8,128)(2,1)S(1)}, u32[]{:S(2)}) copy-start(bf16[2,256,128]{2,1,0:T(8,128)(2,1)S(1)} %collective-permute-done) | copy-start | bytes 393220

commit v15 on v13

--- a/solution.py
+++ b/solution.py
@@ -80,7 +80,7 @@
             partials_ref[entries * slot_index + entry_index, 1] = out_imag
         return carry
 
-    lax.fori_loop(0, slot_count, body, 0, unroll=4)
+    lax.fori_loop(0, slot_count, body, 0, unroll=True)
 
     def block_sum(peer, part):
         block = peer * owned + part

time: 41 us -> 40.4 us (0.985)
  Pallas kernels: 29 us -> 28.5 us
    pallas_call x1, Pallas kernels: 29 us -> 28.5 us  [local(): pl.pallas_call(functools.partial(fused_kernel, slot_count, entries), out_...]
where the time goes in v15:
time: 40.4 us; the launch traced here: 40.2 us
  Pallas kernels  28.5 us (71%)
  local copies, waits for them, and re-layouts  6.57 us (16%)
  starting transfers between devices  3.68 us (9%)
  other arithmetic  0.73 us (2%)
  between operations  0.72 us (2%)
    pallas_call x1, Pallas kernels, local(): pl.pallas_call(functools.partial(fused_kernel, slot_count, entries), out_...  28.5 us
    unnamed x13, local copies, waits for them, and re-layouts  4.1 us
    ppermute x1, starting transfers between devices, local(): lax.ppermute(mode_fields[:, :, -tap_count:], 'tm', [(k, k + 1) for k in r...  3.68 us
    another operation x1, local copies, waits for them, and re-layouts, local(): values = raman_values[0].reshape(slot_count, entries, square, square)  1.15 us
    slice x1, local copies, waits for them, and re-layouts, local(): mode_fields[:, :, -tap_count:]  0.96 us
  transfers between devices with their start and end apart: 1, of which 0 were waited for; matrix products, arithmetic and copies ran while one was open for 6% of the time, Pallas kernels for 0%

profile of v15, /device:TPU:11, one launch (start us, length us, event | category | flops | bytes accessed | tf_op | source)
XLA Modules:
  0.0 40.2 jit_solution(8927700760178390396)
XLA Ops:
  0.0 0.0 copy-start
  0.0 1.0 %slice.3 = bf16[2,256,128]{2,1,0:T(8,128)(2,1)S(1)} slice(bf16[2,256,512]{2,1,0:T(8,128)(2,1)} %param.7), slice={[0:2], [0:256], [384:512]} | slice | bytes 262144 | tf_op jit(solution)/shard_map/slice | solution.py:151
  1.0 3.7 %collective-permute-start = (bf16[2,256,128]{2,1,0:T(8,128)(2,1)S(1)}, bf16[2,256,128]{2,1,0:T(8,128)(2,1)S(1)}, u32[]{:S(2)}, u32[]{:S(2)}) collective-permute-start(bf16[2,256,128]{2,1,0:T(8,128)(2,1)S(1)} %slice.3), channel_id=1, source_target_pairs={{0,32},{32,64},{64,96},{96,128},{128,160},{160,192},{192,224},{1,3... | collective-permute-start | bytes 393224 | tf_op jit(solution)/shard_map/ppermute | solution.py:150
  5.3 0.0 copy-start.4
  5.3 0.6 %copy-done.4 = s32[32,1]{0,1:T(1,128)S(1)} copy-done((s32[32,1]{0,1:T(1,128)S(1)}, s32[32,1]{0,1:T(1,128)}, u32[]{:S(2)}) %copy-start.4) | copy-done | bytes 152
  6.0 0.1 select_reduce_fusion.1
  6.1 0.0 copy-start.2
  6.1 0.7 %copy-done.2 = s32[1,16,2]{1,2,0:T(2,128)S(1)} copy-done((s32[1,16,2]{1,2,0:T(2,128)S(1)}, s32[1,16,2]{1,2,0:T(2,128)}, u32[]{:S(2)}) %copy-start.2) | copy-done | bytes 152
  6.8 0.1 copy.14
  6.9 0.0 copy-start.3
  6.9 0.1 reshape.48
  7.0 0.6 %copy-done.3 = s32[1,16,2]{1,2,0:T(2,128)S(1)} copy-done((s32[1,16,2]{1,2,0:T(2,128)S(1)}, s32[1,16,2]{1,2,0:T(2,128)}, u32[]{:S(2)}) %copy-start.3) | copy-done | bytes 152
  7.5 0.1 copy.15
  7.6 0.1 reshape.49
  7.7 0.1 copy.16
  7.8 0.1 reshape.50
  7.9 0.0 copy-done
  7.9 1.1 %reshape_squeeze.3.values_ref = bf16[16,2,64,64]{3,2,1,0:T(8,128)(2,1)} reshape(bf16[1,16,2,4096]{3,2,1,0:T(2,128)(2,1)S(1)} %copy-done) | data formatting | bytes 524288 | tf_op jit(solution)/shard_map/reshape;squeeze | solution.py:156
  9.1 0.6 %pad_add_fusion.1.ints_ref = s32[128]{0:T(128)} fusion(s32[64]{0:T(128)S(1)} %reshape.50, s32[32]{0:T(128)S(1)} %reshape.49, s32[32]{0:T(128)S(1)} %reshape.48), kind=kLoop, calls=%fused_computation.11 | loop fusion | flops 256 | bytes 1024 | tf_op jit(solution)/shard_map/concatenate | solution.py:163
  9.7 0.0 collective-permute-done
  9.7 0.0 copy-start.1
  9.7 0.7 %copy-done.1 = bf16[2,256,128]{2,1,0:T(8,128)(2,1)} copy-done((bf16[2,256,128]{2,1,0:T(8,128)(2,1)}, bf16[2,256,128]{2,1,0:T(8,128)(2,1)S(1)}, u32[]{:S(2)}) %copy-start.1) | copy-done | bytes 131096
  10.3 28.5 %shard_map.73 = f32[1,2,8,512]{3,2,1,0:T(8,128)} custom-call(s32[128]{0:T(128)} %pad_add_fusion.1.ints_ref, bf16[2,32,8,128]{3,2,1,0:T(8,128)(2,1)} %bitcast.13, bf16[2,32,8,512]{3,2,1,0:T(8,128)(2,1)} %bitcast.11, bf16[1,128]{1,0:T(2,128)(2,1)} %bitcast.15, bf16[16,2,64,64]{3,2,1,0:T(8,128)(2,1)} %reshape_squeeze.3.values_ref), custom_call_target="tpu_custom_call" | custom-call | tf_op jit(solution)/shard_map/pallas_call | solution.py:169
  38.8 1.4 %copy.19 = f32[2,8,512]{2,1,0:T(8,128)} copy(f32[2,8,512]{2,1,0:T(8,128)} %bitcast.12) | data formatting | bytes 65536
  (3 shorter events, 0.0 us)
Async XLA Ops:
  0.0 7.9 %copy-start = (bf16[1,16,2,4096]{3,2,1,0:T(2,128)(2,1)S(1)}, bf16[1,16,2,4096]{3,2,1,0:T(2,128)(2,1)}, u32[]{:S(2)}) copy-start(bf16[1,16,2,4096]{3,2,1,0:T(2,128)(2,1)} %param.12) | copy-start | bytes 786436
  1.0 8.7 %collective-permute-start = (bf16[2,256,128]{2,1,0:T(8,128)(2,1)S(1)}, bf16[2,256,128]{2,1,0:T(8,128)(2,1)S(1)}, u32[]{:S(2)}, u32[]{:S(2)}) collective-permute-start(bf16[2,256,128]{2,1,0:T(8,128)(2,1)S(1)} %slice.3), channel_id=1, source_target_pairs={{0,32},{32,64},{64,96},{96,128},{128,160},{160,192},{192,224},{1,3... | collective-permute-start | bytes 393224 | tf_op jit(solution)/shard_map/ppermute | solution.py:150
  5.3 0.7 %copy-start.4 = (s32[32,1]{0,1:T(1,128)S(1)}, s32[32,1]{0,1:T(1,128)}, u32[]{:S(2)}) copy-start(s32[32,1]{0,1:T(1,128)} %param.11) | copy-start | bytes 388
  6.1 0.7 %copy-start.2 = (s32[1,16,2]{1,2,0:T(2,128)S(1)}, s32[1,16,2]{1,2,0:T(2,128)}, u32[]{:S(2)}) copy-start(s32[1,16,2]{1,2,0:T(2,128)} %param.9) | copy-start | bytes 388
  6.9 0.7 %copy-start.3 = (s32[1,16,2]{1,2,0:T(2,128)S(1)}, s32[1,16,2]{1,2,0:T(2,128)}, u32[]{:S(2)}) copy-start(s32[1,16,2]{1,2,0:T(2,128)} %param.10) | copy-start | bytes 388
  9.7 0.7 %copy-start.1 = (bf16[2,256,128]{2,1,0:T(8,128)(2,1)}, bf16[2,256,128]{2,1,0:T(8,128)(2,1)S(1)}, u32[]{:S(2)}) copy-start(bf16[2,256,128]{2,1,0:T(8,128)(2,1)S(1)} %collective-permute-done) | copy-start | bytes 393220

commit v16 on v15

--- a/solution.py
+++ b/solution.py
@@ -39,11 +39,12 @@
 
     partials_ref[zero_row] = jnp.zeros(partials_ref.shape[1:], partials_ref.dtype)
     tap_count = halo_ref.shape[3]
+    period = (fields_ref.shape[3] + halo_ref.shape[3] + fields_ref.shape[3]) // tap_count * tap_count
     taps = table_ref[...].astype(jnp.float32)
-    padded = jnp.concatenate([taps, jnp.zeros((1, 2 * tap_count), jnp.float32)], 1)
-    spread = jnp.broadcast_to(padded, (2 * tap_count, 3 * tap_count))
-    rolled = pltpu.roll(spread, 2 * tap_count + 1, 1, stride=1, stride_axis=0)
-    table = rolled[:, :tap_count].astype(jnp.bfloat16)
+    padded = jnp.concatenate([taps, jnp.zeros((1, period - tap_count), jnp.float32)], 1)
+    spread = jnp.broadcast_to(padded, (fields_ref.shape[3] + tap_count, period))
+    rolled = pltpu.roll(spread, period - tap_count + 1, 1, stride=1, stride_axis=0)
+    table = rolled[:, :fields_ref.shape[3]].astype(jnp.bfloat16)
 
     def window(part, block):
         return jnp.concatenate([halo_ref[part, block], fields_ref[part, block]], 1).astype(jnp.float32)
@@ -58,11 +59,7 @@
         real_part = (left_real * right_real + left_imag * right_imag).reshape(square, width)
         imag_part = (left_imag * right_real - left_real * right_imag).reshape(square, width)
         intensity = jnp.concatenate([real_part, imag_part], 0).astype(jnp.bfloat16)
-        pieces = []
-        for piece in range(length // tap_count):
-            span = intensity[:, piece * tap_count:piece * tap_count + 2 * tap_count]
-            pieces.append(jnp.dot(span, table, preferred_element_type=jnp.float32))
-        response = jnp.concatenate(pieces, 1).astype(jnp.bfloat16)
+        response = jnp.dot(intensity, table, preferred_element_type=jnp.float32).astype(jnp.bfloat16)
         for entry_index in range(entries):
             matrix = values_ref[slot_index, entry_index]
             mixed_real = jnp.dot(matrix, response[:square], preferred_element_type=jnp.float32).reshape(

time: 40.4 us -> 42.7 us (1.057)
  Pallas kernels: 28.5 us -> 30.7 us
    pallas_call x1, Pallas kernels: 28.5 us -> 30.7 us  [local(): pl.pallas_call(functools.partial(fused_kernel, slot_count, entries), out_...]
where the time goes in v16:
time: 42.7 us; the launch traced here: 42.4 us
  Pallas kernels  30.7 us (72%)
  local copies, waits for them, and re-layouts  6.57 us (15%)
  starting transfers between devices  3.68 us (9%)
  other arithmetic  0.73 us (2%)
  between operations  0.72 us (2%)
    pallas_call x1, Pallas kernels, local(): pl.pallas_call(functools.partial(fused_kernel, slot_count, entries), out_...  30.7 us
    unnamed x13, local copies, waits for them, and re-layouts  4.1 us
    ppermute x1, starting transfers between devices, local(): lax.ppermute(mode_fields[:, :, -tap_count:], 'tm', [(k, k + 1) for k in r...  3.68 us
    another operation x1, local copies, waits for them, and re-layouts, local(): values = raman_values[0].reshape(slot_count, entries, square, square)  1.15 us
    slice x1, local copies, waits for them, and re-layouts, local(): mode_fields[:, :, -tap_count:]  0.96 us
  transfers between devices with their start and end apart: 1, of which 0 were waited for; matrix products, arithmetic and copies ran while one was open for 6% of the time, Pallas kernels for 0%

profile of v16, /device:TPU:11, one launch (start us, length us, event | category | flops | bytes accessed | tf_op | source)
XLA Modules:
  0.0 42.4 jit_solution(18021068809987145296)
XLA Ops:
  0.0 0.0 copy-start
  0.0 1.0 %slice.3 = bf16[2,256,128]{2,1,0:T(8,128)(2,1)S(1)} slice(bf16[2,256,512]{2,1,0:T(8,128)(2,1)} %param.7), slice={[0:2], [0:256], [384:512]} | slice | bytes 262144 | tf_op jit(solution)/shard_map/slice | solution.py:148
  1.0 3.7 %collective-permute-start = (bf16[2,256,128]{2,1,0:T(8,128)(2,1)S(1)}, bf16[2,256,128]{2,1,0:T(8,128)(2,1)S(1)}, u32[]{:S(2)}, u32[]{:S(2)}) collective-permute-start(bf16[2,256,128]{2,1,0:T(8,128)(2,1)S(1)} %slice.3), channel_id=1, source_target_pairs={{0,32},{32,64},{64,96},{96,128},{128,160},{160,192},{192,224},{1,3... | collective-permute-start | bytes 393224 | tf_op jit(solution)/shard_map/ppermute | solution.py:147
  5.3 0.0 copy-start.4
  5.3 0.6 %copy-done.4 = s32[32,1]{0,1:T(1,128)S(1)} copy-done((s32[32,1]{0,1:T(1,128)S(1)}, s32[32,1]{0,1:T(1,128)}, u32[]{:S(2)}) %copy-start.4) | copy-done | bytes 152
  6.0 0.1 select_reduce_fusion.1
  6.1 0.0 copy-start.2
  6.1 0.7 %copy-done.2 = s32[1,16,2]{1,2,0:T(2,128)S(1)} copy-done((s32[1,16,2]{1,2,0:T(2,128)S(1)}, s32[1,16,2]{1,2,0:T(2,128)}, u32[]{:S(2)}) %copy-start.2) | copy-done | bytes 152
  6.8 0.1 copy.14
  6.9 0.0 copy-start.3
  6.9 0.1 reshape.48
  7.0 0.6 %copy-done.3 = s32[1,16,2]{1,2,0:T(2,128)S(1)} copy-done((s32[1,16,2]{1,2,0:T(2,128)S(1)}, s32[1,16,2]{1,2,0:T(2,128)}, u32[]{:S(2)}) %copy-start.3) | copy-done | bytes 152
  7.5 0.1 copy.15
  7.6 0.1 reshape.49
  7.7 0.1 copy.16
  7.8 0.1 reshape.50
  7.9 0.0 copy-done
  7.9 1.1 %reshape_squeeze.3.values_ref = bf16[16,2,64,64]{3,2,1,0:T(8,128)(2,1)} reshape(bf16[1,16,2,4096]{3,2,1,0:T(2,128)(2,1)S(1)} %copy-done) | data formatting | bytes 524288 | tf_op jit(solution)/shard_map/reshape;squeeze | solution.py:153
  9.1 0.6 %pad_add_fusion.1.ints_ref = s32[128]{0:T(128)} fusion(s32[64]{0:T(128)S(1)} %reshape.50, s32[32]{0:T(128)S(1)} %reshape.49, s32[32]{0:T(128)S(1)} %reshape.48), kind=kLoop, calls=%fused_computation.11 | loop fusion | flops 256 | bytes 1024 | tf_op jit(solution)/shard_map/concatenate | solution.py:160
  9.7 0.0 collective-permute-done
  9.7 0.0 copy-start.1
  9.7 0.7 %copy-done.1 = bf16[2,256,128]{2,1,0:T(8,128)(2,1)} copy-done((bf16[2,256,128]{2,1,0:T(8,128)(2,1)}, bf16[2,256,128]{2,1,0:T(8,128)(2,1)S(1)}, u32[]{:S(2)}) %copy-start.1) | copy-done | bytes 131096
  10.3 30.7 %shard_map.73 = f32[1,2,8,512]{3,2,1,0:T(8,128)} custom-call(s32[128]{0:T(128)} %pad_add_fusion.1.ints_ref, bf16[2,32,8,128]{3,2,1,0:T(8,128)(2,1)} %bitcast.13, bf16[2,32,8,512]{3,2,1,0:T(8,128)(2,1)} %bitcast.11, bf16[1,128]{1,0:T(2,128)(2,1)} %bitcast.15, bf16[16,2,64,64]{3,2,1,0:T(8,128)(2,1)} %reshape_squeeze.3.values_ref), custom_call_target="tpu_custom_call" | custom-call | tf_op jit(solution)/shard_map/pallas_call | solution.py:166
  41.0 1.4 %copy.19 = f32[2,8,512]{2,1,0:T(8,128)} copy(f32[2,8,512]{2,1,0:T(8,128)} %bitcast.12) | data formatting | bytes 65536
  (3 shorter events, 0.0 us)
Async XLA Ops:
  0.0 7.9 %copy-start = (bf16[1,16,2,4096]{3,2,1,0:T(2,128)(2,1)S(1)}, bf16[1,16,2,4096]{3,2,1,0:T(2,128)(2,1)}, u32[]{:S(2)}) copy-start(bf16[1,16,2,4096]{3,2,1,0:T(2,128)(2,1)} %param.12) | copy-start | bytes 786436
  1.0 8.7 %collective-permute-start = (bf16[2,256,128]{2,1,0:T(8,128)(2,1)S(1)}, bf16[2,256,128]{2,1,0:T(8,128)(2,1)S(1)}, u32[]{:S(2)}, u32[]{:S(2)}) collective-permute-start(bf16[2,256,128]{2,1,0:T(8,128)(2,1)S(1)} %slice.3), channel_id=1, source_target_pairs={{0,32},{32,64},{64,96},{96,128},{128,160},{160,192},{192,224},{1,3... | collective-permute-start | bytes 393224 | tf_op jit(solution)/shard_map/ppermute | solution.py:147
  5.3 0.7 %copy-start.4 = (s32[32,1]{0,1:T(1,128)S(1)}, s32[32,1]{0,1:T(1,128)}, u32[]{:S(2)}) copy-start(s32[32,1]{0,1:T(1,128)} %param.11) | copy-start | bytes 388
  6.1 0.7 %copy-start.2 = (s32[1,16,2]{1,2,0:T(2,128)S(1)}, s32[1,16,2]{1,2,0:T(2,128)}, u32[]{:S(2)}) copy-start(s32[1,16,2]{1,2,0:T(2,128)} %param.9) | copy-start | bytes 388
  6.9 0.7 %copy-start.3 = (s32[1,16,2]{1,2,0:T(2,128)S(1)}, s32[1,16,2]{1,2,0:T(2,128)}, u32[]{:S(2)}) copy-start(s32[1,16,2]{1,2,0:T(2,128)} %param.10) | copy-start | bytes 388
  9.7 0.7 %copy-start.1 = (bf16[2,256,128]{2,1,0:T(8,128)(2,1)}, bf16[2,256,128]{2,1,0:T(8,128)(2,1)S(1)}, u32[]{:S(2)}) copy-start(bf16[2,256,128]{2,1,0:T(8,128)(2,1)S(1)} %collective-permute-done) | copy-start | bytes 393220

commit v17 on v15

--- a/solution.py
+++ b/solution.py
@@ -63,14 +63,13 @@
             span = intensity[:, piece * tap_count:piece * tap_count + 2 * tap_count]
             pieces.append(jnp.dot(span, table, preferred_element_type=jnp.float32))
         response = jnp.concatenate(pieces, 1).astype(jnp.bfloat16)
+        matrices = values_ref[slot_index].reshape(entries * square, square)
+        sides = jnp.concatenate([response[:square], response[square:]], 1)
+        mixed = jnp.dot(matrices, sides, preferred_element_type=jnp.float32)
         for entry_index in range(entries):
-            matrix = values_ref[slot_index, entry_index]
-            mixed_real = jnp.dot(matrix, response[:square], preferred_element_type=jnp.float32).reshape(
-                block_size, block_size, length
-            )
-            mixed_imag = jnp.dot(matrix, response[square:], preferred_element_type=jnp.float32).reshape(
-                block_size, block_size, length
-            )
+            rows = mixed[entry_index * square:(entry_index + 1) * square]
+            mixed_real = rows[:, :length].reshape(block_size, block_size, length)
+            mixed_imag = rows[:, length:].reshape(block_size, block_size, length)
             light = ints_ref[light_base + entries * slot_index + entry_index]
             light_real = fields_ref[0, light].astype(jnp.float32)[None]
             light_imag = fields_ref[1, light].astype(jnp.float32)[None]

time: 40.4 us -> 40.6 us (level)
  no operation moved by 1% of the time
where the time goes in v17:
time: 40.6 us; the launch traced here: 40.3 us
  Pallas kernels  28.6 us (70%)
  local copies, waits for them, and re-layouts  6.57 us (16%)
  starting transfers between devices  3.68 us (9%)
  other arithmetic  0.73 us (2%)
  between operations  0.72 us (2%)
    pallas_call x1, Pallas kernels, local(): pl.pallas_call(functools.partial(fused_kernel, slot_count, entries), out_...  28.6 us
    unnamed x13, local copies, waits for them, and re-layouts  4.1 us
    ppermute x1, starting transfers between devices, local(): lax.ppermute(mode_fields[:, :, -tap_count:], 'tm', [(k, k + 1) for k in r...  3.68 us
    another operation x1, local copies, waits for them, and re-layouts, local(): values = raman_values[0].reshape(slot_count, entries, square, square)  1.15 us
    slice x1, local copies, waits for them, and re-layouts, local(): mode_fields[:, :, -tap_count:]  0.96 us
  transfers between devices with their start and end apart: 1, of which 0 were waited for; matrix products, arithmetic and copies ran while one was open for 6% of the time, Pallas kernels for 0%

profile of v17, /device:TPU:11, one launch (start us, length us, event | category | flops | bytes accessed | tf_op | source)
XLA Modules:
  0.0 40.3 jit_solution(7674058266492945998)
XLA Ops:
  0.0 0.0 copy-start
  0.0 1.0 %slice.3 = bf16[2,256,128]{2,1,0:T(8,128)(2,1)S(1)} slice(bf16[2,256,512]{2,1,0:T(8,128)(2,1)} %param.7), slice={[0:2], [0:256], [384:512]} | slice | bytes 262144 | tf_op jit(solution)/shard_map/slice | solution.py:150
  1.0 3.7 %collective-permute-start = (bf16[2,256,128]{2,1,0:T(8,128)(2,1)S(1)}, bf16[2,256,128]{2,1,0:T(8,128)(2,1)S(1)}, u32[]{:S(2)}, u32[]{:S(2)}) collective-permute-start(bf16[2,256,128]{2,1,0:T(8,128)(2,1)S(1)} %slice.3), channel_id=1, source_target_pairs={{0,32},{32,64},{64,96},{96,128},{128,160},{160,192},{192,224},{1,3... | collective-permute-start | bytes 393224 | tf_op jit(solution)/shard_map/ppermute | solution.py:149
  5.3 0.0 copy-start.4
  5.3 0.6 %copy-done.4 = s32[32,1]{0,1:T(1,128)S(1)} copy-done((s32[32,1]{0,1:T(1,128)S(1)}, s32[32,1]{0,1:T(1,128)}, u32[]{:S(2)}) %copy-start.4) | copy-done | bytes 152
  6.0 0.1 select_reduce_fusion.1
  6.1 0.0 copy-start.2
  6.1 0.7 %copy-done.2 = s32[1,16,2]{1,2,0:T(2,128)S(1)} copy-done((s32[1,16,2]{1,2,0:T(2,128)S(1)}, s32[1,16,2]{1,2,0:T(2,128)}, u32[]{:S(2)}) %copy-start.2) | copy-done | bytes 152
  6.8 0.1 copy.14
  6.9 0.0 copy-start.3
  6.9 0.1 reshape.48
  7.0 0.6 %copy-done.3 = s32[1,16,2]{1,2,0:T(2,128)S(1)} copy-done((s32[1,16,2]{1,2,0:T(2,128)S(1)}, s32[1,16,2]{1,2,0:T(2,128)}, u32[]{:S(2)}) %copy-start.3) | copy-done | bytes 152
  7.5 0.1 copy.15
  7.6 0.1 reshape.49
  7.7 0.1 copy.16
  7.8 0.1 reshape.50
  7.9 0.0 copy-done
  7.9 1.1 %reshape_squeeze.3.values_ref = bf16[16,2,64,64]{3,2,1,0:T(8,128)(2,1)} reshape(bf16[1,16,2,4096]{3,2,1,0:T(2,128)(2,1)S(1)} %copy-done) | data formatting | bytes 524288 | tf_op jit(solution)/shard_map/reshape;squeeze | solution.py:155
  9.1 0.6 %pad_add_fusion.1.ints_ref = s32[128]{0:T(128)} fusion(s32[64]{0:T(128)S(1)} %reshape.50, s32[32]{0:T(128)S(1)} %reshape.49, s32[32]{0:T(128)S(1)} %reshape.48), kind=kLoop, calls=%fused_computation.11 | loop fusion | flops 256 | bytes 1024 | tf_op jit(solution)/shard_map/concatenate | solution.py:162
  9.7 0.0 collective-permute-done
  9.7 0.0 copy-start.1
  9.7 0.7 %copy-done.1 = bf16[2,256,128]{2,1,0:T(8,128)(2,1)} copy-done((bf16[2,256,128]{2,1,0:T(8,128)(2,1)}, bf16[2,256,128]{2,1,0:T(8,128)(2,1)S(1)}, u32[]{:S(2)}) %copy-start.1) | copy-done | bytes 131096
  10.3 28.6 %shard_map.73 = f32[1,2,8,512]{3,2,1,0:T(8,128)} custom-call(s32[128]{0:T(128)} %pad_add_fusion.1.ints_ref, bf16[2,32,8,128]{3,2,1,0:T(8,128)(2,1)} %bitcast.13, bf16[2,32,8,512]{3,2,1,0:T(8,128)(2,1)} %bitcast.11, bf16[1,128]{1,0:T(2,128)(2,1)} %bitcast.15, bf16[16,2,64,64]{3,2,1,0:T(8,128)(2,1)} %reshape_squeeze.3.values_ref), custom_call_target="tpu_custom_call" | custom-call | tf_op jit(solution)/shard_map/pallas_call | solution.py:168
  39.0 1.4 %copy.19 = f32[2,8,512]{2,1,0:T(8,128)} copy(f32[2,8,512]{2,1,0:T(8,128)} %bitcast.12) | data formatting | bytes 65536
  (3 shorter events, 0.0 us)
Async XLA Ops:
  0.0 7.9 %copy-start = (bf16[1,16,2,4096]{3,2,1,0:T(2,128)(2,1)S(1)}, bf16[1,16,2,4096]{3,2,1,0:T(2,128)(2,1)}, u32[]{:S(2)}) copy-start(bf16[1,16,2,4096]{3,2,1,0:T(2,128)(2,1)} %param.12) | copy-start | bytes 786436
  1.0 8.7 %collective-permute-start = (bf16[2,256,128]{2,1,0:T(8,128)(2,1)S(1)}, bf16[2,256,128]{2,1,0:T(8,128)(2,1)S(1)}, u32[]{:S(2)}, u32[]{:S(2)}) collective-permute-start(bf16[2,256,128]{2,1,0:T(8,128)(2,1)S(1)} %slice.3), channel_id=1, source_target_pairs={{0,32},{32,64},{64,96},{96,128},{128,160},{160,192},{192,224},{1,3... | collective-permute-start | bytes 393224 | tf_op jit(solution)/shard_map/ppermute | solution.py:149
  5.3 0.7 %copy-start.4 = (s32[32,1]{0,1:T(1,128)S(1)}, s32[32,1]{0,1:T(1,128)}, u32[]{:S(2)}) copy-start(s32[32,1]{0,1:T(1,128)} %param.11) | copy-start | bytes 388
  6.1 0.7 %copy-start.2 = (s32[1,16,2]{1,2,0:T(2,128)S(1)}, s32[1,16,2]{1,2,0:T(2,128)}, u32[]{:S(2)}) copy-start(s32[1,16,2]{1,2,0:T(2,128)} %param.9) | copy-start | bytes 388
  6.9 0.7 %copy-start.3 = (s32[1,16,2]{1,2,0:T(2,128)S(1)}, s32[1,16,2]{1,2,0:T(2,128)}, u32[]{:S(2)}) copy-start(s32[1,16,2]{1,2,0:T(2,128)} %param.10) | copy-start | bytes 388
  9.7 0.7 %copy-start.1 = (bf16[2,256,128]{2,1,0:T(8,128)(2,1)}, bf16[2,256,128]{2,1,0:T(8,128)(2,1)S(1)}, u32[]{:S(2)}) copy-start(bf16[2,256,128]{2,1,0:T(8,128)(2,1)S(1)} %collective-permute-done) | copy-start | bytes 393220

commit v18 on v15

--- a/solution.py
+++ b/solution.py
@@ -12,8 +12,8 @@
 
 def fused_kernel(
     slot_count, entries,
-    ints_ref, halo_ref, fields_ref, table_ref, values_ref, out_ref,
-    partials_ref, send_ref, recv_ref, send_sems, recv_sems,
+    ints_ref, halo_hbm, fields_ref, table_ref, values_ref, out_ref,
+    partials_ref, send_ref, recv_ref, send_sems, recv_sems, halo_ref, halo_sem,
 ):
     block_size = fields_ref.shape[2]
     length = fields_ref.shape[3]
@@ -35,7 +35,10 @@
         pl.semaphore_signal(barrier, inc=1, device_id=(row, peer), device_id_type=mesh_ids)
         return carry
 
+    halo_copy = pltpu.make_async_copy(halo_hbm, halo_ref, halo_sem)
+    halo_copy.start()
     lax.fori_loop(1, pair_count, greet, 0)
+    halo_copy.wait()
 
     partials_ref[zero_row] = jnp.zeros(partials_ref.shape[1:], partials_ref.dtype)
     tap_count = halo_ref.shape[3]
@@ -169,7 +172,7 @@
     shared = pl.pallas_call(
         functools.partial(fused_kernel, slot_count, entries),
         out_shape=jax.ShapeDtypeStruct((owned, 2, block_size, length), jnp.float32),
-        in_specs=[smem, vmem, vmem, vmem, vmem],
+        in_specs=[smem, pl.BlockSpec(memory_space=pl.ANY), vmem, vmem, vmem],
         out_specs=vmem,
         scratch_shapes=[
             pltpu.VMEM((rows + 1, 2, block_size, length), jnp.float32),
@@ -177,6 +180,8 @@
             pltpu.VMEM(exchange_shape, jnp.bfloat16),
             pltpu.SemaphoreType.DMA((pair_count,)),
             pltpu.SemaphoreType.DMA((pair_count,)),
+            pltpu.VMEM((2, blocks, block_size, tap_count), mode_fields.dtype),
+            pltpu.SemaphoreType.DMA(()),
         ],
         compiler_params=pltpu.CompilerParams(collective_id=0, has_side_effects=True),
     )(ints, halo, fields, raman_taps.reshape(1, tap_count), values)

time: 40.4 us -> 40.9 us (1.012)
  no operation moved by 1% of the time
where the time goes in v18:
time: 40.9 us; the launch traced here: 40.6 us
  Pallas kernels  28.9 us (71%)
  local copies, waits for them, and re-layouts  6.57 us (16%)
  starting transfers between devices  3.68 us (9%)
  other arithmetic  0.73 us (2%)
  between operations  0.72 us (2%)
    pallas_call x1, Pallas kernels, local(): pl.pallas_call(functools.partial(fused_kernel, slot_count, entries), out_...  28.9 us
    unnamed x13, local copies, waits for them, and re-layouts  4.1 us
    ppermute x1, starting transfers between devices, local(): lax.ppermute(mode_fields[:, :, -tap_count:], 'tm', [(k, k + 1) for k in r...  3.68 us
    another operation x1, local copies, waits for them, and re-layouts, local(): values = raman_values[0].reshape(slot_count, entries, square, square)  1.15 us
    slice x1, local copies, waits for them, and re-layouts, local(): mode_fields[:, :, -tap_count:]  0.96 us
  transfers between devices with their start and end apart: 1, of which 0 were waited for; matrix products, arithmetic and copies ran while one was open for 6% of the time, Pallas kernels for 0%

profile of v18, /device:TPU:11, one launch (start us, length us, event | category | flops | bytes accessed | tf_op | source)
XLA Modules:
  0.0 40.6 jit_solution(1202126178598865100)
XLA Ops:
  0.0 0.0 copy-start
  0.0 1.0 %slice.3 = bf16[2,256,128]{2,1,0:T(8,128)(2,1)S(1)} slice(bf16[2,256,512]{2,1,0:T(8,128)(2,1)} %param.7), slice={[0:2], [0:256], [384:512]} | slice | bytes 262144 | tf_op jit(solution)/shard_map/slice | solution.py:154
  1.0 3.7 %collective-permute-start = (bf16[2,256,128]{2,1,0:T(8,128)(2,1)S(1)}, bf16[2,256,128]{2,1,0:T(8,128)(2,1)S(1)}, u32[]{:S(2)}, u32[]{:S(2)}) collective-permute-start(bf16[2,256,128]{2,1,0:T(8,128)(2,1)S(1)} %slice.3), channel_id=1, source_target_pairs={{0,32},{32,64},{64,96},{96,128},{128,160},{160,192},{192,224},{1,3... | collective-permute-start | bytes 393224 | tf_op jit(solution)/shard_map/ppermute | solution.py:153
  5.3 0.0 copy-start.4
  5.3 0.6 %copy-done.4 = s32[32,1]{0,1:T(1,128)S(1)} copy-done((s32[32,1]{0,1:T(1,128)S(1)}, s32[32,1]{0,1:T(1,128)}, u32[]{:S(2)}) %copy-start.4) | copy-done | bytes 152
  6.0 0.1 select_reduce_fusion.1
  6.1 0.0 copy-start.2
  6.1 0.7 %copy-done.2 = s32[1,16,2]{1,2,0:T(2,128)S(1)} copy-done((s32[1,16,2]{1,2,0:T(2,128)S(1)}, s32[1,16,2]{1,2,0:T(2,128)}, u32[]{:S(2)}) %copy-start.2) | copy-done | bytes 152
  6.8 0.1 copy.14
  6.9 0.0 copy-start.3
  6.9 0.1 reshape.48
  7.0 0.6 %copy-done.3 = s32[1,16,2]{1,2,0:T(2,128)S(1)} copy-done((s32[1,16,2]{1,2,0:T(2,128)S(1)}, s32[1,16,2]{1,2,0:T(2,128)}, u32[]{:S(2)}) %copy-start.3) | copy-done | bytes 152
  7.5 0.1 copy.15
  7.6 0.1 reshape.49
  7.7 0.1 copy.16
  7.8 0.1 reshape.50
  7.9 0.0 copy-done
  7.9 1.1 %reshape_squeeze.3.values_ref = bf16[16,2,64,64]{3,2,1,0:T(8,128)(2,1)} reshape(bf16[1,16,2,4096]{3,2,1,0:T(2,128)(2,1)S(1)} %copy-done) | data formatting | bytes 524288 | tf_op jit(solution)/shard_map/reshape;squeeze | solution.py:159
  9.1 0.6 %pad_add_fusion.1.ints_ref = s32[128]{0:T(128)} fusion(s32[64]{0:T(128)S(1)} %reshape.50, s32[32]{0:T(128)S(1)} %reshape.49, s32[32]{0:T(128)S(1)} %reshape.48), kind=kLoop, calls=%fused_computation.11 | loop fusion | flops 256 | bytes 1024 | tf_op jit(solution)/shard_map/concatenate | solution.py:166
  9.7 0.0 collective-permute-done
  9.7 0.0 copy-start.1
  9.7 0.7 %copy-done.1 = bf16[2,256,128]{2,1,0:T(8,128)(2,1)} copy-done((bf16[2,256,128]{2,1,0:T(8,128)(2,1)}, bf16[2,256,128]{2,1,0:T(8,128)(2,1)S(1)}, u32[]{:S(2)}) %copy-start.1) | copy-done | bytes 131096
  10.3 28.9 %shard_map.73 = f32[1,2,8,512]{3,2,1,0:T(8,128)} custom-call(s32[128]{0:T(128)} %pad_add_fusion.1.ints_ref, bf16[2,32,8,128]{3,2,1,0:T(8,128)(2,1)} %bitcast.13, bf16[2,32,8,512]{3,2,1,0:T(8,128)(2,1)} %bitcast.11, bf16[1,128]{1,0:T(2,128)(2,1)} %bitcast.15, bf16[16,2,64,64]{3,2,1,0:T(8,128)(2,1)} %reshape_squeeze.3.values_ref), custom_call_target="tpu_custom_call" | custom-call | tf_op jit(solution)/shard_map/pallas_call | solution.py:172
  39.2 1.4 %copy.19 = f32[2,8,512]{2,1,0:T(8,128)} copy(f32[2,8,512]{2,1,0:T(8,128)} %bitcast.12) | data formatting | bytes 65536
  (3 shorter events, 0.0 us)
Async XLA Ops:
  0.0 7.9 %copy-start = (bf16[1,16,2,4096]{3,2,1,0:T(2,128)(2,1)S(1)}, bf16[1,16,2,4096]{3,2,1,0:T(2,128)(2,1)}, u32[]{:S(2)}) copy-start(bf16[1,16,2,4096]{3,2,1,0:T(2,128)(2,1)} %param.12) | copy-start | bytes 786436
  1.0 8.7 %collective-permute-start = (bf16[2,256,128]{2,1,0:T(8,128)(2,1)S(1)}, bf16[2,256,128]{2,1,0:T(8,128)(2,1)S(1)}, u32[]{:S(2)}, u32[]{:S(2)}) collective-permute-start(bf16[2,256,128]{2,1,0:T(8,128)(2,1)S(1)} %slice.3), channel_id=1, source_target_pairs={{0,32},{32,64},{64,96},{96,128},{128,160},{160,192},{192,224},{1,3... | collective-permute-start | bytes 393224 | tf_op jit(solution)/shard_map/ppermute | solution.py:153
  5.3 0.7 %copy-start.4 = (s32[32,1]{0,1:T(1,128)S(1)}, s32[32,1]{0,1:T(1,128)}, u32[]{:S(2)}) copy-start(s32[32,1]{0,1:T(1,128)} %param.11) | copy-start | bytes 388
  6.1 0.7 %copy-start.2 = (s32[1,16,2]{1,2,0:T(2,128)S(1)}, s32[1,16,2]{1,2,0:T(2,128)}, u32[]{:S(2)}) copy-start(s32[1,16,2]{1,2,0:T(2,128)} %param.9) | copy-start | bytes 388
  6.9 0.7 %copy-start.3 = (s32[1,16,2]{1,2,0:T(2,128)S(1)}, s32[1,16,2]{1,2,0:T(2,128)}, u32[]{:S(2)}) copy-start(s32[1,16,2]{1,2,0:T(2,128)} %param.10) | copy-start | bytes 388
  9.7 0.7 %copy-start.1 = (bf16[2,256,128]{2,1,0:T(8,128)(2,1)}, bf16[2,256,128]{2,1,0:T(8,128)(2,1)S(1)}, u32[]{:S(2)}) copy-start(bf16[2,256,128]{2,1,0:T(8,128)(2,1)S(1)} %collective-permute-done) | copy-start | bytes 393220

commit v19 on v15

--- a/solution.py
+++ b/solution.py
@@ -8,6 +8,7 @@
 from jax.experimental.pallas import tpu as pltpu
 
 MB = 8
+Y_IN_PAIR = 4
 
 
 def fused_kernel(
@@ -100,14 +101,21 @@
             device_id_type=mesh_ids,
         )
 
-    def send(step, carry):
-        peer = lax.rem(me + step, pair_count)
+    y_count = Y_IN_PAIR
+    z_count = pair_count // y_count
+    my_y = lax.rem(me, y_count)
+    my_z = me // y_count
+
+    def hops(offset):
+        dz, dy = offset
+        return min(dz, z_count - dz) + min(dy, y_count - dy)
+
+    offsets = [(dz, dy) for dz in range(z_count) for dy in range(y_count) if (dz, dy) != (0, 0)]
+    for dz, dy in sorted(offsets, key=lambda offset: -hops(offset)):
+        peer = lax.rem(my_z + dz, z_count) * y_count + lax.rem(my_y + dy, y_count)
         for part in range(owned):
             send_ref[peer, part] = block_sum(peer, part).astype(send_ref.dtype)
         outgoing(peer).start()
-        return carry
-
-    lax.fori_loop(1, pair_count, send, 0)
 
     def gather(step, total):
         peer = lax.rem(me + pair_count - step, pair_count)

time: 40.4 us -> 40.5 us (level)
  the two profiles are of different devices: /device:TPU:11 before, /device:TPU:1 now
where the time goes in v19:
time: 40.5 us; the launch traced here: 40.2 us
  Pallas kernels  27.7 us (68%)
  local copies, waits for them, and re-layouts  6.57 us (16%)
  starting transfers between devices  4.51 us (11%)
  other arithmetic  0.73 us (2%)
  between operations  0.72 us (2%)
    pallas_call x1, Pallas kernels, local(): pl.pallas_call(functools.partial(fused_kernel, slot_count, entries), out_...  27.7 us
    ppermute x1, starting transfers between devices, local(): lax.ppermute(mode_fields[:, :, -tap_count:], 'tm', [(k, k + 1) for k in r...  4.51 us
    unnamed x13, local copies, waits for them, and re-layouts  4.1 us
    another operation x1, local copies, waits for them, and re-layouts, local(): values = raman_values[0].reshape(slot_count, entries, square, square)  1.15 us
    slice x1, local copies, waits for them, and re-layouts, local(): mode_fields[:, :, -tap_count:]  0.96 us
  transfers between devices with their start and end apart: 1, of which 0 were waited for; matrix products, arithmetic and copies ran while one was open for 6% of the time, Pallas kernels for 0%

profile of v19, /device:TPU:1, one launch (start us, length us, event | category | flops | bytes accessed | tf_op | source)
XLA Modules:
  0.0 40.2 jit_solution(14596458536703870878)
XLA Ops:
  0.0 0.0 copy-start
  0.0 1.0 %slice.3 = bf16[2,256,128]{2,1,0:T(8,128)(2,1)S(1)} slice(bf16[2,256,512]{2,1,0:T(8,128)(2,1)} %param.7), slice={[0:2], [0:256], [384:512]} | slice | bytes 262144 | tf_op jit(solution)/shard_map/slice | solution.py:159
  1.0 4.5 %collective-permute-start = (bf16[2,256,128]{2,1,0:T(8,128)(2,1)S(1)}, bf16[2,256,128]{2,1,0:T(8,128)(2,1)S(1)}, u32[]{:S(2)}, u32[]{:S(2)}) collective-permute-start(bf16[2,256,128]{2,1,0:T(8,128)(2,1)S(1)} %slice.3), channel_id=1, source_target_pairs={{0,32},{32,64},{64,96},{96,128},{128,160},{160,192},{192,224},{1,3... | collective-permute-start | bytes 393224 | tf_op jit(solution)/shard_map/ppermute | solution.py:158
  6.1 0.0 copy-start.4
  6.2 0.6 %copy-done.4 = s32[32,1]{0,1:T(1,128)S(1)} copy-done((s32[32,1]{0,1:T(1,128)S(1)}, s32[32,1]{0,1:T(1,128)}, u32[]{:S(2)}) %copy-start.4) | copy-done | bytes 152
  6.8 0.1 select_reduce_fusion.1
  6.9 0.0 copy-start.2
  7.0 0.7 %copy-done.2 = s32[1,16,2]{1,2,0:T(2,128)S(1)} copy-done((s32[1,16,2]{1,2,0:T(2,128)S(1)}, s32[1,16,2]{1,2,0:T(2,128)}, u32[]{:S(2)}) %copy-start.2) | copy-done | bytes 152
  7.6 0.1 copy.14
  7.7 0.0 copy-start.3
  7.7 0.1 reshape.48
  7.8 0.6 %copy-done.3 = s32[1,16,2]{1,2,0:T(2,128)S(1)} copy-done((s32[1,16,2]{1,2,0:T(2,128)S(1)}, s32[1,16,2]{1,2,0:T(2,128)}, u32[]{:S(2)}) %copy-start.3) | copy-done | bytes 152
  8.4 0.1 copy.15
  8.5 0.1 reshape.49
  8.5 0.1 copy.16
  8.6 0.1 reshape.50
  8.7 0.0 copy-done
  8.8 1.1 %reshape_squeeze.3.values_ref = bf16[16,2,64,64]{3,2,1,0:T(8,128)(2,1)} reshape(bf16[1,16,2,4096]{3,2,1,0:T(2,128)(2,1)S(1)} %copy-done) | data formatting | bytes 524288 | tf_op jit(solution)/shard_map/reshape;squeeze | solution.py:164
  9.9 0.6 %pad_add_fusion.1.ints_ref = s32[128]{0:T(128)} fusion(s32[64]{0:T(128)S(1)} %reshape.50, s32[32]{0:T(128)S(1)} %reshape.49, s32[32]{0:T(128)S(1)} %reshape.48), kind=kLoop, calls=%fused_computation.11 | loop fusion | flops 256 | bytes 1024 | tf_op jit(solution)/shard_map/concatenate | solution.py:171
  10.5 0.0 collective-permute-done
  10.5 0.0 copy-start.1
  10.5 0.7 %copy-done.1 = bf16[2,256,128]{2,1,0:T(8,128)(2,1)} copy-done((bf16[2,256,128]{2,1,0:T(8,128)(2,1)}, bf16[2,256,128]{2,1,0:T(8,128)(2,1)S(1)}, u32[]{:S(2)}) %copy-start.1) | copy-done | bytes 131096
  11.1 27.7 %shard_map.73 = f32[1,2,8,512]{3,2,1,0:T(8,128)} custom-call(s32[128]{0:T(128)} %pad_add_fusion.1.ints_ref, bf16[2,32,8,128]{3,2,1,0:T(8,128)(2,1)} %bitcast.13, bf16[2,32,8,512]{3,2,1,0:T(8,128)(2,1)} %bitcast.11, bf16[1,128]{1,0:T(2,128)(2,1)} %bitcast.15, bf16[16,2,64,64]{3,2,1,0:T(8,128)(2,1)} %reshape_squeeze.3.values_ref), custom_call_target="tpu_custom_call" | custom-call | tf_op jit(solution)/shard_map/pallas_call | solution.py:177
  38.8 1.4 %copy.19 = f32[2,8,512]{2,1,0:T(8,128)} copy(f32[2,8,512]{2,1,0:T(8,128)} %bitcast.12) | data formatting | bytes 65536
  (3 shorter events, 0.0 us)
Async XLA Ops:
  0.0 8.7 %copy-start = (bf16[1,16,2,4096]{3,2,1,0:T(2,128)(2,1)S(1)}, bf16[1,16,2,4096]{3,2,1,0:T(2,128)(2,1)}, u32[]{:S(2)}) copy-start(bf16[1,16,2,4096]{3,2,1,0:T(2,128)(2,1)} %param.12) | copy-start | bytes 786436
  1.0 9.5 %collective-permute-start = (bf16[2,256,128]{2,1,0:T(8,128)(2,1)S(1)}, bf16[2,256,128]{2,1,0:T(8,128)(2,1)S(1)}, u32[]{:S(2)}, u32[]{:S(2)}) collective-permute-start(bf16[2,256,128]{2,1,0:T(8,128)(2,1)S(1)} %slice.3), channel_id=1, source_target_pairs={{0,32},{32,64},{64,96},{96,128},{128,160},{160,192},{192,224},{1,3... | collective-permute-start | bytes 393224 | tf_op jit(solution)/shard_map/ppermute | solution.py:158
  6.1 0.7 %copy-start.4 = (s32[32,1]{0,1:T(1,128)S(1)}, s32[32,1]{0,1:T(1,128)}, u32[]{:S(2)}) copy-start(s32[32,1]{0,1:T(1,128)} %param.11) | copy-start | bytes 388
  6.9 0.7 %copy-start.2 = (s32[1,16,2]{1,2,0:T(2,128)S(1)}, s32[1,16,2]{1,2,0:T(2,128)}, u32[]{:S(2)}) copy-start(s32[1,16,2]{1,2,0:T(2,128)} %param.9) | copy-start | bytes 388
  7.7 0.7 %copy-start.3 = (s32[1,16,2]{1,2,0:T(2,128)S(1)}, s32[1,16,2]{1,2,0:T(2,128)}, u32[]{:S(2)}) copy-start(s32[1,16,2]{1,2,0:T(2,128)} %param.10) | copy-start | bytes 388
  10.5 0.7 %copy-start.1 = (bf16[2,256,128]{2,1,0:T(8,128)(2,1)}, bf16[2,256,128]{2,1,0:T(8,128)(2,1)S(1)}, u32[]{:S(2)}) copy-start(bf16[2,256,128]{2,1,0:T(8,128)(2,1)S(1)} %collective-permute-done) | copy-start | bytes 393220
